TPU v7x, 32 devices: a whole 2x2x4 slice. The times are simulated.
32 devices in a mesh: lon: 8 (over z, x), lat: 4 (over y, core).
Axes of the slice: x: 2, y: 2, z: 4, core: 2. Of those that a mesh axis runs over, the one named last changes fastest.
Arguments:
- obs_feat: bfloat16 [32768, 128], P(('lon', 'lat')), may hold values from -6 to 6
- obs_tile: int32 [32768, 1], P(('lon', 'lat')), may hold values from 0 to 31; in each aligned block of 1024 rows (0 to 1023, 1024 to 2047, ...) at most 64 rows name the same one
- obs_cell: int32 [32768], P(('lon', 'lat')), may hold values from 0 to 4095
- w_embed: bfloat16 [128, 256], replicated, may hold values from -0.5 to 0.5
- background: bfloat16 [128, 1024, 256], P('lat', 'lon'), may hold values from -6 to 6
- w_conv: bfloat16 [9, 256, 256], replicated, may hold values from -0.125 to 0.125
- cotangent: bfloat16 [128, 1024, 256], P('lat', 'lon'), may hold values from -6 to 6
Outputs:
- encoded: bfloat16 [128, 1024, 256], P('lat', 'lon')
- record_grad: bfloat16 [32768, 256], P(('lon', 'lat'))
- conv_grad: float32 [9, 256, 256], replicated
- embed_grad: float32 [128, 256], replicated
Inputs may be any that keep to these rules, and one draw needn't show every extreme that they name: `obs_tile`: among the records of one device each tile is named at most 64 times, a bound that some block reaches.
All inputs are finite; a program needn't handle non-finite values.
Results may differ from a plain program's by a relative error of at most 0.0037.
Values may be sent and summed in bfloat16 or wider, within the bound.
No kernel may reach another device: no remote copies, remote signals or barrier semaphores. Data moves between devices by JAX's collectives and lax.ppermute only.
A program may use at most 128 MiB of HBM per device.

v0:
```python
import jax
import jax.numpy as jnp
from jax import lax
from jax.sharding import PartitionSpec as P


def padded(x, sides, width, wrap):
    for axis, dim in sides:
        count, length = (lax.axis_size(axis), x.shape[dim])
        up = [(i, (i + 1) % count) for i in range(count if wrap else count - 1)]
        down = [(j, i) for i, j in up]
        last = lax.slice_in_dim(x, length - width, length, axis=dim)
        initial = lax.slice_in_dim(x, 0, width, axis=dim)
        before = lax.ppermute(last, axis, up)
        after = lax.ppermute(initial, axis, down)
        x = jnp.concatenate([before, x, after], axis=dim)
    return x


def gelu_tanh(value):
    return jax.nn.gelu(value, approximate=True)


def extend(grid):
    wide = padded(grid, (("lon", 1),), 1, True)
    return padded(wide, (("lat", 0),), 1, False)


def send_out(payload, codes, lon_count, lat_count, slots):
    moved, moved_codes = (
        lax.all_to_all(
            payload.reshape(lon_count * lat_count, slots, -1),
            ("lon", "lat"),
            split_axis=0,
            concat_axis=0,
            tiled=True,
        ),
        lax.all_to_all(
            codes.reshape(lon_count * lat_count, slots),
            ("lon", "lat"),
            split_axis=0,
            concat_axis=0,
            tiled=True,
        ),
    )
    return (moved.reshape(lon_count * lat_count * slots, -1), moved_codes.reshape(-1))


def send_back(rows, lon_count, lat_count, slots):
    moved = lax.all_to_all(
        rows.reshape(lon_count * lat_count, slots, -1),
        ("lon", "lat"),
        split_axis=0,
        concat_axis=0,
        tiled=True,
    )
    return moved.reshape(lon_count * lat_count * slots, -1)


def feature_grad(features, hidden, grad_rows):
    _, pullback = jax.vjp(gelu_tanh, hidden)
    dhidden = pullback(grad_rows.astype(jnp.float32))[0]
    return jnp.dot(features.astype(jnp.float32).T, dhidden, precision=lax.Precision.HIGHEST)


def on_device(obs_feat, obs_tile, obs_cell, w_embed, background, w_conv, cotangent):
    lon_count = lax.axis_size("lon")
    lat_count = lax.axis_size("lat")
    owners = lon_count * lat_count
    records = obs_feat.shape[0]
    slots = 2 * records // owners
    rows, cols, width = background.shape
    cells = rows * cols
    target = obs_tile[:, 0]
    onehot = (target[:, None] == jnp.arange(owners, dtype=jnp.int32)[None, :]).astype(jnp.int32)
    rank = jnp.sum(jnp.cumsum(onehot, axis=0) * onehot, axis=1) - 1
    place = target * slots + rank
    code_buf = jnp.zeros((owners * slots,), jnp.int32).at[place].set(obs_cell + 1)
    hidden = jnp.dot(obs_feat, w_embed, preferred_element_type=jnp.float32)
    embed = gelu_tanh(hidden).astype(jnp.bfloat16)
    embed_buf = jnp.zeros((owners * slots, width), jnp.bfloat16).at[place].set(embed)
    arrived, arrived_codes = send_out(embed_buf, code_buf, lon_count, lat_count, slots)
    cell_index = jnp.maximum(arrived_codes - 1, 0)
    aggregated = (
        jnp.zeros((cells, width), jnp.float32).at[cell_index].add(arrived.astype(jnp.float32))
    )
    field_flat = (background.reshape(cells, width).astype(jnp.float32) + aggregated).astype(
        jnp.bfloat16
    )
    field_pad = extend(field_flat.reshape(rows, cols, width))
    cot_pad = extend(cotangent)
    cot_flat = cotangent.reshape(cells, width)
    conv = jnp.zeros((cells, width), jnp.float32)
    back = jnp.zeros((cells, width), jnp.float32)
    grads = []
    for tap in range(9):
        a, b = (tap // 3, tap % 3)
        part = field_pad[a : a + rows, b : b + cols].reshape(cells, width)
        conv = conv + jnp.dot(part, w_conv[tap], preferred_element_type=jnp.float32)
        grads.append(
            lax.dot_general(
                part, cot_flat, (((0,), (0,)), ((), ())), preferred_element_type=jnp.float32
            )
        )
        cpart = cot_pad[2 - a : 2 - a + rows, 2 - b : 2 - b + cols].reshape(cells, width)
        back = back + lax.dot_general(
            cpart, w_conv[tap], (((1,), (1,)), ((), ())), preferred_element_type=jnp.float32
        )
    encoded = (
        (field_flat.astype(jnp.float32) + conv).astype(jnp.bfloat16).reshape(rows, cols, width)
    )
    dfield = (cot_flat.astype(jnp.float32) + back).astype(jnp.bfloat16)
    local_conv_grad = jnp.stack(grads)
    slot_grad = dfield[cell_index]
    returned = send_back(slot_grad, lon_count, lat_count, slots)
    record_grad = returned[place]
    local_embed_grad = feature_grad(obs_feat, hidden, record_grad)
    conv_grad, embed_grad = lax.psum((local_conv_grad, local_embed_grad), ("lon", "lat"))
    return (encoded, record_grad, conv_grad, embed_grad)


def solution(mesh):
    placed = (
        P(("lon", "lat"), None),
        P(("lon", "lat"), None),
        P(("lon", "lat")),
        P(),
        P("lat", "lon", None),
        P(),
        P("lat", "lon", None),
    )
    return jax.shard_map(
        on_device,
        mesh=mesh,
        in_specs=placed,
        out_specs=(P("lat", "lon", None), P(("lon", "lat"), None), P(), P()),
        check_vma=False,
    )
```

profile of v0, /device:TPU:0, one launch (start us, length us, event | category | flops | bytes accessed | tf_op | source)
XLA Modules:
  0.0 390.1 jit_solution(7500907045221961652)
XLA Ops:
  16.2 9.0 %reduce-window.6 = s32[32,8,128]{2,1,0:T(8,128)S(1)} reduce-window(s32[32,8,128]{2,1,0:T(8,128)S(1)} %fusion.72, s32[]{:T(128)} %constant.12.clone.1), window={size=1x1x128 pad=0_0x0_0x127_0}, to_apply=%region_0.0 | reduce-window | flops 4161536 | bytes 262148 | tf_op jit(solution)/shard_map/reduce-window
  27.2 4.3 %scatter_custom_fusion = s32[2048]{0:T(1024)S(1)} fusion(s32[1024]{0:T(1024)S(1)} %bitcast.200, s32[1024]{0:T(1024)S(1)} %broadcast_add_fusion.1, s32[]{:T(128)} %constant.12.clone.1), kind=kCustom, calls=%fused_computation.143 | custom fusion | bytes 8196 | tf_op jit(solution)/shard_map/scatter | solution.py:78
  35.6 4.1 %bitcast_convert_fusion = f32[4096,256]{1,0:T(8,128)} fusion(bf16[32,128,256]{2,1,0:T(8,128)(2,1)} %param.11), kind=kLoop, calls=%fused_computation.35 | loop fusion | flops 1048576 | bytes 6291456 | tf_op jit(solution)/shard_map/convert_element_type | solution.py:87
  44.3 6.7 %scatter_custom_fusion.1 = bf16[2048,256]{1,0:T(8,128)(2,1)} fusion(s32[1024]{0:T(1024)} %bitcast.201, f32[1024,256]{1,0:T(8,128)} %fusion.111, f32[]{:T(128)} %constant.32.clone.1, f32[]{:T(128)} %constant.11.clone.1, f32[]{:T(128)} %constant.10.clone.1, f32[]{:T(128)} %constant.9.clone.1, bf16[]{:T(256)} %constant.8.clone.1), kind=kCustom, calls=%fused_computation.75 | custom fusion | flops 2359296 | bytes 2099712 | tf_op jit(solution)/shard_map/scatter | solution.py:81
  51.1 6.0 %all-to-all-start.1 = ((bf16[32,64,256]{2,1,0:T(8,128)(2,1)}), bf16[32,64,256]{2,1,0:T(8,128)(2,1)}, u32[]{:S(2)}, u32[]{:S(2)}) async-start(bf16[32,64,256]{2,1,0:T(8,128)(2,1)} %bitcast.193), calls=%async_computation.1 | async-start | bytes 2097152 | tf_op jit(solution)/shard_map/all_to_all | solution.py:31
  69.1 3.9 fusion.107
  83.2 16.8 %scatter_custom_fusion.2 = f32[4096,256]{1,0:T(8,128)} fusion(f32[4096,256]{1,0:T(8,128)} %bitcast_convert_fusion, s32[2048]{0:T(1024)S(1)} %reshape.188, bf16[2048,256]{1,0:T(8,128)(2,1)} %bitcast.58), kind=kCustom, calls=%fused_computation.33 | custom fusion | flops 1048576 | bytes 5242880 | tf_op jit(solution)/shard_map/scatter-add | solution.py:85
  105.2 3.7 collective-permute-start.1
  111.2 10.3 %gather_fusion = bf16[2048,256]{1,0:T(8,128)(2,1)} fusion(bf16[4096,256]{1,0:T(8,128)(2,1)} %fusion.5, s32[2048]{0:T(1024)S(1)} %broadcast_clamp_fusion), kind=kCustom, calls=%fused_computation | custom fusion | bytes 2105344 | tf_op jit(solution)/shard_map/gather | solution.py:114
  121.5 8.2 %all-to-all-start.2 = ((bf16[32,64,256]{2,1,0:T(8,128)(2,1)}), bf16[32,64,256]{2,1,0:T(8,128)(2,1)S(1)}, u32[]{:S(2)}, u32[]{:S(2)}) async-start(bf16[32,64,256]{2,1,0:T(8,128)(2,1)} %bitcast.194), calls=%async_computation.2 | async-start | bytes 2097152 | tf_op jit(solution)/shard_map/all_to_all | solution.py:50
  129.8 4.1 %copy.38 = bf16[32,128,256]{1,2,0:T(8,128)(2,1)} copy(bf16[32,128,256]{2,1,0:T(8,128)(2,1)} %bitcast.175) | data formatting | bytes 4194304 | tf_op jit(solution)/shard_map/reshape | solution.py:90
  149.7 4.1 %copy.48 = bf16[32,128,256]{2,1,0:T(8,128)(2,1)} copy(bf16[32,128,256]{1,2,0:T(8,128)(2,1)} %get-tuple-element.42) | data formatting | bytes 4194304 | tf_op jit(solution)/shard_map/slice | solution.py:98
  153.7 4.1 %copy.45 = bf16[32,128,256]{2,1,0:T(8,128)(2,1)} copy(bf16[32,128,256]{1,2,0:T(8,128)(2,1)} %get-tuple-element.43) | data formatting | bytes 4194304 | tf_op jit(solution)/shard_map/slice | solution.py:98
  157.9 10.4 %pad_maximum_fusion = (bf16[33,130,256]{1,2,0:T(8,128)(2,1)S(1)}, bf16[33,130,256]{1,2,0:T(8,128)(2,1)S(1)}) fusion(bf16[1,130,256]{1,2,0:T(8,128)(2,1)} %collective-permute-done.3, bf16[32,1,256]{1,2,0:T(8,128)(2,1)} %copy.39, bf16[32,128,256]{1,2,0:T(8,128)(2,1)} %copy.38, bf16[32,1,256]{1,2,0:T(8,128)(2,1)} %copy.37, ...), kind=kLoop, calls=%fused_computation.26 | loop fusion | flops 17571840 | bytes 6656000 | tf_op jit(solution)/shard_map/concatenate | solution.py:16
  175.6 5.9 %fusion.105 = (bf16[32,128,256]{1,2,0:T(8,128)(2,1)}, bf16[32,128,256]{1,2,0:T(8,128)(2,1)}, bf16[32,128,256]{1,2,0:T(8,128)(2,1)}, bf16[32,128,256]{1,2,0:T(8,1...) fusion(bf16[33,130,256]{1,2,0:T(8,128)(2,1)S(1)} %get-tuple-element.18, ...), kind=kLoop, calls=%fused_computation.160 | loop fusion | bytes 25165824 | tf_op jit(solution)/shard_map/slice | solution.py:98
  184.7 4.3 %copy.40 = bf16[32,128,256]{2,1,0:T(8,128)(2,1)} copy(bf16[32,128,256]{1,2,0:T(8,128)(2,1)} %get-tuple-element.46) | data formatting | bytes 4194304 | tf_op jit(solution)/shard_map/slice | solution.py:98
  189.0 4.3 %fusion.70 = f32[4096,256]{1,0:T(8,128)} fusion(bf16[4096,256]{1,0:T(8,128)(2,1)} %bitcast.179, bf16[9,256,256]{2,1,0:T(8,128)(2,1)} %param.12), kind=kOutput, calls=%fused_computation.113 | convolution fusion | flops 536870912 | bytes 6422528 | tf_op jit(solution)/shard_map/dot_general | solution.py:99
  193.3 3.9 fusion.8
  197.2 4.1 %copy.51 = bf16[32,128,256]{2,1,0:T(8,128)(2,1)} copy(bf16[32,128,256]{1,2,0:T(8,128)(2,1)} %get-tuple-element.22) | data formatting | bytes 4194304 | tf_op jit(solution)/shard_map/slice | solution.py:98
  201.3 4.2 %copy.50 = bf16[32,128,256]{2,1,0:T(8,128)(2,1)} copy(bf16[32,128,256]{1,2,0:T(8,128)(2,1)} %get-tuple-element.23) | data formatting | bytes 4194304 | tf_op jit(solution)/shard_map/slice | solution.py:98
  208.5 4.2 %copy.41 = bf16[32,128,256]{2,1,0:T(8,128)(2,1)} copy(bf16[32,128,256]{1,2,0:T(8,128)(2,1)} %get-tuple-element.47) | data formatting | bytes 4194304 | tf_op jit(solution)/shard_map/slice | solution.py:98
  226.6 5.0 %gather_fusion.1 = bf16[1024,256]{1,0:T(8,128)(2,1)} fusion(bf16[2048,256]{1,0:T(8,128)(2,1)S(1)} %bitcast.176, s32[1024]{0:T(1024)S(1)} %copy-done.25), kind=kCustom, calls=%fused_computation.1 | custom fusion | bytes 1052672 | tf_op jit(solution)/shard_map/gather | solution.py:116
  235.2 5.6 %convolution_add_fusion.9 = f32[4096,256]{1,0:T(8,128)} fusion(f32[4096,256]{1,0:T(8,128)} %convolution_add_fusion.10, bf16[4096,256]{1,0:T(8,128)(2,1)} %bitcast.186, bf16[9,256,256]{2,1,0:T(8,128)(2,1)} %param.12), kind=kOutput, calls=%fused_computation.18 | convolution fusion | flops 537919488 | bytes 10616832 | tf_op jit(solution)/shard_map/dot_general | solution.py:99
  249.4 128.5 %all-reduce.3.cloned.1.call-done = (f32[9,256,256]{2,1,0:T(8,128)}, f32[128,256]{0,1:T(8,128)}) async-done(((f32[9,256,256]{2,1,0:T(8,128)}, f32[128,256]{0,1:T(8,128)}), (f32[9,256,256]{2,1,0:T(8,128)}, f32[128,256]{0,1:T(8,128)})) %all-reduce.3.cloned.1.call-update) | async-done | bytes 2490384 | tf_op jit(solution)/shard_map/psum | solution.py:118
  (131 shorter events, 109.4 us)
Async XLA Ops:
  7.2 32.5 %copy-start = (bf16[1024,128]{1,0:T(8,128)(2,1)S(1)}, bf16[1024,128]{1,0:T(8,128)(2,1)}, u32[]{:S(2)}) copy-start(bf16[1024,128]{1,0:T(8,128)(2,1)} %param.7) | copy-start | bytes 786436
  8.9 49.6 %collective-permute-start.4 = (bf16[32,1,256]{2,1,0:T(2,128)(2,1)}, bf16[32,1,256]{2,1,0:T(2,128)(2,1)}, u32[]{:S(2)}, u32[]{:S(2)}) collective-permute-start(bf16[32,1,256]{2,1,0:T(2,128)(2,1)} %get-tuple-element.40), channel_id=1, source_target_pairs={{0,4},{4,8},{8,12},{12,16},{16,20},{20,24},{24,28},{28,0},{1,5},{5... | collective-permute-start | bytes 49160 | tf_op jit(solution)/shard_map/ppermute | solution.py:14
  11.8 46.7 %collective-permute-start.5 = (bf16[32,1,256]{2,1,0:T(2,128)(2,1)}, bf16[32,1,256]{2,1,0:T(2,128)(2,1)}, u32[]{:S(2)}, u32[]{:S(2)}) collective-permute-start(bf16[32,1,256]{2,1,0:T(2,128)(2,1)} %get-tuple-element.41), channel_id=1, source_target_pairs={{4,0},{8,4},{12,8},{16,12},{20,16},{24,20},{28,24},{0,28},{5,1},{9... | collective-permute-start | bytes 49160 | tf_op jit(solution)/shard_map/ppermute | solution.py:15
  27.2 5.0 %copy-start.23 = (s32[1024,1]{0,1:T(1,128)}, s32[1024,1]{0,1:T(1,128)S(1)}, u32[]{:S(2)}) copy-start(s32[1024,1]{0,1:T(1,128)S(1)} %compare_select_fusion) | copy-start | bytes 12292
  32.2 18.9 %all-to-all-start = ((s32[32,1,64]{2,1,0:T(1,128)}), s32[32,1,64]{2,1,0:T(1,128)S(1)}, u32[]{:S(2)}, u32[]{:S(2)}) async-start(s32[32,1,64]{2,1,0:T(1,128)} %all_to_all.12), calls=%async_computation | async-start | bytes 32768 | tf_op jit(solution)/shard_map/all_to_all | solution.py:38
  35.5 5.4 %copy-start.1 = (bf16[32,128,256]{2,1,0:T(8,128)(2,1)S(1)}, bf16[32,128,256]{2,1,0:T(8,128)(2,1)}, u32[]{:S(2)}) copy-start(bf16[32,128,256]{2,1,0:T(8,128)(2,1)} %param.13) | copy-start | bytes 6291460
  35.6 5.4 %copy-start.20 = (bf16[9,256,256]{2,1,0:T(8,128)(2,1)S(1)}, bf16[9,256,256]{2,1,0:T(8,128)(2,1)}, u32[]{:S(2)}) copy-start(bf16[9,256,256]{2,1,0:T(8,128)(2,1)} %param.12) | copy-start | bytes 3538948
  51.1 32.2 %all-to-all-start.1 = ((bf16[32,64,256]{2,1,0:T(8,128)(2,1)}), bf16[32,64,256]{2,1,0:T(8,128)(2,1)}, u32[]{:S(2)}, u32[]{:S(2)}) async-start(bf16[32,64,256]{2,1,0:T(8,128)(2,1)} %bitcast.193), calls=%async_computation.1 | async-start | bytes 2097152 | tf_op jit(solution)/shard_map/all_to_all | solution.py:31
  59.2 6.8 %collective-permute-start.6 = (bf16[1,130,256]{2,1,0:T(8,128)(2,1)S(1)}, bf16[1,130,256]{2,1,0:T(8,128)(2,1)S(1)}, u32[]{:S(2)}, u32[]{:S(2)}) collective-permute-start(bf16[1,130,256]{2,1,0:T(8,128)(2,1)S(1)} %get-tuple-element.36), channel_id=1, source_target_pairs={{1,0},{2,1},{3,2},{5,4},{6,5},{7,6},{9,8},{10,9},{11,10},{13,12},{... | collective-permute-start | bytes 199688 | tf_op jit(solution)/shard_map/ppermute | solution.py:15
  60.5 5.5 %collective-permute-start.7 = (bf16[1,130,256]{2,1,0:T(8,128)(2,1)S(1)}, bf16[1,130,256]{2,1,0:T(8,128)(2,1)S(1)}, u32[]{:S(2)}, u32[]{:S(2)}) collective-permute-start(bf16[1,130,256]{2,1,0:T(8,128)(2,1)S(1)} %get-tuple-element.37), channel_id=1, source_target_pairs={{0,1},{1,2},{2,3},{4,5},{5,6},{6,7},{8,9},{9,10},{10,11},{12,13},{... | collective-permute-start | bytes 199688 | tf_op jit(solution)/shard_map/ppermute | solution.py:14
  100.0 9.1 %copy-start.10 = (f32[4096,256]{1,0:T(8,128)S(1)}, f32[4096,256]{1,0:T(8,128)}, u32[]{:S(2)}) copy-start(f32[4096,256]{1,0:T(8,128)} %convolution_add_fusion.1) | copy-start | bytes 12582916
  100.0 9.1 %copy-start.15 = (bf16[32,128,256]{2,1,0:T(8,128)(2,1)S(1)}, bf16[32,128,256]{2,1,0:T(8,128)(2,1)}, u32[]{:S(2)}) copy-start(bf16[32,128,256]{2,1,0:T(8,128)(2,1)} %get-tuple-element.28) | copy-start | bytes 6291460
  105.2 31.2 %collective-permute-start.1 = (bf16[32,1,256]{2,0,1:T(8,128)(2,1)}, bf16[32,1,256]{2,0,1:T(8,128)(2,1)}, u32[]{:S(2)}, u32[]{:S(2)}) collective-permute-start(bf16[32,1,256]{2,0,1:T(8,128)(2,1)} %copy.54), channel_id=1, source_target_pairs={{4,0},{8,4},{12,8},{16,12},{20,16},{24,20},{28,24},{0,28},{5,1},{9... | collective-permute-start | bytes 49160 | tf_op jit(solution)/shard_map/ppermute | solution.py:15
  108.9 25.0 %collective-permute-start = (bf16[32,1,256]{2,0,1:T(8,128)(2,1)}, bf16[32,1,256]{2,0,1:T(8,128)(2,1)}, u32[]{:S(2)}, u32[]{:S(2)}) collective-permute-start(bf16[32,1,256]{2,0,1:T(8,128)(2,1)} %copy.53), channel_id=1, source_target_pairs={{0,4},{4,8},{8,12},{12,16},{16,20},{20,24},{24,28},{28,0},{1,5},{5... | collective-permute-start | bytes 49160 | tf_op jit(solution)/shard_map/ppermute | solution.py:14
  121.5 105.1 %all-to-all-start.2 = ((bf16[32,64,256]{2,1,0:T(8,128)(2,1)}), bf16[32,64,256]{2,1,0:T(8,128)(2,1)S(1)}, u32[]{:S(2)}, u32[]{:S(2)}) async-start(bf16[32,64,256]{2,1,0:T(8,128)(2,1)} %bitcast.194), calls=%async_computation.2 | async-start | bytes 2097152 | tf_op jit(solution)/shard_map/all_to_all | solution.py:50
  129.7 248.2 %all-reduce.3.cloned.1.call-start = ((), (), s32[]{:S(2)}) async-start(), calls=%async_computation.3 | async-start | bytes 4980736 | tf_op jit(solution)/shard_map/psum | solution.py:118
  138.9 7.1 %copy-start.5 = (bf16[32,128,256]{1,2,0:T(8,128)(2,1)S(1)}, bf16[32,128,256]{1,2,0:T(8,128)(2,1)}, u32[]{:S(2)}) copy-start(bf16[32,128,256]{1,2,0:T(8,128)(2,1)} %copy.38) | copy-start | bytes 6291460
  138.9 7.1 %copy-start.6 = (bf16[32,1,256]{1,2,0:T(8,128)(2,1)S(1)}, bf16[32,1,256]{1,2,0:T(8,128)(2,1)}, u32[]{:S(2)}) copy-start(bf16[32,1,256]{1,2,0:T(8,128)(2,1)} %copy.37) | copy-start | bytes 49156
  138.9 7.1 %copy-start.7 = (bf16[32,1,256]{1,2,0:T(8,128)(2,1)S(1)}, bf16[32,1,256]{1,2,0:T(8,128)(2,1)}, u32[]{:S(2)}) copy-start(bf16[32,1,256]{1,2,0:T(8,128)(2,1)} %copy.39) | copy-start | bytes 49156
  140.9 17.0 %collective-permute-start.3 = (bf16[1,130,256]{1,2,0:T(8,128)(2,1)}, bf16[1,130,256]{1,2,0:T(8,128)(2,1)}, u32[]{:S(2)}, u32[]{:S(2)}) collective-permute-start(bf16[1,130,256]{1,2,0:T(8,128)(2,1)} %get-tuple-element.20), channel_id=1, source_target_pairs={{1,0},{2,1},{3,2},{5,4},{6,5},{7,6},{9,8},{10,9},{11,10},{13,12},{... | collective-permute-start | bytes 199688 | tf_op jit(solution)/shard_map/ppermute | solution.py:15
  142.3 15.6 %collective-permute-start.2 = (bf16[1,130,256]{1,2,0:T(8,128)(2,1)S(1)}, bf16[1,130,256]{1,2,0:T(8,128)(2,1)}, u32[]{:S(2)}, u32[]{:S(2)}) collective-permute-start(bf16[1,130,256]{1,2,0:T(8,128)(2,1)S(1)} %get-tuple-element.21), channel_id=1, source_target_pairs={{0,1},{1,2},{2,3},{4,5},{5,6},{6,7},{8,9},{9,10},{10,11},{12,13},{... | collective-permute-start | bytes 199688 | tf_op jit(solution)/shard_map/ppermute | solution.py:14
  168.2 13.9 %copy-start.9 = (bf16[33,130,256]{1,2,0:T(8,128)(2,1)}, bf16[33,130,256]{1,2,0:T(8,128)(2,1)S(1)}, u32[]{:S(2)}) copy-start(bf16[33,130,256]{1,2,0:T(8,128)(2,1)S(1)} %get-tuple-element.18) | copy-start | bytes 6589444
  201.3 4.2 %copy-start.14 = (bf16[32,128,256]{1,2,0:T(8,128)(2,1)S(1)}, bf16[32,128,256]{1,2,0:T(8,128)(2,1)}, u32[]{:S(2)}) copy-start(bf16[32,128,256]{1,2,0:T(8,128)(2,1)} %get-tuple-element.24) | copy-start | bytes 6291460
  208.5 4.2 %copy-start.13 = (bf16[32,128,256]{1,2,0:T(8,128)(2,1)S(1)}, bf16[32,128,256]{1,2,0:T(8,128)(2,1)}, u32[]{:S(2)}) copy-start(bf16[32,128,256]{1,2,0:T(8,128)(2,1)} %get-tuple-element.48) | copy-start | bytes 6291460
  (14 other events, 33.2 us)
Sparse Core Ops, SparseCore 0:
  241.0 136.8 all-reduce.2
where the time goes:
time: 396 us; the launch traced here: 390 us
  waiting for transfers between devices  130 us (33%)
  local copies, waits for them, and re-layouts  85.5 us (22%)
  other arithmetic  65.4 us (17%)
  matrix products  57.5 us (15%)
  starting transfers between devices  37.1 us (9%)
  between operations  15 us (4%)
    psum x1, waiting for transfers between devices, on_device(): lax.psum((local_conv_grad, local_embed_grad), ('lon', 'lat'))  128 us
    slice x9, local copies, waits for them, and re-layouts, on_device(): part = field_pad[a:a + rows, b:b + cols].reshape(cells, width)  36.8 us
    dot_general x9, matrix products, on_device(): conv = conv + jnp.dot(part, w_conv[tap], preferred_element_type=jnp.float32)  29.4 us
    concatenate x5, other arithmetic, padded(): x = jnp.concatenate([before, x, after], axis=dim)  21.3 us
    scatter-add x1, other arithmetic, on_device(): jnp.zeros((cells, width), jnp.float32).at[cell_index]  16.8 us
    unnamed x56, local copies, waits for them, and re-layouts  12.5 us
    dot_general x9, matrix products, on_device(): lax.dot_general(cpart, w_conv[tap], (((1,), (1,)), ((), ())), preferred_e...  12.5 us
    dot_general x9, matrix products, on_device(): lax.dot_general(part, cot_flat, (((0,), (0,)), ((), ())), preferred_eleme...  10.7 us
  transfers between devices with their start and end apart: 12, of which 2 were waited for; matrix products, arithmetic and copies ran while one was open for 41% of the time, Pallas kernels for 0%

commit v1 on v0

v1 whole, which is shorter than its diff:
```python
import functools

import jax
import jax.numpy as jnp
from jax import lax
from jax.experimental import pallas as pl
from jax.experimental.pallas import tpu as pltpu
from jax.sharding import PartitionSpec as P

AXES = ("lon", "lat")
BF = jnp.bfloat16
F32 = jnp.float32
I32 = jnp.int32
VMEM_LIMIT = 56 << 20


def dot(a, b, ca=1, cb=0):
    return lax.dot_general(a, b, (((ca,), (cb,)), ((), ())), preferred_element_type=F32)


def iota(shape, dim):
    return lax.broadcasted_iota(I32, shape, dim)


def kernel_call(body, outs, args, flops=0, scratch=(), smem=(), hbm=()):
    spaces = [
        pltpu.SMEM if i in smem else pl.ANY if i in hbm else pltpu.VMEM for i in range(len(args))
    ]
    moved = sum(a.size * a.dtype.itemsize for a in args) + sum(
        o.size * o.dtype.itemsize for o in outs
    )
    return pl.pallas_call(
        body,
        out_shape=list(outs),
        in_specs=[pl.BlockSpec(memory_space=s) for s in spaces],
        out_specs=[pl.BlockSpec(memory_space=pltpu.VMEM) for _ in outs],
        scratch_shapes=list(scratch),
        compiler_params=pltpu.CompilerParams(vmem_limit_bytes=VMEM_LIMIT),
        cost_estimate=pl.CostEstimate(flops=flops, bytes_accessed=moved, transcendentals=0),
    )(*args)


def shape(dims, dtype):
    return jax.ShapeDtypeStruct(tuple(dims), dtype)


def route_body(me_ref, tile_ref, cell_ref, feat_ref, send_ref, place_ref, mask_ref, *, owners, slots):
    records = feat_ref.shape[0]
    lanes = 128
    blocks = records // lanes
    tile = tile_ref[...]
    hot = (iota((owners, records), 0) == tile).astype(F32)
    hot16 = hot.astype(BF)
    upper = (iota((lanes, lanes), 0) <= iota((lanes, lanes), 1)).astype(BF)
    carry = jnp.zeros((owners, 1), F32)
    counts = []
    for blk in range(blocks):
        local = dot(hot16[:, blk * lanes : (blk + 1) * lanes], upper)
        counts.append(local + carry)
        carry = carry + local[:, lanes - 1 : lanes]
    count = jnp.concatenate(counts, axis=1)
    rank = jnp.sum(count * hot, axis=0, keepdims=True).astype(I32) - 1
    place_ref[...] = tile * slots + rank
    shift = (me_ref[0] % (lanes // slots)) * slots
    cell = cell_ref[...]
    at = (iota((lanes, records), 0) == rank + shift).astype(BF)
    high = (hot * (cell // lanes + 1).astype(F32)).astype(BF)
    low = (hot * (cell % lanes).astype(F32)).astype(BF)
    high = dot(high, at, 1, 1)
    low = dot(low, at, 1, 1)
    zero = jnp.zeros((6, lanes), F32)
    for t in range(owners):
        extra = jnp.concatenate([high[t : t + 1], low[t : t + 1], zero], axis=0)
        send_ref[t, slots:, :] = extra.astype(BF)
    ranked = (iota((slots, records), 0) == rank).astype(BF)
    group = 512 // slots
    feat = feat_ref[...]
    for g in range(owners // group):
        for t in range(group):
            mask_ref[t * slots : (t + 1) * slots, :] = ranked * hot16[g * group + t : g * group + t + 1, :]
        rows = dot(mask_ref[...], feat).astype(BF)
        for t in range(group):
            send_ref[g * group + t, :slots, :] = rows[t * slots : (t + 1) * slots]


def unroute_body(place_ref, back_ref, out_ref):
    records = place_ref.shape[0]
    count = back_ref.shape[0]
    size = 512
    for blk in range(records // size):
        place = place_ref[blk * size : (blk + 1) * size, :]
        mask = (iota((size, count), 1) == place).astype(BF)
        out_ref[blk * size : (blk + 1) * size, :] = dot(mask, back_ref[...]).astype(BF)


def shifted(row, edge, step):
    cols = row.shape[0]
    wide = pltpu.roll(row.astype(F32), step % cols, 0)
    at = 0 if step == 1 else cols - 1
    return jnp.where(iota((cols, 1), 0) == at, edge.astype(F32), wide).astype(BF)


def fill_shifts(grid_ref, left_ref, right_ref, top_ref, bottom_ref, pad_ref):
    rows, cols, _ = grid_ref.shape

    def put(i, row, left, right):
        pad_ref[0, i] = shifted(row, left, 1)
        pad_ref[1, i] = row
        pad_ref[2, i] = shifted(row, right, -1)

    for i, ref in ((0, top_ref), (rows + 1, bottom_ref)):
        put(i, ref[0:cols, :], ref[cols : cols + 1, :], ref[cols + 8 : cols + 9, :])

    def step(i, carry):
        put(i + 1, grid_ref[i], left_ref[i], right_ref[i])
        return carry

    lax.fori_loop(0, rows, step, 0)


def conv_body(grid_ref, left_ref, right_ref, top_ref, bottom_ref, w_ref, out_ref, pad_ref, *, back):
    rows, cols, width = grid_ref.shape
    fill_shifts(grid_ref, left_ref, right_ref, top_ref, bottom_ref, pad_ref)
    high = 8

    def step(n, carry):
        i = n * high
        acc = grid_ref[pl.ds(i, high)].astype(F32).reshape(high * cols, width)
        for a in range(3):
            for b in range(3):
                part = pad_ref[b, pl.ds(i + a, high)].reshape(high * cols, width)
                tap = a * 3 + b
                acc = acc + (dot(part, w_ref[8 - tap], 1, 1) if back else dot(part, w_ref[tap]))
        out_ref[pl.ds(i, high)] = acc.astype(BF).reshape(high, cols, width)
        return carry

    lax.fori_loop(0, rows // high, step, 0)


def edges(grid):
    rows, cols, width = grid.shape
    count = lax.axis_size("lon")
    up = [(i, (i + 1) % count) for i in range(count)]
    down = [(j, i) for i, j in up]
    left = lax.ppermute(grid[:, cols - 1 :, :], "lon", up)
    right = lax.ppermute(grid[:, :1, :], "lon", down)
    count = lax.axis_size("lat")
    up = [(i, i + 1) for i in range(count - 1)]
    down = [(j, i) for i, j in up]
    pad = ((0, 7), (0, 0))

    def row(i):
        return jnp.concatenate([grid[i], jnp.pad(left[i], pad), jnp.pad(right[i], pad)], axis=0)

    top = lax.ppermute(row(rows - 1), "lat", up)
    bottom = lax.ppermute(row(0), "lat", down)
    return left, right, top, bottom


def conv(grid, halo, w, back):
    rows, cols, width = grid.shape
    outs = [shape(grid.shape, BF)]
    pad = shape((3, rows + 2, cols, width), BF)
    scratch = []
    if back:
        outs.append(pad)
    else:
        scratch.append(pltpu.VMEM(pad.shape, BF))
    flops = 18 * rows * cols * width * width
    body = functools.partial(conv_body, back=back)
    return kernel_call(body, outs, (grid, *halo, w), flops, scratch)


def gelu_parts(x):
    scale = 0.7978845608028654
    inner = scale * (x + 0.044715 * x * x * x)
    th = jnp.tanh(inner)
    value = 0.5 * x * (1.0 + th)
    slope = 0.5 * (1.0 + th) + 0.5 * x * (1.0 - th * th) * scale * (1.0 + 3 * 0.044715 * x * x)
    return value, slope


def cell_codes(recv_ref, slots):
    owners = recv_ref.shape[0]
    per = 128 // slots
    high, low = [], []
    for p in range(owners // per):
        total = recv_ref[p * per, slots : slots + 8, :].astype(F32)
        for q in range(1, per):
            total = total + recv_ref[p * per + q, slots : slots + 8, :].astype(F32)
        high.append(total[0:1])
        low.append(total[1:2])
    high = jnp.concatenate(high, axis=0)
    low = jnp.concatenate(low, axis=0)
    return (high - 1.0) * 128.0 + low


def gather_body(recv_ref, dfield_ref, w_ref, grad_ref, eg_ref, embed_ref, *, slots):
    owners = recv_ref.shape[0]
    cells = dfield_ref.shape[0]
    size = 512
    group = size // slots
    codes = cell_codes(recv_ref, slots).T.astype(I32)
    total = jnp.zeros(eg_ref.shape, F32)
    for blk in range(owners // group):
        code = jnp.concatenate([codes[:, blk * 4 + q : blk * 4 + q + 1] for q in range(4)], axis=0)
        mask = (iota((size, cells), 1) == code).astype(BF)
        rows = dot(mask, dfield_ref[...]).astype(BF)
        grad_ref[blk * size : (blk + 1) * size, :] = rows
        feat = jnp.concatenate([recv_ref[blk * group + q, :slots, :] for q in range(group)], axis=0)
        value, slope = gelu_parts(dot(feat, w_ref[...]))
        embed_ref[blk * size : (blk + 1) * size, :] = value.astype(BF)
        dh = rows.astype(F32) * slope
        part = dh.astype(BF)
        rest = (dh - part.astype(F32)).astype(BF)
        total = total + dot(feat, part, 0, 0) + dot(feat, rest, 0, 0)
    eg_ref[...] = total


def field_body(me_ref, recv_ref, embed_ref, bg_ref, pad_ref, eg_ref, field_ref, keep_ref, give_ref, acc_ref, *, slots):
    cells, width = bg_ref.shape
    cols = pad_ref.shape[2]
    half = width // 2
    codes = cell_codes(recv_ref, slots).astype(I32)
    acc_ref[...] = jnp.zeros_like(acc_ref)
    size = 512
    deep = 2 * size

    def step(n, carry):
        for k in range(deep // size):
            base = n * deep + k * size
            where = iota((size, 128), 0) + base
            mask = jnp.concatenate(
                [(where == codes[p : p + 1, :]).astype(BF) for p in range(codes.shape[0])], axis=1
            )
            at = pl.ds(pl.multiple_of(base, size), size)
            total = dot(mask, embed_ref[...]) + bg_ref[at, :].astype(F32)
            field_ref[at, :] = total.astype(BF)
        at = pl.ds(pl.multiple_of(n * deep, deep), deep)
        field = field_ref[at, :]
        high = deep // cols
        for a in range(3):
            for b in range(3):
                part = pad_ref[2 - b, pl.ds(n * high + 2 - a, high)].reshape(deep, width)
                acc_ref[3 * a + b] += dot(field, part, 0, 0)
        return carry

    lax.fori_loop(0, cells // deep, step, 0)
    side = me_ref[0] % 2
    taps = acc_ref.shape[0] * width
    inputs = eg_ref.shape[0]
    for s in range(2):
        lanes = slice(s * half, (s + 1) * half)
        for ref, want in ((keep_ref, s), (give_ref, 1 - s)):

            @pl.when(side == want)
            def _():
                for t in range(acc_ref.shape[0]):
                    ref[t * width : (t + 1) * width, :] = acc_ref[t, :, lanes]
                ref[taps : taps + inputs, :] = eg_ref[:, lanes]
                left = ref.shape[0] - taps - inputs
                if left:
                    ref[taps + inputs :, :] = jnp.zeros((left, half), F32)


def swap(x, bit):
    count = lax.axis_size("lon") * lax.axis_size("lat")
    return lax.ppermute(x, AXES, [(i, i ^ bit) for i in range(count)])


def split_body(mine_ref, *refs, moves, exact):
    terms = 0
    n = len(moves)
    ins = refs[: len(refs) - 1 - n]
    keep_ref = refs[len(refs) - 1 - n]
    outs = refs[len(refs) - n :]
    size = keep_ref.shape[0]

    def block(index):
        at = pl.ds(pl.multiple_of(index * size, 8), size)
        total = ins[0][at, :].astype(F32)
        for ref in ins[1:]:
            total = total + ref[at, :].astype(F32)
        return total

    mine = mine_ref[0]
    keep_ref[...] = block(mine).astype(keep_ref.dtype)
    for ref, move in zip(outs, moves):
        ref[...] = block(mine ^ move).astype(ref.dtype)


def join_body(mine_ref, *refs):
    out_ref = refs[-1]
    size = refs[0].shape[0]
    mine = mine_ref[0]
    for move, ref in enumerate(refs[:-1]):
        out_ref[pl.ds(pl.multiple_of((mine ^ move) * size, 8), size), :] = ref[...]


def final_body(mine_ref, own_ref, other_ref, conv_ref, embed_ref):
    side = mine_ref[0]
    half = own_ref.shape[1]
    taps, width, _ = conv_ref.shape
    inputs = embed_ref.shape[0]
    for s in range(2):
        lanes = slice(s * half, (s + 1) * half)
        for ref, want in ((own_ref, s), (other_ref, 1 - s)):

            @pl.when(side == want)
            def _():
                for t in range(taps):
                    conv_ref[t, :, lanes] = ref[t * width : (t + 1) * width, :].astype(F32)
                embed_ref[:, lanes] = ref[taps * width : taps * width + inputs, :].astype(F32)


def stages(count):
    bits, found = [], 2
    while found < count:
        bits.append(found)
        found *= 2
    return [bits[i : i + 2] for i in range(0, len(bits), 2)]


def reduce_all(me, keep, give, taps, width, inputs):
    count = lax.axis_size("lon") * lax.axis_size("lat")
    terms = [keep, swap(give, 1)]
    plan = stages(count)
    for bits in plan:
        ways = 2 ** len(bits)
        mine = (me // bits[0]) % ways
        size = terms[0].shape[0] // ways
        half = terms[0].shape[1]
        moves = list(range(1, ways))
        outs = [shape((size, half), F32)] + [shape((size, half), BF)] * len(moves)
        body = functools.partial(split_body, moves=moves, exact=False)
        own, *send = kernel_call(body, outs, (mine, *terms), smem=(0,))
        terms = [own] + [swap(x, m * bits[0]) for m, x in zip(moves, send)]
    body = functools.partial(split_body, moves=[], exact=False)
    (block,) = kernel_call(
        body, [shape(terms[0].shape, BF)], (jnp.zeros((1,), I32), *terms), smem=(0,)
    )
    for bits in reversed(plan):
        ways = 2 ** len(bits)
        mine = (me // bits[0]) % ways
        parts = [block] + [swap(block, m * bits[0]) for m in range(1, ways)]
        rows, half = block.shape
        (block,) = kernel_call(join_body, [shape((rows * ways, half), BF)], (mine, *parts), smem=(0,))
    other = swap(block, 1)
    outs = [shape((taps, width, width), F32), shape((inputs, width), F32)]
    return kernel_call(final_body, outs, (me % 2, block, other), smem=(0,))


def on_device(obs_feat, obs_tile, obs_cell, w_embed, background, w_conv, cotangent):
    lon_count = lax.axis_size("lon")
    lat_count = lax.axis_size("lat")
    owners = lon_count * lat_count
    records, inputs = obs_feat.shape
    slots = 2 * records // owners
    rows, cols, width = background.shape
    cells = rows * cols
    taps = w_conv.shape[0]
    me = (lax.axis_index("lon") * lat_count + lax.axis_index("lat")).astype(I32).reshape(1)

    outs = [shape((owners, slots + 8, inputs), BF), shape((1, records), I32)]
    send, place = kernel_call(
        functools.partial(route_body, owners=owners, slots=slots),
        outs,
        (me, obs_tile.reshape(1, records), obs_cell.reshape(1, records), obs_feat),
        flops=4 * records * records * inputs,
        scratch=[pltpu.VMEM((512, records), BF)],
        smem=(0,),
    )
    recv = lax.all_to_all(send, AXES, split_axis=0, concat_axis=0, tiled=True)

    dfield, pad = conv(cotangent, edges(cotangent), w_conv, True)

    count = owners * slots
    grad, local_eg, embed = kernel_call(
        functools.partial(gather_body, slots=slots),
        [shape((count, width), BF), shape((inputs, width), F32), shape((count, width), BF)],
        (recv, dfield.reshape(cells, width), w_embed),
        flops=2 * count * cells * width,
    )
    blocks = owners // 2
    size = 8 * blocks
    total = -(-(taps * width + inputs) // size) * size
    field, keep, give = kernel_call(
        functools.partial(field_body, slots=slots),
        [shape((cells, width), BF), shape((total, width // 2), F32), shape((total, width // 2), F32)],
        (me, recv, embed, background.reshape(cells, width), pad, local_eg),
        flops=2 * count * cells * width + 18 * cells * width * width,
        scratch=[pltpu.VMEM((taps, width, width), F32)],
        smem=(0,),
    )
    conv_grad, embed_grad = reduce_all(me, keep, give, taps, width, inputs)

    grad, field = lax.optimization_barrier((grad, field))
    back = lax.all_to_all(grad.reshape(owners, slots, width), AXES, split_axis=0, concat_axis=0, tiled=True)
    (record_grad,) = kernel_call(
        unroute_body,
        [shape((records, width), BF)],
        (place.reshape(records, 1), back.reshape(count, width)),
        flops=2 * count * records * width,
    )
    field = field.reshape(rows, cols, width)
    (encoded,) = conv(field, edges(field), w_conv, False)
    return encoded, record_grad, conv_grad, embed_grad


def solution(mesh):
    placed = (
        P(("lon", "lat"), None),
        P(("lon", "lat"), None),
        P(("lon", "lat")),
        P(),
        P("lat", "lon", None),
        P(),
        P("lat", "lon", None),
    )
    return jax.shard_map(
        on_device,
        mesh=mesh,
        in_specs=placed,
        out_specs=(P("lat", "lon", None), P(("lon", "lat"), None), P(), P()),
        check_vma=False,
    )
```

time: 396 us -> 162 us (0.41); the launches traced: 390 us -> 161 us
  waiting for transfers between devices: 130 us -> 32.5 us
  local copies, waits for them, and re-layouts: 85.5 us -> 13 us
  Pallas kernels: 0 us -> 70.4 us
  other arithmetic: 65.4 us -> 0.04 us
  matrix products: 57.5 us -> 0 us
  between operations: 15 us -> 0.92 us
  starting transfers between devices: 37.1 us -> 44.6 us
    psum x1 -> x0, waiting for transfers between devices: 128 us -> none  [on_device(): lax.psum((local_conv_grad, local_embed_grad), ('lon', 'lat'))]
    pallas_call x0 -> x12, Pallas kernels: none -> 70.4 us  [kernel_call(): pl.pallas_call(body, out_shape=list(outs), in_specs=[pl.BlockSpec(memory_...]
    dot_general x29 -> x0, matrix products: 57.5 us -> none  [the longest x9 29.4 us: on_device(): conv = conv + jnp.dot(part, w_conv[tap], preferred_element_type=jnp.float32)]
    slice x14 -> x3, local copies, waits for them, and re-layouts: 42.6 us -> 2.93 us  [the longest x2 2.05 us: edges(): right = lax.ppermute(grid[:, :1, :], 'lon', down)]
    ppermute x8 -> x22, waiting for transfers between devices: 0.02 us -> 32.5 us  [the longest x14 19.8 us: swap(): return lax.ppermute(x, AXES, [(i, i ^ bit) for i in range(count)])]
    concatenate x5 -> x4, other arithmetic: 21.3 us -> 0.04 us  [row(): jnp.concatenate([grid[i], jnp.pad(left[i], pad), jnp.pad(right[i], pad)],...]
    scatter-add x1 -> x0, other arithmetic: 16.8 us -> none  [on_device(): jnp.zeros((cells, width), jnp.float32).at[cell_index]]
    gather x2 -> x0, local copies, waits for them, and re-layouts: 15.3 us -> none  [the longest x1 10.3 us: on_device(): slot_grad = dfield[cell_index]]
  transfers between devices with their start and end apart: 12 -> 24, of which waited for: 2 -> 12; matrix products, arithmetic and copies ran while one was open for 41% -> 3% of each run, Pallas kernels for 0% -> 21%
where the time goes in v1:
time: 162 us; the launch traced here: 161 us
  Pallas kernels  70.4 us (43%)
  starting transfers between devices  44.6 us (28%)
  waiting for transfers between devices  32.5 us (20%)
  local copies, waits for them, and re-layouts  13 us (8%)
    pallas_call x12, Pallas kernels, kernel_call(): pl.pallas_call(body, out_shape=list(outs), in_specs=[pl.BlockSpec(memory_...  70.4 us
    ppermute x14, waiting for transfers between devices, swap(): return lax.ppermute(x, AXES, [(i, i ^ bit) for i in range(count)])  19.8 us
    ppermute x14, starting transfers between devices, swap(): return lax.ppermute(x, AXES, [(i, i ^ bit) for i in range(count)])  19.5 us
    unnamed x50, local copies, waits for them, and re-layouts  8.14 us
    ppermute x2, starting transfers between devices, edges(): right = lax.ppermute(grid[:, :1, :], 'lon', down)  7.54 us
    all_to_all x1, starting transfers between devices, on_device(): recv = lax.all_to_all(send, AXES, split_axis=0, concat_axis=0, tiled=True)  7.3 us
    ppermute x2, waiting for transfers between devices, edges(): left = lax.ppermute(grid[:, cols - 1:, :], 'lon', up)  4.89 us
    ppermute x2, waiting for transfers between devices, edges(): right = lax.ppermute(grid[:, :1, :], 'lon', down)  4.23 us
  transfers between devices with their start and end apart: 24, of which 12 were waited for; matrix products, arithmetic and copies ran while one was open for 3% of the time, Pallas kernels for 21%

profile of v1, /device:TPU:0, one launch (start us, length us, event | category | flops | bytes accessed | tf_op | source)
XLA Modules:
  0.0 161.4 jit_solution(14743030162316350798)
XLA Ops:
  0.6 3.5 %shard_map.102 = (bf16[32,72,128]{2,1,0:T(8,128)(2,1)}, s32[1,1024]{1,0:T(1,128)}) custom-call(s32[1]{0:T(128)} %bitcast.me_ref, s32[1,1024]{1,0:T(1,128)} %bitcast.34, s32[1,1024]{1,0:T(1,128)} %bitcast.35, bf16[1024,128]{1,0:T(8,128)(2,1)} %feat_ref.1), custom_call_target="tpu_custom_call" | custom-call | flops 536870912 | bytes 864260 | tf_op jit(solution)/shard_map/pallas_call | solution.py:32
  4.1 7.3 %all-to-all-start = ((bf16[32,72,128]{2,1,0:T(8,128)(2,1)}), bf16[32,72,128]{2,1,0:T(8,128)(2,1)S(1)}, u32[]{:S(2)}, u32[]{:S(2)}) async-start(bf16[32,72,128]{2,1,0:T(8,128)(2,1)} %get-tuple-element.26), calls=%async_computation | async-start | bytes 1179648 | tf_op jit(solution)/shard_map/all_to_all | solution.py:373
  14.2 3.0 %collective-permute-start.1 = (bf16[32,1,256]{2,1,0:T(2,128)(2,1)S(1)}, bf16[32,1,256]{2,1,0:T(2,128)(2,1)S(1)}, u32[]{:S(2)}, u32[]{:S(2)}) collective-permute-start(bf16[32,1,256]{2,1,0:T(2,128)(2,1)S(1)} %get-tuple-element.54), channel_id=1, source_target_pairs={{4,0},{8,4},{12,8},{16,12},{20,16},{24,20},{28,24},{0,28},{5,1},{9... | collective-permute-start | bytes 49160 | tf_op jit(solution)/shard_map/ppermute | solution.py:146
  18.1 4.2 %collective-permute-done.1.right_ref = bf16[32,1,256]{2,1,0:T(2,128)(2,1)S(1)} collective-permute-done((bf16[32,1,256]{2,1,0:T(2,128)(2,1)S(1)}, bf16[32,1,256]{2,1,0:T(2,128)(2,1)S(1)}, u32[]{:S(2)}, u32[]{:S(2)}) %collective-permute-start.1) | collective-permute-done | bytes 16416 | tf_op jit(solution)/shard_map/ppermute | solution.py:146
  22.3 4.9 %collective-permute-done.left_ref = bf16[32,1,256]{2,1,0:T(2,128)(2,1)S(1)} collective-permute-done((bf16[32,1,256]{2,1,0:T(2,128)(2,1)S(1)}, bf16[32,1,256]{2,1,0:T(2,128)(2,1)S(1)}, u32[]{:S(2)}, u32[]{:S(2)}) %collective-permute-start) | collective-permute-done | bytes 16416 | tf_op jit(solution)/shard_map/ppermute | solution.py:145
  29.9 3.6 %collective-permute-done.3.bottom_ref = bf16[144,256]{1,0:T(8,128)(2,1)S(1)} collective-permute-done((bf16[144,256]{1,0:T(8,128)(2,1)S(1)}, bf16[144,256]{1,0:T(8,128)(2,1)S(1)}, u32[]{:S(2)}, u32[]{:S(2)}) %collective-permute-start.3) | collective-permute-done | bytes 73760 | tf_op jit(solution)/shard_map/ppermute | solution.py:156
  34.1 10.9 %shard_map.103 = (bf16[32,128,256]{2,1,0:T(8,128)(2,1)}, bf16[3,34,128,256]{3,2,1,0:T(8,128)(2,1)}) custom-call(bf16[32,128,256]{2,1,0:T(8,128)(2,1)} %grid_ref.1, bf16[32,1,256]{2,1,0:T(2,128)(2,1)} %copy-done.19, bf16[32,1,256]{2,1,0:T(2,128)(2,1)} %copy-done.20, bf16[144,256]{1,0:T(8,128)(2,1)} %copy-done.23, bf16[144,256]{1,0:T(8,128)(2,1)} %copy-done.24, ...), custom_call_target="tpu_custom_call" | custom-call | flops 4831838208 | bytes 12238848 | tf_op jit(solution)/shard_map/pallas_call | solution.py:32
  45.8 11.7 %shard_map.104 = (bf16[2048,256]{1,0:T(8,128)(2,1)}, f32[128,256]{1,0:T(8,128)}, bf16[2048,256]{1,0:T(8,128)(2,1)}) custom-call(bf16[32,72,128]{2,1,0:T(8,128)(2,1)} %copy-done.3, bf16[4096,256]{1,0:T(8,128)(2,1)} %bitcast.36, bf16[128,256]{1,0:T(8,128)(2,1)} %w_ref.4), custom_call_target="tpu_custom_call" | custom-call | flops 4294967296 | bytes 4980736 | tf_op jit(solution)/shard_map/pallas_call | solution.py:32
  57.4 18.5 %shard_map.105 = (bf16[4096,256]{1,0:T(8,128)(2,1)}, f32[2432,128]{1,0:T(8,128)}, f32[2432,128]{1,0:T(8,128)}) custom-call(s32[1]{0:T(128)} %bitcast.me_ref, bf16[32,72,128]{2,1,0:T(8,128)(2,1)} %copy-done.3, bf16[2048,256]{1,0:T(8,128)(2,1)} %get-tuple-element.29.embed_ref, bf16[4096,256]{1,0:T(8,128)(2,1)} %bitcast.33, ...), custom_call_target="tpu_custom_call" | custom-call | flops 9126805504 | bytes 15138820 | tf_op jit(solution)/shard_map/pallas_call | solution.py:32
  75.9 3.0 %collective-permute-start.8 = (f32[2432,128]{1,0:T(8,128)}, f32[2432,128]{1,0:T(8,128)S(1)}, u32[]{:S(2)}, u32[]{:S(2)}) collective-permute-start(f32[2432,128]{1,0:T(8,128)} %get-tuple-element.37), channel_id=1, source_target_pairs={{0,1},{1,0},{2,3},{3,2},{4,5},{5,4},{6,7},{7,6},{8,9},{9,8},{10,11... | collective-permute-start | bytes 3735560 | tf_op jit(solution)/shard_map/ppermute | solution.py:268
  79.0 3.1 %all-to-all-start.1 = ((bf16[32,64,256]{2,1,0:T(8,128)(2,1)}), bf16[32,64,256]{2,1,0:T(8,128)(2,1)S(1)}, u32[]{:S(2)}, u32[]{:S(2)}) async-start(bf16[32,64,256]{2,1,0:T(8,128)(2,1)} %bitcast.17), calls=%async_computation.1 | async-start | bytes 2097152 | tf_op jit(solution)/shard_map/all_to_all | solution.py:398
  83.2 4.6 %collective-permute-start.5 = (bf16[32,1,256]{2,1,0:T(2,128)(2,1)S(1)}, bf16[32,1,256]{2,1,0:T(2,128)(2,1)S(1)}, u32[]{:S(2)}, u32[]{:S(2)}) collective-permute-start(bf16[32,1,256]{2,1,0:T(2,128)(2,1)S(1)} %get-tuple-element.50), channel_id=1, source_target_pairs={{4,0},{8,4},{12,8},{16,12},{20,16},{24,20},{28,24},{0,28},{5,1},{9... | collective-permute-start | bytes 49160 | tf_op jit(solution)/shard_map/ppermute | solution.py:146
  88.8 2.6 %shard_map.108 = (f32[608,128]{1,0:T(8,128)}, bf16[608,128]{1,0:T(8,128)(2,1)}, bf16[608,128]{1,0:T(8,128)(2,1)}, bf16[608,128]{1,0:T(8,128)(2,1)}) custom-call(s32[1]{0:T(128)S(6)} %select_n.31.mine_ref, f32[2432,128]{1,0:T(8,128)} %get-tuple-element.36.refs_0_, f32[2432,128]{1,0:T(8,128)} %copy-done), custom_call_target="tpu_custom_call" | custom-call | bytes 3268612 | tf_op jit(solution)/shard_map/pallas_call | solution.py:32
  95.9 4.6 %collective-permute-done.9.refs_1_ = bf16[608,128]{1,0:T(8,128)(2,1)S(1)} collective-permute-done((bf16[608,128]{1,0:T(8,128)(2,1)}, bf16[608,128]{1,0:T(8,128)(2,1)S(1)}, u32[]{:S(2)}, u32[]{:S(2)}) %collective-permute-start.9) | collective-permute-done | bytes 155680 | tf_op jit(solution)/shard_map/ppermute | solution.py:268
  101.6 3.5 %collective-permute-done.11.refs_3_ = bf16[608,128]{1,0:T(8,128)(2,1)S(1)} collective-permute-done((bf16[608,128]{1,0:T(8,128)(2,1)}, bf16[608,128]{1,0:T(8,128)(2,1)S(1)}, u32[]{:S(2)}, u32[]{:S(2)}) %collective-permute-start.11) | collective-permute-done | bytes 155680 | tf_op jit(solution)/shard_map/ppermute | solution.py:268
  108.4 2.6 %collective-permute-start.13 = (bf16[152,128]{1,0:T(8,128)(2,1)}, bf16[152,128]{1,0:T(8,128)(2,1)S(1)}, u32[]{:S(2)}, u32[]{:S(2)}) collective-permute-start(bf16[152,128]{1,0:T(8,128)(2,1)} %get-tuple-element.44), channel_id=1, source_target_pairs={{0,16},{1,17},{2,18},{3,19},{4,20},{5,21},{6,22},{7,23},{8,24},{9,... | collective-permute-start | bytes 116744 | tf_op jit(solution)/shard_map/ppermute | solution.py:268
  113.9 3.1 %collective-permute-done.14.refs_3_ = bf16[152,128]{1,0:T(8,128)(2,1)S(1)} collective-permute-done((bf16[152,128]{1,0:T(8,128)(2,1)}, bf16[152,128]{1,0:T(8,128)(2,1)S(1)}, u32[]{:S(2)}, u32[]{:S(2)}) %collective-permute-start.14) | collective-permute-done | bytes 38944 | tf_op jit(solution)/shard_map/ppermute | solution.py:268
  120.8 2.7 %collective-permute-start.17 = (bf16[152,128]{1,0:T(8,128)(2,1)}, bf16[152,128]{1,0:T(8,128)(2,1)S(1)}, u32[]{:S(2)}, u32[]{:S(2)}) collective-permute-start(bf16[152,128]{1,0:T(8,128)(2,1)} %shard_map.110.refs_0_), channel_id=1, source_target_pairs={{0,24},{1,25},{2,26},{3,27},{4,28},{5,29},{6,30},{7,31},{8,16},{9,... | collective-permute-start | bytes 116744 | tf_op jit(solution)/shard_map/ppermute | solution.py:268
  124.2 2.6 %collective-permute-done.17.refs_3_ = bf16[152,128]{1,0:T(8,128)(2,1)S(1)} collective-permute-done((bf16[152,128]{1,0:T(8,128)(2,1)}, bf16[152,128]{1,0:T(8,128)(2,1)S(1)}, u32[]{:S(2)}, u32[]{:S(2)}) %collective-permute-start.17) | collective-permute-done | bytes 38944 | tf_op jit(solution)/shard_map/ppermute | solution.py:268
  135.5 2.0 %collective-permute-done.20.refs_3_ = bf16[608,128]{1,0:T(8,128)(2,1)S(1)} collective-permute-done((bf16[608,128]{1,0:T(8,128)(2,1)}, bf16[608,128]{1,0:T(8,128)(2,1)S(1)}, u32[]{:S(2)}, u32[]{:S(2)}) %collective-permute-start.20) | collective-permute-done | bytes 155680 | tf_op jit(solution)/shard_map/ppermute | solution.py:268
  138.2 2.0 %shard_map.112.own_ref = bf16[2432,128]{1,0:T(8,128)(2,1)} custom-call(s32[1]{0:T(128)S(6)} %select_n.31.mine_ref, bf16[608,128]{1,0:T(8,128)(2,1)} %shard_map.111.refs_0_, bf16[608,128]{1,0:T(8,128)(2,1)} %copy-done.4, bf16[608,128]{1,0:T(8,128)(2,1)} %copy-done.5, bf16[608,128]{1,0:T(8,128)(2,1)} %copy-done.7), custom_call_target="tpu_custom_call" | custom-call | bytes 1245188 | tf_op jit(solution)/shard_map/pallas_call | solution.py:32
  143.2 10.0 %shard_map.106 = bf16[32,128,256]{2,1,0:T(8,128)(2,1)} custom-call(bf16[32,128,256]{2,1,0:T(8,128)(2,1)} %bitcast.31, bf16[32,1,256]{2,1,0:T(2,128)(2,1)} %copy-done.18, bf16[32,1,256]{2,1,0:T(2,128)(2,1)} %copy-done.17, bf16[144,256]{1,0:T(8,128)(2,1)} %copy-done.21, bf16[144,256]{1,0:T(8,128)(2,1)} %copy-done.22, bf16[9,256,256]{2,1,0:T(8,128)(2,1)} %w_ref.5), custom_call_target="tpu_custom_call" | custom-call | flops 4831838208 | bytes 5554176 | tf_op jit(solution)/shard_map/pallas_call | solution.py:32
  154.2 3.5 %shard_map.107 = bf16[1024,256]{1,0:T(8,128)(2,1)} custom-call(s32[1024,1]{1,0:T(8,128)} %copy.11.place_ref, bf16[2048,256]{1,0:T(8,128)(2,1)} %bitcast.29), custom_call_target="tpu_custom_call" | custom-call | flops 1073741824 | bytes 1576960 | tf_op jit(solution)/shard_map/pallas_call | solution.py:32
  158.5 2.9 %shard_map.113 = (f32[9,256,256]{2,1,0:T(8,128)}, f32[128,256]{1,0:T(8,128)}) custom-call(s32[1]{0:T(128)S(6)} %select_n.29.mine_ref, bf16[2432,128]{1,0:T(8,128)(2,1)} %shard_map.112.own_ref, bf16[2432,128]{1,0:T(8,128)(2,1)} %copy-done.2), custom_call_target="tpu_custom_call" | custom-call | bytes 3735556 | tf_op jit(solution)/shard_map/pallas_call | solution.py:32
  (99 shorter events, 40.2 us)
Async XLA Ops:
  4.1 40.9 %all-to-all-start = ((bf16[32,72,128]{2,1,0:T(8,128)(2,1)}), bf16[32,72,128]{2,1,0:T(8,128)(2,1)S(1)}, u32[]{:S(2)}, u32[]{:S(2)}) async-start(bf16[32,72,128]{2,1,0:T(8,128)(2,1)} %get-tuple-element.26), calls=%async_computation | async-start | bytes 1179648 | tf_op jit(solution)/shard_map/all_to_all | solution.py:373
  12.4 14.8 %collective-permute-start = (bf16[32,1,256]{2,1,0:T(2,128)(2,1)S(1)}, bf16[32,1,256]{2,1,0:T(2,128)(2,1)S(1)}, u32[]{:S(2)}, u32[]{:S(2)}) collective-permute-start(bf16[32,1,256]{2,1,0:T(2,128)(2,1)S(1)} %get-tuple-element.55), channel_id=1, source_target_pairs={{0,4},{4,8},{8,12},{12,16},{16,20},{20,24},{24,28},{28,0},{1,5},{5... | collective-permute-start | bytes 49160 | tf_op jit(solution)/shard_map/ppermute | solution.py:145
  14.2 8.1 %collective-permute-start.1 = (bf16[32,1,256]{2,1,0:T(2,128)(2,1)S(1)}, bf16[32,1,256]{2,1,0:T(2,128)(2,1)S(1)}, u32[]{:S(2)}, u32[]{:S(2)}) collective-permute-start(bf16[32,1,256]{2,1,0:T(2,128)(2,1)S(1)} %get-tuple-element.54), channel_id=1, source_target_pairs={{4,0},{8,4},{12,8},{16,12},{20,16},{24,20},{28,24},{0,28},{5,1},{9... | collective-permute-start | bytes 49160 | tf_op jit(solution)/shard_map/ppermute | solution.py:146
  27.2 2.6 %collective-permute-start.2 = (bf16[144,256]{1,0:T(8,128)(2,1)S(1)}, bf16[144,256]{1,0:T(8,128)(2,1)S(1)}, u32[]{:S(2)}, u32[]{:S(2)}) collective-permute-start(bf16[144,256]{1,0:T(8,128)(2,1)S(1)} %fusion.5), channel_id=1, source_target_pairs={{0,1},{1,2},{2,3},{4,5},{5,6},{6,7},{8,9},{9,10},{10,11},{12,13},{... | collective-permute-start | bytes 221192 | tf_op jit(solution)/shard_map/ppermute | solution.py:155
  28.6 4.9 %collective-permute-start.3 = (bf16[144,256]{1,0:T(8,128)(2,1)S(1)}, bf16[144,256]{1,0:T(8,128)(2,1)S(1)}, u32[]{:S(2)}, u32[]{:S(2)}) collective-permute-start(bf16[144,256]{1,0:T(8,128)(2,1)S(1)} %fusion.6), channel_id=1, source_target_pairs={{1,0},{2,1},{3,2},{5,4},{6,5},{7,6},{9,8},{10,9},{11,10},{13,12},{... | collective-permute-start | bytes 221192 | tf_op jit(solution)/shard_map/ppermute | solution.py:156
  75.9 11.8 %collective-permute-start.8 = (f32[2432,128]{1,0:T(8,128)}, f32[2432,128]{1,0:T(8,128)S(1)}, u32[]{:S(2)}, u32[]{:S(2)}) collective-permute-start(f32[2432,128]{1,0:T(8,128)} %get-tuple-element.37), channel_id=1, source_target_pairs={{0,1},{1,0},{2,3},{3,2},{4,5},{5,4},{6,7},{7,6},{8,9},{9,8},{10,11... | collective-permute-start | bytes 3735560 | tf_op jit(solution)/shard_map/ppermute | solution.py:268
  79.0 74.3 %all-to-all-start.1 = ((bf16[32,64,256]{2,1,0:T(8,128)(2,1)}), bf16[32,64,256]{2,1,0:T(8,128)(2,1)S(1)}, u32[]{:S(2)}, u32[]{:S(2)}) async-start(bf16[32,64,256]{2,1,0:T(8,128)(2,1)} %bitcast.17), calls=%async_computation.1 | async-start | bytes 2097152 | tf_op jit(solution)/shard_map/all_to_all | solution.py:398
  83.2 28.9 %collective-permute-start.5 = (bf16[32,1,256]{2,1,0:T(2,128)(2,1)S(1)}, bf16[32,1,256]{2,1,0:T(2,128)(2,1)S(1)}, u32[]{:S(2)}, u32[]{:S(2)}) collective-permute-start(bf16[32,1,256]{2,1,0:T(2,128)(2,1)S(1)} %get-tuple-element.50), channel_id=1, source_target_pairs={{4,0},{8,4},{12,8},{16,12},{20,16},{24,20},{28,24},{0,28},{5,1},{9... | collective-permute-start | bytes 49160 | tf_op jit(solution)/shard_map/ppermute | solution.py:146
  91.5 9.1 %collective-permute-start.9 = (bf16[608,128]{1,0:T(8,128)(2,1)}, bf16[608,128]{1,0:T(8,128)(2,1)S(1)}, u32[]{:S(2)}, u32[]{:S(2)}) collective-permute-start(bf16[608,128]{1,0:T(8,128)(2,1)} %get-tuple-element.39), channel_id=1, source_target_pairs={{0,2},{1,3},{2,0},{3,1},{4,6},{5,7},{6,4},{7,5},{8,10},{9,11},{10,... | collective-permute-start | bytes 466952 | tf_op jit(solution)/shard_map/ppermute | solution.py:268
  93.0 8.7 %collective-permute-start.10 = (bf16[608,128]{1,0:T(8,128)(2,1)}, bf16[608,128]{1,0:T(8,128)(2,1)S(1)}, u32[]{:S(2)}, u32[]{:S(2)}) collective-permute-start(bf16[608,128]{1,0:T(8,128)(2,1)} %get-tuple-element.40), channel_id=1, source_target_pairs={{0,4},{1,5},{2,6},{3,7},{4,0},{5,1},{6,2},{7,3},{8,12},{9,13},{10,... | collective-permute-start | bytes 466952 | tf_op jit(solution)/shard_map/ppermute | solution.py:268
  93.0 12.2 %collective-permute-start.11 = (bf16[608,128]{1,0:T(8,128)(2,1)}, bf16[608,128]{1,0:T(8,128)(2,1)S(1)}, u32[]{:S(2)}, u32[]{:S(2)}) collective-permute-start(bf16[608,128]{1,0:T(8,128)(2,1)} %get-tuple-element.41), channel_id=1, source_target_pairs={{0,6},{1,7},{2,4},{3,5},{4,2},{5,3},{6,0},{7,1},{8,14},{9,15},{10,... | collective-permute-start | bytes 466952 | tf_op jit(solution)/shard_map/ppermute | solution.py:268
  95.8 27.6 %collective-permute-start.4 = (bf16[32,1,256]{2,1,0:T(2,128)(2,1)S(1)}, bf16[32,1,256]{2,1,0:T(2,128)(2,1)S(1)}, u32[]{:S(2)}, u32[]{:S(2)}) collective-permute-start(bf16[32,1,256]{2,1,0:T(2,128)(2,1)S(1)} %get-tuple-element.51), channel_id=1, source_target_pairs={{0,4},{4,8},{8,12},{12,16},{16,20},{20,24},{24,28},{28,0},{1,5},{5... | collective-permute-start | bytes 49160 | tf_op jit(solution)/shard_map/ppermute | solution.py:145
  107.7 4.4 %collective-permute-start.12 = (bf16[152,128]{1,0:T(8,128)(2,1)}, bf16[152,128]{1,0:T(8,128)(2,1)S(1)}, u32[]{:S(2)}, u32[]{:S(2)}) collective-permute-start(bf16[152,128]{1,0:T(8,128)(2,1)} %get-tuple-element.43), channel_id=1, source_target_pairs={{0,8},{1,9},{2,10},{3,11},{4,12},{5,13},{6,14},{7,15},{8,0},{9,1},... | collective-permute-start | bytes 116744 | tf_op jit(solution)/shard_map/ppermute | solution.py:268
  108.4 5.5 %collective-permute-start.13 = (bf16[152,128]{1,0:T(8,128)(2,1)}, bf16[152,128]{1,0:T(8,128)(2,1)S(1)}, u32[]{:S(2)}, u32[]{:S(2)}) collective-permute-start(bf16[152,128]{1,0:T(8,128)(2,1)} %get-tuple-element.44), channel_id=1, source_target_pairs={{0,16},{1,17},{2,18},{3,19},{4,20},{5,21},{6,22},{7,23},{8,24},{9,... | collective-permute-start | bytes 116744 | tf_op jit(solution)/shard_map/ppermute | solution.py:268
  110.9 6.0 %collective-permute-start.14 = (bf16[152,128]{1,0:T(8,128)(2,1)}, bf16[152,128]{1,0:T(8,128)(2,1)S(1)}, u32[]{:S(2)}, u32[]{:S(2)}) collective-permute-start(bf16[152,128]{1,0:T(8,128)(2,1)} %get-tuple-element.45), channel_id=1, source_target_pairs={{0,24},{1,25},{2,26},{3,27},{4,28},{5,29},{6,30},{7,31},{8,16},{9,... | collective-permute-start | bytes 116744 | tf_op jit(solution)/shard_map/ppermute | solution.py:268
  119.1 4.4 %collective-permute-start.15 = (bf16[152,128]{1,0:T(8,128)(2,1)}, bf16[152,128]{1,0:T(8,128)(2,1)S(1)}, u32[]{:S(2)}, u32[]{:S(2)}) collective-permute-start(bf16[152,128]{1,0:T(8,128)(2,1)} %shard_map.110.refs_0_), channel_id=1, source_target_pairs={{0,8},{1,9},{2,10},{3,11},{4,12},{5,13},{6,14},{7,15},{8,0},{9,1},... | collective-permute-start | bytes 116744 | tf_op jit(solution)/shard_map/ppermute | solution.py:268
  119.1 5.1 %collective-permute-start.16 = (bf16[152,128]{1,0:T(8,128)(2,1)}, bf16[152,128]{1,0:T(8,128)(2,1)S(1)}, u32[]{:S(2)}, u32[]{:S(2)}) collective-permute-start(bf16[152,128]{1,0:T(8,128)(2,1)} %shard_map.110.refs_0_), channel_id=1, source_target_pairs={{0,16},{1,17},{2,18},{3,19},{4,20},{5,21},{6,22},{7,23},{8,24},{9,... | collective-permute-start | bytes 116744 | tf_op jit(solution)/shard_map/ppermute | solution.py:268
  120.8 6.0 %collective-permute-start.17 = (bf16[152,128]{1,0:T(8,128)(2,1)}, bf16[152,128]{1,0:T(8,128)(2,1)S(1)}, u32[]{:S(2)}, u32[]{:S(2)}) collective-permute-start(bf16[152,128]{1,0:T(8,128)(2,1)} %shard_map.110.refs_0_), channel_id=1, source_target_pairs={{0,24},{1,25},{2,26},{3,27},{4,28},{5,29},{6,30},{7,31},{8,16},{9,... | collective-permute-start | bytes 116744 | tf_op jit(solution)/shard_map/ppermute | solution.py:268
  128.9 6.1 %collective-permute-start.18 = (bf16[608,128]{1,0:T(8,128)(2,1)}, bf16[608,128]{1,0:T(8,128)(2,1)S(1)}, u32[]{:S(2)}, u32[]{:S(2)}) collective-permute-start(bf16[608,128]{1,0:T(8,128)(2,1)} %shard_map.111.refs_0_), channel_id=1, source_target_pairs={{0,2},{1,3},{2,0},{3,1},{4,6},{5,7},{6,4},{7,5},{8,10},{9,11},{10,... | collective-permute-start | bytes 466952 | tf_op jit(solution)/shard_map/ppermute | solution.py:268
  130.0 5.4 %collective-permute-start.19 = (bf16[608,128]{1,0:T(8,128)(2,1)}, bf16[608,128]{1,0:T(8,128)(2,1)S(1)}, u32[]{:S(2)}, u32[]{:S(2)}) collective-permute-start(bf16[608,128]{1,0:T(8,128)(2,1)} %shard_map.111.refs_0_), channel_id=1, source_target_pairs={{0,4},{1,5},{2,6},{3,7},{4,0},{5,1},{6,2},{7,3},{8,12},{9,13},{10,... | collective-permute-start | bytes 466952 | tf_op jit(solution)/shard_map/ppermute | solution.py:268
  130.9 6.6 %collective-permute-start.20 = (bf16[608,128]{1,0:T(8,128)(2,1)}, bf16[608,128]{1,0:T(8,128)(2,1)S(1)}, u32[]{:S(2)}, u32[]{:S(2)}) collective-permute-start(bf16[608,128]{1,0:T(8,128)(2,1)} %shard_map.111.refs_0_), channel_id=1, source_target_pairs={{0,6},{1,7},{2,4},{3,5},{4,2},{5,3},{6,0},{7,1},{8,14},{9,15},{10,... | collective-permute-start | bytes 466952 | tf_op jit(solution)/shard_map/ppermute | solution.py:268
  132.4 9.6 %collective-permute-start.6 = (bf16[144,256]{1,0:T(8,128)(2,1)S(1)}, bf16[144,256]{1,0:T(8,128)(2,1)S(1)}, u32[]{:S(2)}, u32[]{:S(2)}) collective-permute-start(bf16[144,256]{1,0:T(8,128)(2,1)S(1)} %fusion.7), channel_id=1, source_target_pairs={{0,1},{1,2},{2,3},{4,5},{5,6},{6,7},{8,9},{9,10},{10,11},{12,13},{... | collective-permute-start | bytes 221192 | tf_op jit(solution)/shard_map/ppermute | solution.py:155
  133.7 8.2 %collective-permute-start.7 = (bf16[144,256]{1,0:T(8,128)(2,1)S(1)}, bf16[144,256]{1,0:T(8,128)(2,1)S(1)}, u32[]{:S(2)}, u32[]{:S(2)}) collective-permute-start(bf16[144,256]{1,0:T(8,128)(2,1)S(1)} %fusion.8), channel_id=1, source_target_pairs={{1,0},{2,1},{3,2},{5,4},{6,5},{7,6},{9,8},{10,9},{11,10},{13,12},{... | collective-permute-start | bytes 221192 | tf_op jit(solution)/shard_map/ppermute | solution.py:156
  140.2 17.5 %collective-permute-start.21 = (bf16[2432,128]{1,0:T(8,128)(2,1)}, bf16[2432,128]{1,0:T(8,128)(2,1)S(1)}, u32[]{:S(2)}, u32[]{:S(2)}) collective-permute-start(bf16[2432,128]{1,0:T(8,128)(2,1)} %shard_map.112.own_ref), channel_id=1, source_target_pairs={{0,1},{1,0},{2,3},{3,2},{4,5},{5,4},{6,7},{7,6},{8,9},{9,8},{10,11... | collective-permute-start | bytes 1867784 | tf_op jit(solution)/shard_map/ppermute | solution.py:268
  (25 other events, 153.4 us)

commit v2 on v1

v2 whole, which is shorter than its diff:
```python
import functools
import math

import jax
import jax.numpy as jnp
from jax import lax
from jax.experimental import pallas as pl
from jax.experimental.pallas import tpu as pltpu
from jax.sharding import PartitionSpec as P

AXES = ("lon", "lat")
BF = jnp.bfloat16
F32 = jnp.float32
I32 = jnp.int32


def dot(a, b, ca=1, cb=0):
    return lax.dot_general(a, b, (((ca,), (cb,)), ((), ())), preferred_element_type=F32)


def iota(shape, dim):
    return lax.broadcasted_iota(I32, shape, dim)


def kernel_call(body, outs, args, flops=0, scratch=(), smem=(), hbm=(), far=(), temp=2):
    spaces = [
        pltpu.SMEM if i in smem else pltpu.HBM if i in hbm else pltpu.VMEM for i in range(len(args))
    ]
    near = [a for i, a in enumerate(args) if i not in hbm]
    near += [o for i, o in enumerate(outs) if i not in far]
    near += [r for r in scratch if getattr(r, "memory_space", None) == pltpu.VMEM]
    held = sum(math.prod(r.shape) * r.dtype.itemsize for r in near)
    moved = sum(math.prod(r.shape) * r.dtype.itemsize for r in (*args, *outs))
    limit = (held // (1 << 20) + 1 + temp) << 20
    return pl.pallas_call(
        body,
        out_shape=[pltpu.HBM(o.shape, o.dtype) if i in far else o for i, o in enumerate(outs)],
        in_specs=[pl.BlockSpec(memory_space=s) for s in spaces],
        out_specs=[
            pl.BlockSpec(memory_space=pltpu.HBM if i in far else pltpu.VMEM) for i in range(len(outs))
        ],
        scratch_shapes=list(scratch),
        compiler_params=pltpu.CompilerParams(vmem_limit_bytes=limit),
        cost_estimate=pl.CostEstimate(flops=flops, bytes_accessed=moved, transcendentals=0),
    )(*[pltpu.with_memory_space_constraint(a, pltpu.HBM) if i in hbm else a for i, a in enumerate(args)])


def begin(src, dst, sem):
    move = pltpu.make_async_copy(src, dst, sem)
    move.start()
    return move


DMA = pltpu.SemaphoreType.DMA


def shape(dims, dtype):
    return jax.ShapeDtypeStruct(tuple(dims), dtype)


def route_body(
    me_ref, tile_hbm, cell_hbm, feat_hbm, send_ref, place_ref,
    mask_ref, tile_ref, cell_ref, feat_ref, sems, *, owners, slots,
):
    load_tile = begin(tile_hbm, tile_ref, sems.at[0])
    load_cell = begin(cell_hbm, cell_ref, sems.at[1])
    load_feat = begin(feat_hbm, feat_ref, sems.at[2])
    load_tile.wait()
    records = feat_ref.shape[0]
    lanes = 128
    blocks = records // lanes
    tile = tile_ref[...]
    hot = (iota((owners, records), 0) == tile).astype(F32)
    hot16 = hot.astype(BF)
    upper = (iota((lanes, lanes), 0) <= iota((lanes, lanes), 1)).astype(BF)
    carry = jnp.zeros((owners, 1), F32)
    counts = []
    for blk in range(blocks):
        local = dot(hot16[:, blk * lanes : (blk + 1) * lanes], upper)
        counts.append(local + carry)
        carry = carry + local[:, lanes - 1 : lanes]
    count = jnp.concatenate(counts, axis=1)
    rank = jnp.sum(count * hot, axis=0, keepdims=True).astype(I32) - 1
    place_ref[...] = tile * slots + rank
    shift = (me_ref[0] % (lanes // slots)) * slots
    load_cell.wait()
    cell = cell_ref[...]
    at = (iota((lanes, records), 0) == rank + shift).astype(BF)
    high = (hot * (cell // lanes + 1).astype(F32)).astype(BF)
    low = (hot * (cell % lanes).astype(F32)).astype(BF)
    high = dot(high, at, 1, 1)
    low = dot(low, at, 1, 1)
    zero = jnp.zeros((6, lanes), F32)
    for t in range(owners):
        extra = jnp.concatenate([high[t : t + 1], low[t : t + 1], zero], axis=0)
        send_ref[t, slots:, :] = extra.astype(BF)
    ranked = (iota((slots, records), 0) == rank).astype(BF)
    group = 512 // slots
    load_feat.wait()
    feat = feat_ref[...]
    for g in range(owners // group):
        for t in range(group):
            mask_ref[t * slots : (t + 1) * slots, :] = ranked * hot16[g * group + t : g * group + t + 1, :]
        rows = dot(mask_ref[...], feat).astype(BF)
        for t in range(group):
            send_ref[g * group + t, :slots, :] = rows[t * slots : (t + 1) * slots]


def unroute_body(place_ref, back_ref, out_ref):
    records = place_ref.shape[0]
    count = back_ref.shape[0]
    size = 512
    for blk in range(records // size):
        place = place_ref[blk * size : (blk + 1) * size, :]
        mask = (iota((size, count), 1) == place).astype(BF)
        out_ref[blk * size : (blk + 1) * size, :] = dot(mask, back_ref[...]).astype(BF)


def shifted(row, edge, step):
    cols = row.shape[0]
    wide = pltpu.roll(row.astype(F32), step % cols, 0)
    at = 0 if step == 1 else cols - 1
    return jnp.where(iota((cols, 1), 0) == at, edge.astype(F32), wide).astype(BF)


def conv_body(inside_ref, grid_hbm, left_ref, right_ref, top_ref, bottom_ref, w_hbm, *refs, back):
    if back:
        out_hbm, pad_hbm, grid_ref, w_ref, pad_ref, out_ref, in_sem, w_sem, out_sem, pad_sem = refs
    else:
        out_hbm, grid_ref, w_ref, pad_ref, out_ref, in_sem, w_sem, out_sem = refs
    rows, cols, width = grid_ref.shape
    high = 8
    blocks = rows // high

    def band(n):
        return slice(n * high, (n + 1) * high)

    loads = [begin(grid_hbm.at[band(n)], grid_ref.at[band(n)], in_sem.at[n]) for n in range(blocks)]
    load_w = begin(w_hbm, w_ref, w_sem)

    def put(i, row, left, right):
        pad_ref[0, i] = shifted(row, left, 1)
        pad_ref[1, i] = row
        pad_ref[2, i] = shifted(row, right, -1)

    for side, i, ref in ((0, 0, top_ref), (1, rows + 1, bottom_ref)):

        @pl.when(inside_ref[side] > 0)
        def _():
            put(i, ref[0:cols, :], ref[cols : cols + 1, :], ref[cols + 8 : cols + 9, :])

        @pl.when(inside_ref[side] == 0)
        def _():
            for b in range(3):
                pad_ref[b, i] = jnp.zeros(pad_ref.shape[2:], BF)

    def fill(i, carry):
        put(i + 1, grid_ref[i], left_ref[i], right_ref[i])
        return carry

    for n in range(blocks):
        loads[n].wait()
        lax.fori_loop(n * high, (n + 1) * high, fill, 0)
    stores = []
    if back:
        stores += [begin(pad_ref.at[b], pad_hbm.at[b], pad_sem.at[b]) for b in range(3)]
    load_w.wait()

    def store(n):
        some = pl.ds(n * high, high)
        return pltpu.make_async_copy(out_ref.at[some], out_hbm.at[some], out_sem.at[n])

    def step(n, carry):
        i = n * high
        acc = grid_ref[pl.ds(i, high)].astype(F32).reshape(high * cols, width)
        for a in range(3):
            for b in range(3):
                part = pad_ref[b, pl.ds(i + a, high)].reshape(high * cols, width)
                tap = a * 3 + b
                acc = acc + (dot(part, w_ref[8 - tap], 1, 1) if back else dot(part, w_ref[tap]))
        out_ref[pl.ds(i, high)] = acc.astype(BF).reshape(high, cols, width)
        store(n).start()
        return carry

    lax.fori_loop(0, blocks, step, 0)
    for n in range(blocks):
        store(n).wait()
    for move in stores:
        move.wait()


def side_edges(grid):
    cols = grid.shape[1]
    count = lax.axis_size("lon")
    up = [(i, (i + 1) % count) for i in range(count)]
    down = [(j, i) for i, j in up]
    left = lax.ppermute(grid[:, cols - 1 :, :], "lon", up)
    right = lax.ppermute(grid[:, :1, :], "lon", down)
    return left, right


def end_rows(grid, left, right):
    pad = ((0, 7), (0, 0))

    def row(i):
        return jnp.concatenate([grid[i], jnp.pad(left[i], pad), jnp.pad(right[i], pad)], axis=0)

    return row(grid.shape[0] - 1), row(0)


def end_edges(last, first):
    count = lax.axis_size("lat")
    up = [(i, (i + 1) % count) for i in range(count)]
    down = [(j, i) for i, j in up]
    return lax.ppermute(last, "lat", up), lax.ppermute(first, "lat", down)


def conv(grid, halo, w, back):
    rows, cols, width = grid.shape
    outs = [shape(grid.shape, BF)]
    pad = (3, rows + 2, cols, width)
    blocks = rows // 8
    scratch = [
        pltpu.VMEM(grid.shape, BF),
        pltpu.VMEM(w.shape, BF),
        pltpu.VMEM(pad, BF),
        pltpu.VMEM(grid.shape, BF),
        DMA((blocks,)),
        DMA,
        DMA((blocks,)),
    ]
    if back:
        outs.append(shape(pad, BF))
        scratch.append(DMA((3,)))
    flops = 18 * rows * cols * width * width
    body = functools.partial(conv_body, back=back)
    at = lax.axis_index("lat")
    inside = jnp.stack([at > 0, at < lax.axis_size("lat") - 1]).astype(I32)
    args = (inside, grid, *halo, w)
    return kernel_call(body, outs, args, flops, scratch, smem=(0,), hbm=(1, 6), far=(0, 1), temp=8)


def gelu_parts(x):
    scale = 0.7978845608028654
    inner = scale * (x + 0.044715 * x * x * x)
    th = jnp.tanh(inner)
    value = 0.5 * x * (1.0 + th)
    slope = 0.5 * (1.0 + th) + 0.5 * x * (1.0 - th * th) * scale * (1.0 + 3 * 0.044715 * x * x)
    return value, slope


def cell_codes(recv_ref, slots):
    owners = recv_ref.shape[0]
    per = 128 // slots
    high, low = [], []
    for p in range(owners // per):
        total = recv_ref[p * per, slots : slots + 8, :].astype(F32)
        for q in range(1, per):
            total = total + recv_ref[p * per + q, slots : slots + 8, :].astype(F32)
        high.append(total[0:1])
        low.append(total[1:2])
    high = jnp.concatenate(high, axis=0)
    low = jnp.concatenate(low, axis=0)
    return (high - 1.0) * 128.0 + low


def gather_body(
    recv_ref, dfield_hbm, w_ref, grad_hbm, eg_hbm, embed_hbm, code_hbm,
    dfield_ref, grad_ref, eg_ref, embed_ref, code_ref, slope_ref, in_sem, grad_sem, out_sem, *, slots,
):
    owners = recv_ref.shape[0]
    cells = dfield_ref.shape[0]
    size = 512
    group = size // slots
    blocks = owners // group
    load = begin(dfield_hbm, dfield_ref, in_sem)
    code_ref[...] = cell_codes(recv_ref, slots)
    stores = [begin(code_ref, code_hbm, out_sem.at[0])]

    def features(blk):
        return jnp.concatenate([recv_ref[blk * group + q, :slots, :] for q in range(group)], axis=0)

    for blk in range(blocks):
        at = slice(blk * size, (blk + 1) * size)
        value, slope = gelu_parts(dot(features(blk), w_ref[...]))
        embed_ref[at, :] = value.astype(BF)
        slope_ref[at, :] = slope
    stores.append(begin(embed_ref, embed_hbm, out_sem.at[1]))
    codes = code_ref[...].T.astype(I32)
    total = jnp.zeros(eg_ref.shape, F32)
    load.wait()
    for blk in range(blocks):
        at = slice(blk * size, (blk + 1) * size)
        code = jnp.concatenate([codes[:, blk * 4 + q : blk * 4 + q + 1] for q in range(4)], axis=0)
        mask = (iota((size, cells), 1) == code).astype(BF)
        rows = dot(mask, dfield_ref[...]).astype(BF)
        grad_ref[at, :] = rows
        stores.append(begin(grad_ref.at[at], grad_hbm.at[at], grad_sem.at[blk]))
        dh = rows.astype(F32) * slope_ref[at, :]
        part = dh.astype(BF)
        rest = (dh - part.astype(F32)).astype(BF)
        feat = features(blk)
        total = total + dot(feat, part, 0, 0) + dot(feat, rest, 0, 0)
    eg_ref[...] = total
    stores.append(begin(eg_ref, eg_hbm, out_sem.at[2]))
    for move in stores:
        move.wait()


def field_body(
    me_ref, code_hbm, embed_hbm, bg_hbm, pad_hbm, eg_hbm, field_hbm, keep_ref, give_ref,
    code_ref, embed_ref, bg_ref, pad_ref, eg_ref, field_ref, acc_ref, sems, pad_sems, out_sems,
):
    loads = [
        begin(code_hbm, code_ref, sems.at[0]),
        begin(embed_hbm, embed_ref, sems.at[1]),
        begin(bg_hbm, bg_ref, sems.at[2]),
        begin(pad_hbm, pad_ref, pad_sems),
        begin(eg_hbm, eg_ref, sems.at[3]),
    ]
    cells, width = bg_ref.shape
    cols = pad_ref.shape[2]
    half = width // 2
    size = 512
    deep = 2 * size
    high = deep // cols
    acc_ref[...] = jnp.zeros_like(acc_ref)
    for move in loads[:3]:
        move.wait()
    codes = code_ref[...].astype(I32)

    def store(n):
        at = pl.ds(pl.multiple_of(n * deep, deep), deep)
        return pltpu.make_async_copy(field_ref.at[at], field_hbm.at[at], out_sems.at[n])

    def scatter(n):
        for k in range(deep // size):
            base = n * deep + k * size
            where = iota((size, 128), 0) + base
            mask = jnp.concatenate(
                [(where == codes[p : p + 1, :]).astype(BF) for p in range(codes.shape[0])], axis=1
            )
            at = pl.ds(pl.multiple_of(base, size), size)
            total = dot(mask, embed_ref[...]) + bg_ref[at, :].astype(F32)
            field_ref[at, :] = total.astype(BF)
        store(n).start()

    def correlate(n):
        field = field_ref[pl.ds(pl.multiple_of(n * deep, deep), deep), :]
        for a in range(3):
            for b in range(3):
                part = pad_ref[2 - b, pl.ds(n * high + 2 - a, high)].reshape(deep, width)
                acc_ref[3 * a + b] += dot(field, part, 0, 0)

    def step(n, carry):
        scatter(n)
        correlate(n)
        return carry

    blocks = cells // deep
    scatter(0)
    loads[3].wait()
    correlate(0)
    lax.fori_loop(1, blocks, step, 0)
    loads[4].wait()
    side = me_ref[0] % 2
    taps = acc_ref.shape[0]
    used = taps * width
    inputs = eg_ref.shape[0]
    for s in range(2):
        lanes = slice(s * half, (s + 1) * half)
        for ref, want in ((keep_ref, s), (give_ref, 1 - s)):

            @pl.when(side == want)
            def _():
                for t in range(taps):
                    ref[t * width : (t + 1) * width, :] = acc_ref[t, :, lanes]
                ref[used : used + inputs, :] = eg_ref[:, lanes]
                if used + inputs < ref.shape[0]:
                    ref[used + inputs :, :] = jnp.zeros((ref.shape[0] - used - inputs, half), F32)

    for n in range(blocks):
        store(n).wait()


def swap(x, bit):
    count = lax.axis_size("lon") * lax.axis_size("lat")
    return lax.ppermute(x, AXES, [(i, i ^ bit) for i in range(count)])


def split_body(mine_ref, *refs, moves, parts):
    n = len(moves)
    ins = refs[: len(refs) - 1 - n]
    keep_ref = refs[len(refs) - 1 - n]
    outs = refs[len(refs) - n :]
    mine = mine_ref[0]

    def put(ref, index):
        row = 0
        for p in range(parts):
            terms = ins[p::parts]
            size = terms[0].shape[0] // (n + 1)
            at = pl.ds(pl.multiple_of(index * size, 8), size)
            total = terms[0][at, :].astype(F32)
            for term in terms[1:]:
                total = total + term[at, :].astype(F32)
            ref[row : row + size, :] = total.astype(ref.dtype)
            row += size

    put(keep_ref, mine)
    for ref, move in zip(outs, moves):
        put(ref, mine ^ move)


def join_body(mine_ref, *refs, parts):
    out_ref = refs[-1]
    ways = len(refs) - 1
    mine = mine_ref[0]
    for move, ref in enumerate(refs[:-1]):
        row, base = 0, 0
        for size in parts:
            at = pl.ds(pl.multiple_of(base + (mine ^ move) * size, 8), size)
            out_ref[at, :] = ref[row : row + size, :]
            row += size
            base += size * ways


def final_body(mine_ref, own_ref, other_ref, conv_ref, embed_ref):
    side = mine_ref[0]
    half = own_ref.shape[1]
    taps, width, _ = conv_ref.shape
    inputs = embed_ref.shape[0]
    for s in range(2):
        lanes = slice(s * half, (s + 1) * half)
        for ref, want in ((own_ref, s), (other_ref, 1 - s)):

            @pl.when(side == want)
            def _():
                for t in range(taps):
                    conv_ref[t, :, lanes] = ref[t * width : (t + 1) * width, :].astype(F32)
                embed_ref[:, lanes] = ref[taps * width : taps * width + inputs, :].astype(F32)


def stages(count):
    bits, found = [], 2
    while found < count:
        bits.append(found)
        found *= 2
    return [bits[i : i + 2] for i in range(0, len(bits), 2)]


def reduce_all(me, keeps, gives, taps, width, inputs, beside, encode, unroute):
    count = lax.axis_size("lon") * lax.axis_size("lat")
    terms = [*keeps, *(swap(x, 1) for x in gives)]
    half = width // 2
    plan = stages(count)
    sizes = []
    for bits in plan:
        ways = 2 ** len(bits)
        parts = len(keeps) if bits is plan[0] else 1
        sizes.append([x.shape[0] // ways for x in terms[:parts]])
        mine = (me // bits[0]) % ways
        moves = list(range(1, ways))
        outs = [shape((sum(sizes[-1]), half), F32)] + [shape((sum(sizes[-1]), half), BF)] * len(moves)
        body = functools.partial(split_body, moves=moves, parts=parts)
        own, *send = kernel_call(body, outs, (mine, *terms), smem=(0,))
        if bits is plan[0]:
            send, back = lax.optimization_barrier((send, beside[0]))
            found = encode(beside[1])
        terms = [own] + [swap(x, m * bits[0]) for m, x in zip(moves, send)]
        if bits is plan[0]:
            terms, found = lax.optimization_barrier((terms, found))
    body = functools.partial(split_body, moves=[], parts=1)
    (block,) = kernel_call(
        body, [shape(terms[0].shape, BF)], (jnp.zeros((1,), I32), *terms), smem=(0,)
    )
    for bits, parts in zip(reversed(plan), reversed(sizes)):
        ways = 2 ** len(bits)
        mine = (me // bits[0]) % ways
        pieces = [block] + [swap(block, m * bits[0]) for m in range(1, ways)]
        if bits is plan[0]:
            pieces, gone = lax.optimization_barrier((pieces, unroute(back)))
        rows = block.shape[0]
        body = functools.partial(join_body, parts=parts)
        (block,) = kernel_call(body, [shape((rows * ways, half), BF)], (mine, *pieces), smem=(0,))
    other = swap(block, 1)
    outs = [shape((taps, width, width), F32), shape((inputs, width), F32)]
    return kernel_call(final_body, outs, (me % 2, block, other), smem=(0,)), found, gone


def on_device(obs_feat, obs_tile, obs_cell, w_embed, background, w_conv, cotangent):
    lon_count = lax.axis_size("lon")
    lat_count = lax.axis_size("lat")
    owners = lon_count * lat_count
    records, inputs = obs_feat.shape
    slots = 2 * records // owners
    rows, cols, width = background.shape
    cells = rows * cols
    taps = w_conv.shape[0]
    me = (lax.axis_index("lon") * lat_count + lax.axis_index("lat")).astype(I32).reshape(1)

    outs = [shape((owners, slots + 8, inputs), BF), shape((1, records), I32)]
    send, place = kernel_call(
        functools.partial(route_body, owners=owners, slots=slots),
        outs,
        (me, obs_tile.reshape(1, records), obs_cell.reshape(1, records), obs_feat),
        flops=4 * records * records * inputs,
        scratch=[
            pltpu.VMEM((512, records), BF),
            pltpu.VMEM((1, records), I32),
            pltpu.VMEM((1, records), I32),
            pltpu.VMEM((records, inputs), BF),
            DMA((3,)),
        ],
        smem=(0,),
        hbm=(1, 2, 3),
        temp=4,
    )
    sides = side_edges(cotangent)
    send, sides = lax.optimization_barrier((send, sides))
    ends = end_rows(cotangent, *sides)
    send, ends = lax.optimization_barrier((send, ends))
    halo = (*sides, *end_edges(*ends))
    recv = lax.all_to_all(send, AXES, split_axis=0, concat_axis=0, tiled=True)

    dfield, pad = conv(cotangent, halo, w_conv, True)

    count = owners * slots
    grad, local_eg, embed, codes = kernel_call(
        functools.partial(gather_body, slots=slots),
        [
            shape((count, width), BF),
            shape((inputs, width), F32),
            shape((count, width), BF),
            shape((count // 128, 128), F32),
        ],
        (recv, dfield.reshape(cells, width), w_embed),
        flops=2 * count * cells * width,
        scratch=[
            pltpu.VMEM((cells, width), BF),
            pltpu.VMEM((count, width), BF),
            pltpu.VMEM((inputs, width), F32),
            pltpu.VMEM((count, width), BF),
            pltpu.VMEM((count // 128, 128), F32),
            pltpu.VMEM((count, width), F32),
            DMA,
            DMA((count // 512,)),
            DMA((3,)),
        ],
        hbm=(1,),
        far=(0, 1, 2, 3),
        temp=12,
    )
    blocks = owners // 2
    size = 8 * blocks
    total = -(-(taps * width + inputs) // size) * size
    back = lax.all_to_all(grad.reshape(owners, slots, width), AXES, split_axis=0, concat_axis=0, tiled=True)
    field, keep, give = kernel_call(
        field_body,
        [shape((cells, width), BF)] + [shape((total, width // 2), F32)] * 2,
        (me, codes, embed, background.reshape(cells, width), pad, local_eg),
        flops=2 * count * cells * width + 18 * cells * width * width,
        scratch=[
            pltpu.VMEM((count // 128, 128), F32),
            pltpu.VMEM((count, width), BF),
            pltpu.VMEM((cells, width), BF),
            pltpu.VMEM(pad.shape, BF),
            pltpu.VMEM((inputs, width), F32),
            pltpu.VMEM((cells, width), BF),
            pltpu.VMEM((taps, width, width), F32),
            DMA((4,)),
            DMA,
            DMA((cells // 1024,)),
        ],
        smem=(0,),
        hbm=(1, 2, 3, 4, 5),
        far=(0,),
        temp=8,
    )
    grid = field.reshape(rows, cols, width)
    sides = side_edges(grid)
    halo = (*sides, *end_edges(*end_rows(grid, *sides)))

    def encode(halo):
        return conv(grid, halo, w_conv, False)[0]

    def unroute(back):
        return kernel_call(
            unroute_body,
            [shape((records, width), BF)],
            (place.reshape(records, 1), back.reshape(count, width)),
            flops=2 * count * records * width,
            temp=4,
        )[0]

    (conv_grad, embed_grad), encoded, record_grad = reduce_all(
        me, (keep,), (give,), taps, width, inputs, (back, halo), encode, unroute
    )
    return encoded, record_grad, conv_grad, embed_grad


def solution(mesh):
    placed = (
        P(("lon", "lat"), None),
        P(("lon", "lat"), None),
        P(("lon", "lat")),
        P(),
        P("lat", "lon", None),
        P(),
        P("lat", "lon", None),
    )
    return jax.shard_map(
        on_device,
        mesh=mesh,
        in_specs=placed,
        out_specs=(P("lat", "lon", None), P(("lon", "lat"), None), P(), P()),
        check_vma=False,
    )
```

time: 162 us -> 118 us (0.73)
  Pallas kernels: 70.4 us -> 50.1 us
  waiting for transfers between devices: 32.5 us -> 22.6 us
  local copies, waits for them, and re-layouts: 13 us -> 4.05 us
  starting transfers between devices: 44.6 us -> 40 us
    pallas_call x12, Pallas kernels: 70.4 us -> 50.1 us  [kernel_call(): pl.pallas_call(body, out_shape=[pltpu.HBM(o.shape, o.dtype) if i in far e...]
    unnamed x50 -> x2, local copies, waits for them, and re-layouts: 8.14 us -> 0.01 us
    ppermute x14, waiting for transfers between devices: 19.8 us -> 12.9 us  [swap(): return lax.ppermute(x, AXES, [(i, i ^ bit) for i in range(count)])]
    ppermute x8, waiting for transfers between devices: 12.7 us -> 7.15 us  [the longest x4 5.52 us: end_edges(): return (lax.ppermute(last, 'lat', up), lax.ppermute(first, 'lat', down))]
    all_to_all x1, starting transfers between devices: 7.3 us -> 3.77 us  [on_device(): recv = lax.all_to_all(send, AXES, split_axis=0, concat_axis=0, tiled=True)]
    all_to_all x1, starting transfers between devices: 3.13 us -> 6.21 us  [on_device(): lax.all_to_all(grad.reshape(owners, slots, width), AXES, split_axis=0, co...]
    ppermute x14, starting transfers between devices: 19.5 us -> 16.7 us  [swap(): return lax.ppermute(x, AXES, [(i, i ^ bit) for i in range(count)])]
    all_to_all x1, waiting for transfers between devices: 0.01 us -> 2.51 us  [on_device(): lax.all_to_all(grad.reshape(owners, slots, width), AXES, split_axis=0, co...]
  transfers between devices with their start and end apart: 24 -> 24, of which waited for: 12 -> 12; matrix products, arithmetic and copies ran while one was open for 3% -> 3% of each run, Pallas kernels for 21% -> 33%
where the time goes in v2:
time: 118 us
  Pallas kernels  50.1 us (42%)
  starting transfers between devices  40 us (34%)
  waiting for transfers between devices  22.6 us (19%)
  local copies, waits for them, and re-layouts  4.05 us (3%)
    pallas_call x12, Pallas kernels, kernel_call(): pl.pallas_call(body, out_shape=[pltpu.HBM(o.shape, o.dtype) if i in far e...  50.1 us
    ppermute x14, starting transfers between devices, swap(): return lax.ppermute(x, AXES, [(i, i ^ bit) for i in range(count)])  16.7 us
    ppermute x14, waiting for transfers between devices, swap(): return lax.ppermute(x, AXES, [(i, i ^ bit) for i in range(count)])  12.9 us
    ppermute x2, starting transfers between devices, side_edges(): right = lax.ppermute(grid[:, :1, :], 'lon', down)  6.21 us
    all_to_all x1, starting transfers between devices, on_device(): lax.all_to_all(grad.reshape(owners, slots, width), AXES, split_axis=0, co...  6.21 us
    ppermute x4, waiting for transfers between devices, end_edges(): return (lax.ppermute(last, 'lat', up), lax.ppermute(first, 'lat', down))  5.52 us
    ppermute x2, starting transfers between devices, side_edges(): left = lax.ppermute(grid[:, cols - 1:, :], 'lon', up)  4.71 us
    all_to_all x1, starting transfers between devices, on_device(): recv = lax.all_to_all(send, AXES, split_axis=0, concat_axis=0, tiled=True)  3.77 us
  transfers between devices with their start and end apart: 24, of which 12 were waited for; matrix products, arithmetic and copies ran while one was open for 3% of the time, Pallas kernels for 33%

profile of v2, /device:TPU:0, one launch (start us, length us, event | category | flops | bytes accessed | tf_op | source)
XLA Modules:
  0.0 117.7 jit_solution(8615038946921532295)
XLA Ops:
  1.7 3.0 %collective-permute-start = (bf16[32,1,256]{2,1,0:T(2,128)(2,1)S(1)}, bf16[32,1,256]{2,1,0:T(2,128)(2,1)S(1)}, u32[]{:S(2)}, u32[]{:S(2)}) collective-permute-start(bf16[32,1,256]{2,1,0:T(2,128)(2,1)S(1)} %get-tuple-element.93), channel_id=1, source_target_pairs={{0,4},{4,8},{8,12},{12,16},{16,20},{20,24},{24,28},{28,0},{1,5},{5... | collective-permute-start | bytes 49160 | tf_op jit(solution)/shard_map/ppermute | solution.py:197
  4.7 3.1 %collective-permute-start.1 = (bf16[32,1,256]{2,1,0:T(2,128)(2,1)S(1)}, bf16[32,1,256]{2,1,0:T(2,128)(2,1)S(1)}, u32[]{:S(2)}, u32[]{:S(2)}) collective-permute-start(bf16[32,1,256]{2,1,0:T(2,128)(2,1)S(1)} %get-tuple-element.92), channel_id=1, source_target_pairs={{4,0},{8,4},{12,8},{16,12},{20,16},{24,20},{28,24},{0,28},{5,1},{9... | collective-permute-start | bytes 49160 | tf_op jit(solution)/shard_map/ppermute | solution.py:198
  8.6 3.4 %shard_map.102 = (bf16[32,72,128]{2,1,0:T(8,128)(2,1)}, s32[1,1024]{1,0:T(1,128)S(1)}) custom-call(s32[1]{0:T(128)} %bitcast.me_ref, s32[1,1024]{1,0:T(1,128)} %bitcast.37, s32[1,1024]{1,0:T(1,128)} %bitcast.38, bf16[1024,128]{1,0:T(8,128)(2,1)} %feat_hbm.1), custom_call_target="tpu_custom_call" | custom-call | flops 536870912 | bytes 864260 | tf_op jit(solution)/shard_map/pallas_call | solution.py:35
  12.1 3.8 %all-to-all-start = ((bf16[32,72,128]{2,1,0:T(8,128)(2,1)}), bf16[32,72,128]{2,1,0:T(8,128)(2,1)S(1)}, u32[]{:S(2)}, u32[]{:S(2)}) async-start(bf16[32,72,128]{2,1,0:T(8,128)(2,1)} %get-tuple-element.49), calls=%async_computation | async-start | bytes 1179648 | tf_op jit(solution)/shard_map/all_to_all | solution.py:524
  17.7 3.9 %collective-permute-done.2.top_ref = bf16[144,256]{1,0:T(8,128)(2,1)S(1)} collective-permute-done((bf16[144,256]{1,0:T(8,128)(2,1)S(1)}, bf16[144,256]{1,0:T(8,128)(2,1)S(1)}, u32[]{:S(2)}, u32[]{:S(2)}) %collective-permute-start.2) | collective-permute-done | bytes 73760 | tf_op jit(solution)/shard_map/ppermute | solution.py:215
  23.3 9.2 %shard_map.103 = (bf16[32,128,256]{2,1,0:T(8,128)(2,1)}, bf16[3,34,128,256]{3,2,1,0:T(8,128)(2,1)}) custom-call(s32[2]{0:T(128)S(1)} %add_convert_fusion.inside_ref, bf16[32,128,256]{2,1,0:T(8,128)(2,1)} %grid_hbm.1, bf16[32,1,256]{2,1,0:T(2,128)(2,1)S(1)} %collective-permute-done.left_ref, bf16[32,1,256]{2,1,0:T(2,128)(2,1)S(1)} %collective-permute-done.1.right_ref, ...), custom_call_target="tpu_custom_call" | custom-call | flops 4831838208 | bytes 12238856 | tf_op jit(solution)/shard_map/pallas_call | solution.py:35
  32.6 9.8 %shard_map.104 = (bf16[2048,256]{1,0:T(8,128)(2,1)}, f32[128,256]{1,0:T(8,128)}, bf16[2048,256]{1,0:T(8,128)(2,1)}, f32[16,128]{1,0:T(8,128)}) custom-call(bf16[32,72,128]{2,1,0:T(8,128)(2,1)S(1)} %all-to-all-done.recv_ref, bf16[4096,256]{1,0:T(8,128)(2,1)} %bitcast.39, bf16[128,256]{1,0:T(8,128)(2,1)S(1)} %copy-done), custom_call_target="tpu_custom_call" | custom-call | flops 4294967296 | bytes 4988928 | tf_op jit(solution)/shard_map/pallas_call | solution.py:35
  42.4 6.2 %all-to-all-start.1 = ((bf16[32,64,256]{2,1,0:T(8,128)(2,1)}), bf16[32,64,256]{2,1,0:T(8,128)(2,1)S(1)}, u32[]{:S(2)}, u32[]{:S(2)}) async-start(bf16[32,64,256]{2,1,0:T(8,128)(2,1)} %bitcast.33), calls=%async_computation.1 | async-start | bytes 2097152 | tf_op jit(solution)/shard_map/all_to_all | solution.py:557
  48.6 14.5 %shard_map.105 = (bf16[4096,256]{1,0:T(8,128)(2,1)}, f32[2432,128]{1,0:T(8,128)S(1)}, f32[2432,128]{1,0:T(8,128)S(1)}) custom-call(s32[1]{0:T(128)} %bitcast.me_ref, f32[16,128]{1,0:T(8,128)} %get-tuple-element.53.code_hbm, bf16[2048,256]{1,0:T(8,128)(2,1)} %get-tuple-element.54.embed_hbm, bf16[4096,256]{1,0:T(8,128)(2,1)} %bitcast.36, ...), custom_call_target="tpu_custom_call" | custom-call | flops 9126805504 | bytes 14557188 | tf_op jit(solution)/shard_map/pallas_call | solution.py:35
  64.3 1.7 %collective-permute-start.8 = (bf16[32,1,256]{2,1,0:T(2,128)(2,1)S(1)}, bf16[32,1,256]{2,1,0:T(2,128)(2,1)S(1)}, u32[]{:S(2)}, u32[]{:S(2)}) collective-permute-start(bf16[32,1,256]{2,1,0:T(2,128)(2,1)S(1)} %get-tuple-element.89), channel_id=1, source_target_pairs={{0,4},{4,8},{8,12},{12,16},{16,20},{20,24},{24,28},{28,0},{1,5},{5... | collective-permute-start | bytes 49160 | tf_op jit(solution)/shard_map/ppermute | solution.py:197
  66.9 3.1 %collective-permute-start.9 = (bf16[32,1,256]{2,1,0:T(2,128)(2,1)S(1)}, bf16[32,1,256]{2,1,0:T(2,128)(2,1)S(1)}, u32[]{:S(2)}, u32[]{:S(2)}) collective-permute-start(bf16[32,1,256]{2,1,0:T(2,128)(2,1)S(1)} %get-tuple-element.88), channel_id=1, source_target_pairs={{4,0},{8,4},{12,8},{16,12},{20,16},{24,20},{28,24},{0,28},{5,1},{9... | collective-permute-start | bytes 49160 | tf_op jit(solution)/shard_map/ppermute | solution.py:198
  70.0 1.6 %collective-permute-done.8.left_ref = bf16[32,1,256]{2,1,0:T(2,128)(2,1)S(1)} collective-permute-done((bf16[32,1,256]{2,1,0:T(2,128)(2,1)S(1)}, bf16[32,1,256]{2,1,0:T(2,128)(2,1)S(1)}, u32[]{:S(2)}, u32[]{:S(2)}) %collective-permute-start.8) | collective-permute-done | bytes 16416 | tf_op jit(solution)/shard_map/ppermute | solution.py:197
  72.5 2.5 %all-to-all-done.1 = bf16[32,64,256]{2,1,0:T(8,128)(2,1)S(1)} async-done(((bf16[32,64,256]{2,1,0:T(8,128)(2,1)}), bf16[32,64,256]{2,1,0:T(8,128)(2,1)S(1)}, u32[]{:S(2)}, u32[]{:S(2)}) %all-to-all-start.1) | async-done | bytes 1048608 | tf_op jit(solution)/shard_map/all_to_all | solution.py:557
  76.5 1.8 %collective-permute-start.6 = (bf16[608,128]{1,0:T(8,128)(2,1)S(1)}, bf16[608,128]{1,0:T(8,128)(2,1)S(1)}, u32[]{:S(2)}, u32[]{:S(2)}) collective-permute-start(bf16[608,128]{1,0:T(8,128)(2,1)S(1)} %get-tuple-element.65), channel_id=1, source_target_pairs={{0,4},{1,5},{2,6},{3,7},{4,0},{5,1},{6,2},{7,3},{8,12},{9,13},{10,... | collective-permute-start | bytes 466952 | tf_op jit(solution)/shard_map/ppermute | solution.py:388
  78.5 9.1 %shard_map.107 = bf16[32,128,256]{2,1,0:T(8,128)(2,1)} custom-call(s32[2]{0:T(128)S(1)} %add_convert_fusion.inside_ref, bf16[32,128,256]{2,1,0:T(8,128)(2,1)} %bitcast.35, bf16[32,1,256]{2,1,0:T(2,128)(2,1)S(1)} %collective-permute-done.8.left_ref, bf16[32,1,256]{2,1,0:T(2,128)(2,1)S(1)} %collective-permute-done.9.right_ref, ...), custom_call_target="tpu_custom_call" | custom-call | flops 4831838208 | bytes 5554184 | tf_op jit(solution)/shard_map/pallas_call | solution.py:35
  89.1 2.2 %collective-permute-start.13 = (bf16[152,128]{1,0:T(8,128)(2,1)S(1)}, bf16[152,128]{1,0:T(8,128)(2,1)S(1)}, u32[]{:S(2)}, u32[]{:S(2)}) collective-permute-start(bf16[152,128]{1,0:T(8,128)(2,1)S(1)} %get-tuple-element.75), channel_id=1, source_target_pairs={{0,16},{1,17},{2,18},{3,19},{4,20},{5,21},{6,22},{7,23},{8,24},{9,... | collective-permute-start | bytes 116744 | tf_op jit(solution)/shard_map/ppermute | solution.py:388
  94.3 2.8 %collective-permute-done.14.refs_3_ = bf16[152,128]{1,0:T(8,128)(2,1)S(1)} collective-permute-done((bf16[152,128]{1,0:T(8,128)(2,1)S(1)}, bf16[152,128]{1,0:T(8,128)(2,1)S(1)}, u32[]{:S(2)}, u32[]{:S(2)}) %collective-permute-start.14) | collective-permute-done | bytes 38944 | tf_op jit(solution)/shard_map/ppermute | solution.py:388
  97.4 1.9 %collective-permute-start.16 = (bf16[152,128]{1,0:T(8,128)(2,1)S(1)}, bf16[152,128]{1,0:T(8,128)(2,1)S(1)}, u32[]{:S(2)}, u32[]{:S(2)}) collective-permute-start(bf16[152,128]{1,0:T(8,128)(2,1)S(1)} %shard_map.109.refs_0_), channel_id=1, source_target_pairs={{0,16},{1,17},{2,18},{3,19},{4,20},{5,21},{6,22},{7,23},{8,24},{9,... | collective-permute-start | bytes 116744 | tf_op jit(solution)/shard_map/ppermute | solution.py:388
  99.3 2.3 %collective-permute-start.17 = (bf16[152,128]{1,0:T(8,128)(2,1)S(1)}, bf16[152,128]{1,0:T(8,128)(2,1)S(1)}, u32[]{:S(2)}, u32[]{:S(2)}) collective-permute-start(bf16[152,128]{1,0:T(8,128)(2,1)S(1)} %shard_map.109.refs_0_), channel_id=1, source_target_pairs={{0,24},{1,25},{2,26},{3,27},{4,28},{5,29},{6,30},{7,31},{8,16},{9,... | collective-permute-start | bytes 116744 | tf_op jit(solution)/shard_map/ppermute | solution.py:388
  102.6 2.4 %collective-permute-done.17.refs_3_ = bf16[152,128]{1,0:T(8,128)(2,1)S(1)} collective-permute-done((bf16[152,128]{1,0:T(8,128)(2,1)S(1)}, bf16[152,128]{1,0:T(8,128)(2,1)S(1)}, u32[]{:S(2)}, u32[]{:S(2)}) %collective-permute-start.17) | collective-permute-done | bytes 38944 | tf_op jit(solution)/shard_map/ppermute | solution.py:388
  108.9 2.1 %shard_map.111 = bf16[1024,256]{1,0:T(8,128)(2,1)} custom-call(s32[1024,1]{1,0:T(8,128)S(1)} %copy.11.place_ref, bf16[2048,256]{1,0:T(8,128)(2,1)S(1)} %bitcast.31), custom_call_target="tpu_custom_call" | custom-call | flops 1073741824 | bytes 1576960 | tf_op jit(solution)/shard_map/pallas_call | solution.py:35
  111.7 2.3 %collective-permute-done.20.refs_3_ = bf16[608,128]{1,0:T(8,128)(2,1)S(1)} collective-permute-done((bf16[608,128]{1,0:T(8,128)(2,1)S(1)}, bf16[608,128]{1,0:T(8,128)(2,1)S(1)}, u32[]{:S(2)}, u32[]{:S(2)}) %collective-permute-start.20) | collective-permute-done | bytes 155680 | tf_op jit(solution)/shard_map/ppermute | solution.py:388
  114.1 2.0 %collective-permute-done.21.other_ref = bf16[2432,128]{1,0:T(8,128)(2,1)S(1)} collective-permute-done((bf16[2432,128]{1,0:T(8,128)(2,1)S(1)}, bf16[2432,128]{1,0:T(8,128)(2,1)S(1)}, u32[]{:S(2)}, u32[]{:S(2)}) %collective-permute-start.21) | collective-permute-done | bytes 622624 | tf_op jit(solution)/shard_map/ppermute | solution.py:388
  116.1 1.6 %shard_map.113 = (f32[9,256,256]{2,1,0:T(8,128)}, f32[128,256]{1,0:T(8,128)}) custom-call(s32[1]{0:T(128)S(6)} %select_n.33.mine_ref, bf16[2432,128]{1,0:T(8,128)(2,1)S(1)} %shard_map.112.own_ref, bf16[2432,128]{1,0:T(8,128)(2,1)S(1)} %collective-permute-done.21.other_ref), custom_call_target="tpu_custom_call" | custom-call | bytes 3735556 | tf_op jit(solution)/shard_map/pallas_call | solution.py:35
  (51 shorter events, 20.4 us)
Async XLA Ops:
  1.7 10.4 %collective-permute-start = (bf16[32,1,256]{2,1,0:T(2,128)(2,1)S(1)}, bf16[32,1,256]{2,1,0:T(2,128)(2,1)S(1)}, u32[]{:S(2)}, u32[]{:S(2)}) collective-permute-start(bf16[32,1,256]{2,1,0:T(2,128)(2,1)S(1)} %get-tuple-element.93), channel_id=1, source_target_pairs={{0,4},{4,8},{8,12},{12,16},{16,20},{20,24},{24,28},{28,0},{1,5},{5... | collective-permute-start | bytes 49160 | tf_op jit(solution)/shard_map/ppermute | solution.py:197
  4.7 7.4 %collective-permute-start.1 = (bf16[32,1,256]{2,1,0:T(2,128)(2,1)S(1)}, bf16[32,1,256]{2,1,0:T(2,128)(2,1)S(1)}, u32[]{:S(2)}, u32[]{:S(2)}) collective-permute-start(bf16[32,1,256]{2,1,0:T(2,128)(2,1)S(1)} %get-tuple-element.92), channel_id=1, source_target_pairs={{4,0},{8,4},{12,8},{16,12},{20,16},{24,20},{28,24},{0,28},{5,1},{9... | collective-permute-start | bytes 49160 | tf_op jit(solution)/shard_map/ppermute | solution.py:198
  12.1 20.5 %all-to-all-start = ((bf16[32,72,128]{2,1,0:T(8,128)(2,1)}), bf16[32,72,128]{2,1,0:T(8,128)(2,1)S(1)}, u32[]{:S(2)}, u32[]{:S(2)}) async-start(bf16[32,72,128]{2,1,0:T(8,128)(2,1)} %get-tuple-element.49), calls=%async_computation | async-start | bytes 1179648 | tf_op jit(solution)/shard_map/all_to_all | solution.py:524
  15.9 5.8 %collective-permute-start.2 = (bf16[144,256]{1,0:T(8,128)(2,1)S(1)}, bf16[144,256]{1,0:T(8,128)(2,1)S(1)}, u32[]{:S(2)}, u32[]{:S(2)}) collective-permute-start(bf16[144,256]{1,0:T(8,128)(2,1)S(1)} %fusion.5), channel_id=1, source_target_pairs={{0,1},{1,2},{2,3},{3,0},{4,5},{5,6},{6,7},{7,4},{8,9},{9,10},{10,1... | collective-permute-start | bytes 221192 | tf_op jit(solution)/shard_map/ppermute | solution.py:215
  16.2 7.1 %collective-permute-start.3 = (bf16[144,256]{1,0:T(8,128)(2,1)S(1)}, bf16[144,256]{1,0:T(8,128)(2,1)S(1)}, u32[]{:S(2)}, u32[]{:S(2)}) collective-permute-start(bf16[144,256]{1,0:T(8,128)(2,1)S(1)} %fusion.6), channel_id=1, source_target_pairs={{1,0},{2,1},{3,2},{0,3},{5,4},{6,5},{7,6},{4,7},{9,8},{10,9},{11,1... | collective-permute-start | bytes 221192 | tf_op jit(solution)/shard_map/ppermute | solution.py:215
  42.4 32.6 %all-to-all-start.1 = ((bf16[32,64,256]{2,1,0:T(8,128)(2,1)}), bf16[32,64,256]{2,1,0:T(8,128)(2,1)S(1)}, u32[]{:S(2)}, u32[]{:S(2)}) async-start(bf16[32,64,256]{2,1,0:T(8,128)(2,1)} %bitcast.33), calls=%async_computation.1 | async-start | bytes 2097152 | tf_op jit(solution)/shard_map/all_to_all | solution.py:557
  63.1 9.2 %collective-permute-start.4 = (f32[2432,128]{1,0:T(8,128)S(1)}, f32[2432,128]{1,0:T(8,128)S(1)}, u32[]{:S(2)}, u32[]{:S(2)}) collective-permute-start(f32[2432,128]{1,0:T(8,128)S(1)} %get-tuple-element.58), channel_id=1, source_target_pairs={{0,1},{1,0},{2,3},{3,2},{4,5},{5,4},{6,7},{7,6},{8,9},{9,8},{10,11... | collective-permute-start | bytes 3735560 | tf_op jit(solution)/shard_map/ppermute | solution.py:388
  64.3 7.3 %collective-permute-start.8 = (bf16[32,1,256]{2,1,0:T(2,128)(2,1)S(1)}, bf16[32,1,256]{2,1,0:T(2,128)(2,1)S(1)}, u32[]{:S(2)}, u32[]{:S(2)}) collective-permute-start(bf16[32,1,256]{2,1,0:T(2,128)(2,1)S(1)} %get-tuple-element.89), channel_id=1, source_target_pairs={{0,4},{4,8},{8,12},{12,16},{16,20},{20,24},{24,28},{28,0},{1,5},{5... | collective-permute-start | bytes 49160 | tf_op jit(solution)/shard_map/ppermute | solution.py:197
  66.9 4.7 %collective-permute-start.9 = (bf16[32,1,256]{2,1,0:T(2,128)(2,1)S(1)}, bf16[32,1,256]{2,1,0:T(2,128)(2,1)S(1)}, u32[]{:S(2)}, u32[]{:S(2)}) collective-permute-start(bf16[32,1,256]{2,1,0:T(2,128)(2,1)S(1)} %get-tuple-element.88), channel_id=1, source_target_pairs={{4,0},{8,4},{12,8},{16,12},{20,16},{24,20},{28,24},{0,28},{5,1},{9... | collective-permute-start | bytes 49160 | tf_op jit(solution)/shard_map/ppermute | solution.py:198
  71.7 6.9 %collective-permute-start.11 = (bf16[144,256]{1,0:T(8,128)(2,1)S(1)}, bf16[144,256]{1,0:T(8,128)(2,1)S(1)}, u32[]{:S(2)}, u32[]{:S(2)}) collective-permute-start(bf16[144,256]{1,0:T(8,128)(2,1)S(1)} %fusion.8), channel_id=1, source_target_pairs={{1,0},{2,1},{3,2},{0,3},{5,4},{6,5},{7,6},{4,7},{9,8},{10,9},{11,1... | collective-permute-start | bytes 221192 | tf_op jit(solution)/shard_map/ppermute | solution.py:215
  72.2 6.3 %collective-permute-start.10 = (bf16[144,256]{1,0:T(8,128)(2,1)S(1)}, bf16[144,256]{1,0:T(8,128)(2,1)S(1)}, u32[]{:S(2)}, u32[]{:S(2)}) collective-permute-start(bf16[144,256]{1,0:T(8,128)(2,1)S(1)} %fusion.7), channel_id=1, source_target_pairs={{0,1},{1,2},{2,3},{3,0},{4,5},{5,6},{6,7},{7,4},{8,9},{9,10},{10,1... | collective-permute-start | bytes 221192 | tf_op jit(solution)/shard_map/ppermute | solution.py:215
  75.0 12.6 %collective-permute-start.5 = (bf16[608,128]{1,0:T(8,128)(2,1)S(1)}, bf16[608,128]{1,0:T(8,128)(2,1)S(1)}, u32[]{:S(2)}, u32[]{:S(2)}) collective-permute-start(bf16[608,128]{1,0:T(8,128)(2,1)S(1)} %get-tuple-element.64), channel_id=1, source_target_pairs={{0,2},{1,3},{2,0},{3,1},{4,6},{5,7},{6,4},{7,5},{8,10},{9,11},{10,... | collective-permute-start | bytes 466952 | tf_op jit(solution)/shard_map/ppermute | solution.py:388
  76.5 11.1 %collective-permute-start.6 = (bf16[608,128]{1,0:T(8,128)(2,1)S(1)}, bf16[608,128]{1,0:T(8,128)(2,1)S(1)}, u32[]{:S(2)}, u32[]{:S(2)}) collective-permute-start(bf16[608,128]{1,0:T(8,128)(2,1)S(1)} %get-tuple-element.65), channel_id=1, source_target_pairs={{0,4},{1,5},{2,6},{3,7},{4,0},{5,1},{6,2},{7,3},{8,12},{9,13},{10,... | collective-permute-start | bytes 466952 | tf_op jit(solution)/shard_map/ppermute | solution.py:388
  78.3 9.3 %collective-permute-start.7 = (bf16[608,128]{1,0:T(8,128)(2,1)S(1)}, bf16[608,128]{1,0:T(8,128)(2,1)S(1)}, u32[]{:S(2)}, u32[]{:S(2)}) collective-permute-start(bf16[608,128]{1,0:T(8,128)(2,1)S(1)} %get-tuple-element.66), channel_id=1, source_target_pairs={{0,6},{1,7},{2,4},{3,5},{4,2},{5,3},{6,0},{7,1},{8,14},{9,15},{10,... | collective-permute-start | bytes 466952 | tf_op jit(solution)/shard_map/ppermute | solution.py:388
  87.8 5.0 %collective-permute-start.12 = (bf16[152,128]{1,0:T(8,128)(2,1)S(1)}, bf16[152,128]{1,0:T(8,128)(2,1)S(1)}, u32[]{:S(2)}, u32[]{:S(2)}) collective-permute-start(bf16[152,128]{1,0:T(8,128)(2,1)S(1)} %get-tuple-element.74), channel_id=1, source_target_pairs={{0,8},{1,9},{2,10},{3,11},{4,12},{5,13},{6,14},{7,15},{8,0},{9,1},... | collective-permute-start | bytes 116744 | tf_op jit(solution)/shard_map/ppermute | solution.py:388
  89.1 5.2 %collective-permute-start.13 = (bf16[152,128]{1,0:T(8,128)(2,1)S(1)}, bf16[152,128]{1,0:T(8,128)(2,1)S(1)}, u32[]{:S(2)}, u32[]{:S(2)}) collective-permute-start(bf16[152,128]{1,0:T(8,128)(2,1)S(1)} %get-tuple-element.75), channel_id=1, source_target_pairs={{0,16},{1,17},{2,18},{3,19},{4,20},{5,21},{6,22},{7,23},{8,24},{9,... | collective-permute-start | bytes 116744 | tf_op jit(solution)/shard_map/ppermute | solution.py:388
  91.3 5.8 %collective-permute-start.14 = (bf16[152,128]{1,0:T(8,128)(2,1)S(1)}, bf16[152,128]{1,0:T(8,128)(2,1)S(1)}, u32[]{:S(2)}, u32[]{:S(2)}) collective-permute-start(bf16[152,128]{1,0:T(8,128)(2,1)S(1)} %get-tuple-element.76), channel_id=1, source_target_pairs={{0,24},{1,25},{2,26},{3,27},{4,28},{5,29},{6,30},{7,31},{8,16},{9,... | collective-permute-start | bytes 116744 | tf_op jit(solution)/shard_map/ppermute | solution.py:388
  97.2 4.5 %collective-permute-start.15 = (bf16[152,128]{1,0:T(8,128)(2,1)S(1)}, bf16[152,128]{1,0:T(8,128)(2,1)S(1)}, u32[]{:S(2)}, u32[]{:S(2)}) collective-permute-start(bf16[152,128]{1,0:T(8,128)(2,1)S(1)} %shard_map.109.refs_0_), channel_id=1, source_target_pairs={{0,8},{1,9},{2,10},{3,11},{4,12},{5,13},{6,14},{7,15},{8,0},{9,1},... | collective-permute-start | bytes 116744 | tf_op jit(solution)/shard_map/ppermute | solution.py:388
  97.4 5.3 %collective-permute-start.16 = (bf16[152,128]{1,0:T(8,128)(2,1)S(1)}, bf16[152,128]{1,0:T(8,128)(2,1)S(1)}, u32[]{:S(2)}, u32[]{:S(2)}) collective-permute-start(bf16[152,128]{1,0:T(8,128)(2,1)S(1)} %shard_map.109.refs_0_), channel_id=1, source_target_pairs={{0,16},{1,17},{2,18},{3,19},{4,20},{5,21},{6,22},{7,23},{8,24},{9,... | collective-permute-start | bytes 116744 | tf_op jit(solution)/shard_map/ppermute | solution.py:388
  99.3 5.8 %collective-permute-start.17 = (bf16[152,128]{1,0:T(8,128)(2,1)S(1)}, bf16[152,128]{1,0:T(8,128)(2,1)S(1)}, u32[]{:S(2)}, u32[]{:S(2)}) collective-permute-start(bf16[152,128]{1,0:T(8,128)(2,1)S(1)} %shard_map.109.refs_0_), channel_id=1, source_target_pairs={{0,24},{1,25},{2,26},{3,27},{4,28},{5,29},{6,30},{7,31},{8,16},{9,... | collective-permute-start | bytes 116744 | tf_op jit(solution)/shard_map/ppermute | solution.py:388
  105.1 5.9 %collective-permute-start.18 = (bf16[608,128]{1,0:T(8,128)(2,1)S(1)}, bf16[608,128]{1,0:T(8,128)(2,1)S(1)}, u32[]{:S(2)}, u32[]{:S(2)}) collective-permute-start(bf16[608,128]{1,0:T(8,128)(2,1)S(1)} %shard_map.110.refs_0_), channel_id=1, source_target_pairs={{0,2},{1,3},{2,0},{3,1},{4,6},{5,7},{6,4},{7,5},{8,10},{9,11},{10,... | collective-permute-start | bytes 466952 | tf_op jit(solution)/shard_map/ppermute | solution.py:388
  106.4 5.2 %collective-permute-start.19 = (bf16[608,128]{1,0:T(8,128)(2,1)S(1)}, bf16[608,128]{1,0:T(8,128)(2,1)S(1)}, u32[]{:S(2)}, u32[]{:S(2)}) collective-permute-start(bf16[608,128]{1,0:T(8,128)(2,1)S(1)} %shard_map.110.refs_0_), channel_id=1, source_target_pairs={{0,4},{1,5},{2,6},{3,7},{4,0},{5,1},{6,2},{7,3},{8,12},{9,13},{10,... | collective-permute-start | bytes 466952 | tf_op jit(solution)/shard_map/ppermute | solution.py:388
  107.8 6.1 %collective-permute-start.20 = (bf16[608,128]{1,0:T(8,128)(2,1)S(1)}, bf16[608,128]{1,0:T(8,128)(2,1)S(1)}, u32[]{:S(2)}, u32[]{:S(2)}) collective-permute-start(bf16[608,128]{1,0:T(8,128)(2,1)S(1)} %shard_map.110.refs_0_), channel_id=1, source_target_pairs={{0,6},{1,7},{2,4},{3,5},{4,2},{5,3},{6,0},{7,1},{8,14},{9,15},{10,... | collective-permute-start | bytes 466952 | tf_op jit(solution)/shard_map/ppermute | solution.py:388
  114.0 2.1 %collective-permute-start.21 = (bf16[2432,128]{1,0:T(8,128)(2,1)S(1)}, bf16[2432,128]{1,0:T(8,128)(2,1)S(1)}, u32[]{:S(2)}, u32[]{:S(2)}) collective-permute-start(bf16[2432,128]{1,0:T(8,128)(2,1)S(1)} %shard_map.112.own_ref), channel_id=1, source_target_pairs={{0,1},{1,0},{2,3},{3,2},{4,5},{5,4},{6,7},{7,6},{8,9},{9,8},{10,11... | collective-permute-start | bytes 1867784 | tf_op jit(solution)/shard_map/ppermute | solution.py:388
  (1 other events, 14.9 us)

commit v3 on v2

--- a/solution.py
+++ b/solution.py
@@ -22,7 +22,7 @@
     return lax.broadcasted_iota(I32, shape, dim)
 
 
-def kernel_call(body, outs, args, flops=0, scratch=(), smem=(), hbm=(), far=(), temp=2):
+def kernel_call(body, outs, args, flops=0, scratch=(), smem=(), hbm=(), far=(), temp=2, alias={}):
     spaces = [
         pltpu.SMEM if i in smem else pltpu.HBM if i in hbm else pltpu.VMEM for i in range(len(args))
     ]
@@ -40,6 +40,7 @@
             pl.BlockSpec(memory_space=pltpu.HBM if i in far else pltpu.VMEM) for i in range(len(outs))
         ],
         scratch_shapes=list(scratch),
+        input_output_aliases=alias,
         compiler_params=pltpu.CompilerParams(vmem_limit_bytes=limit),
         cost_estimate=pl.CostEstimate(flops=flops, bytes_accessed=moved, transcendentals=0),
     )(*[pltpu.with_memory_space_constraint(a, pltpu.HBM) if i in hbm else a for i, a in enumerate(args)])
@@ -107,12 +108,15 @@
 
 
 def unroute_body(place_ref, back_ref, out_ref):
-    records = place_ref.shape[0]
+    records = place_ref.shape[1]
     count = back_ref.shape[0]
     size = 512
+    place = place_ref[...].astype(F32)
+    place = jnp.concatenate([place[:, i : i + 128] for i in range(0, records, 128)], axis=0)
+    place = place.T.astype(I32)
     for blk in range(records // size):
-        place = place_ref[blk * size : (blk + 1) * size, :]
-        mask = (iota((size, count), 1) == place).astype(BF)
+        at = jnp.concatenate([place[:, blk * 4 + q : blk * 4 + q + 1] for q in range(4)], axis=0)
+        mask = (iota((size, count), 1) == at).astype(BF)
         out_ref[blk * size : (blk + 1) * size, :] = dot(mask, back_ref[...]).astype(BF)
 
 
@@ -123,27 +127,38 @@
     return jnp.where(iota((cols, 1), 0) == at, edge.astype(F32), wide).astype(BF)
 
 
-def conv_body(inside_ref, grid_hbm, left_ref, right_ref, top_ref, bottom_ref, w_hbm, *refs, back):
+def conv_body(inside_ref, grid_hbm, left_ref, right_ref, top_ref, bottom_ref, w_hbm, *refs, back, start, total):
     if back:
-        out_hbm, pad_hbm, grid_ref, w_ref, pad_ref, out_ref, in_sem, w_sem, out_sem, pad_sem = refs
+        out_hbm, pad_hbm, grid_ref, w_ref, pad_ref, out_ref, left32, right32, in_sem, w_sem, out_sem, pad_sem = refs
     else:
-        out_hbm, grid_ref, w_ref, pad_ref, out_ref, in_sem, w_sem, out_sem = refs
-    rows, cols, width = grid_ref.shape
+        out_hbm, grid_ref, pad_ref, out_ref, left32, right32, in_sem, out_sem = refs[-8:]
+        w_ref = w_hbm
+    rows, cols, width = out_ref.shape
+    held = grid_ref.shape[0]
+    base = max(start - 1, 0)
     high = 8
     blocks = rows // high
-
-    def band(n):
-        return slice(n * high, (n + 1) * high)
-
-    loads = [begin(grid_hbm.at[band(n)], grid_ref.at[band(n)], in_sem.at[n]) for n in range(blocks)]
-    load_w = begin(w_hbm, w_ref, w_sem)
+    cuts = [*range(0, held - 1, high), held]
+    loads = [
+        begin(grid_hbm.at[base + i : base + j], grid_ref.at[i:j], in_sem.at[n])
+        for n, (i, j) in enumerate(zip(cuts[:-1], cuts[1:]))
+    ]
+    if back:
+        load_w = begin(w_hbm, w_ref, w_sem)
+    left32[...] = left_ref[...].astype(F32)
+    right32[...] = right_ref[...].astype(F32)
 
     def put(i, row, left, right):
         pad_ref[0, i] = shifted(row, left, 1)
         pad_ref[1, i] = row
         pad_ref[2, i] = shifted(row, right, -1)
 
-    for side, i, ref in ((0, 0, top_ref), (1, rows + 1, bottom_ref)):
+    ends = []
+    if start == 0:
+        ends.append((0, 0, top_ref))
+    if start + rows == total:
+        ends.append((1, rows + 1, bottom_ref))
+    for side, i, ref in ends:
 
         @pl.when(inside_ref[side] > 0)
         def _():
@@ -155,24 +170,26 @@
                 pad_ref[b, i] = jnp.zeros(pad_ref.shape[2:], BF)
 
     def fill(i, carry):
-        put(i + 1, grid_ref[i], left_ref[i], right_ref[i])
+        at = pl.ds(base + i, 1)
+        put(base + i + 1 - start, grid_ref[i], left32[at, :], right32[at, :])
         return carry
 
-    for n in range(blocks):
-        loads[n].wait()
-        lax.fori_loop(n * high, (n + 1) * high, fill, 0)
+    for load, i, j in zip(loads, cuts[:-1], cuts[1:]):
+        load.wait()
+        lax.fori_loop(i, j, fill, 0)
     stores = []
     if back:
         stores += [begin(pad_ref.at[b], pad_hbm.at[b], pad_sem.at[b]) for b in range(3)]
-    load_w.wait()
+        load_w.wait()
 
     def store(n):
-        some = pl.ds(n * high, high)
-        return pltpu.make_async_copy(out_ref.at[some], out_hbm.at[some], out_sem.at[n])
+        return pltpu.make_async_copy(
+            out_ref.at[pl.ds(n * high, high)], out_hbm.at[pl.ds(start + n * high, high)], out_sem.at[n]
+        )
 
     def step(n, carry):
         i = n * high
-        acc = grid_ref[pl.ds(i, high)].astype(F32).reshape(high * cols, width)
+        acc = grid_ref[pl.ds(start - base + i, high)].astype(F32).reshape(high * cols, width)
         for a in range(3):
             for b in range(3):
                 part = pad_ref[b, pl.ds(i + a, high)].reshape(high * cols, width)
@@ -189,21 +206,18 @@
         move.wait()
 
 
-def side_edges(grid):
-    cols = grid.shape[1]
+def side_edges(last, first):
     count = lax.axis_size("lon")
     up = [(i, (i + 1) % count) for i in range(count)]
     down = [(j, i) for i, j in up]
-    left = lax.ppermute(grid[:, cols - 1 :, :], "lon", up)
-    right = lax.ppermute(grid[:, :1, :], "lon", down)
-    return left, right
+    return lax.ppermute(last, "lon", up), lax.ppermute(first, "lon", down)
 
 
 def end_rows(grid, left, right):
     pad = ((0, 7), (0, 0))
 
     def row(i):
-        return jnp.concatenate([grid[i], jnp.pad(left[i], pad), jnp.pad(right[i], pad)], axis=0)
+        return jnp.concatenate([grid[i], jnp.pad(left[i][None], pad), jnp.pad(right[i][None], pad)], axis=0)
 
     return row(grid.shape[0] - 1), row(0)
 
@@ -215,29 +229,40 @@
     return lax.ppermute(last, "lat", up), lax.ppermute(first, "lat", down)
 
 
-def conv(grid, halo, w, back):
-    rows, cols, width = grid.shape
+def conv(grid, halo, w, back, start=0, stop=None, into=None):
+    total, cols, width = grid.shape
+    stop = stop or total
+    rows = stop - start
+    held = min(stop + 1, total) - max(start - 1, 0)
     outs = [shape(grid.shape, BF)]
     pad = (3, rows + 2, cols, width)
     blocks = rows // 8
     scratch = [
-        pltpu.VMEM(grid.shape, BF),
-        pltpu.VMEM(w.shape, BF),
+        pltpu.VMEM((held, cols, width), BF),
         pltpu.VMEM(pad, BF),
-        pltpu.VMEM(grid.shape, BF),
-        DMA((blocks,)),
-        DMA,
+        pltpu.VMEM((rows, cols, width), BF),
+        pltpu.VMEM((total, width), F32),
+        pltpu.VMEM((total, width), F32),
+        DMA((blocks + 1,)),
         DMA((blocks,)),
     ]
     if back:
         outs.append(shape(pad, BF))
+        scratch.insert(1, pltpu.VMEM(w.shape, BF))
+        scratch.insert(7, DMA)
         scratch.append(DMA((3,)))
     flops = 18 * rows * cols * width * width
-    body = functools.partial(conv_body, back=back)
+    body = functools.partial(conv_body, back=back, start=start, total=total)
     at = lax.axis_index("lat")
     inside = jnp.stack([at > 0, at < lax.axis_size("lat") - 1]).astype(I32)
-    args = (inside, grid, *halo, w)
-    return kernel_call(body, outs, args, flops, scratch, smem=(0,), hbm=(1, 6), far=(0, 1), temp=8)
+    args = [inside, grid, *halo, w]
+    alias = {}
+    if into is not None:
+        alias = {len(args): 0}
+        args.append(into)
+    return kernel_call(
+        body, outs, args, flops, scratch, smem=(0,), hbm=(1, 6 if back else 7), far=(0, 1), temp=8, alias=alias
+    )
 
 
 def gelu_parts(x):
@@ -308,15 +333,13 @@
 
 
 def field_body(
-    me_ref, code_hbm, embed_hbm, bg_hbm, pad_hbm, eg_hbm, field_hbm, keep_ref, give_ref,
-    code_ref, embed_ref, bg_ref, pad_ref, eg_ref, field_ref, acc_ref, sems, pad_sems, out_sems,
+    me_ref, code_hbm, embed_hbm, bg_hbm, pad_hbm, eg_hbm, field_hbm, keep_ref, give_ref, last_ref, first_ref,
+    code_ref, embed_ref, bg_ref, pad_ref, eg_ref, field_ref, acc_ref, last32, first32, sems, pad_sems, out_sems, bg_sems,
 ):
     loads = [
         begin(code_hbm, code_ref, sems.at[0]),
         begin(embed_hbm, embed_ref, sems.at[1]),
-        begin(bg_hbm, bg_ref, sems.at[2]),
-        begin(pad_hbm, pad_ref, pad_sems),
-        begin(eg_hbm, eg_ref, sems.at[3]),
+        begin(pad_hbm.at[:, :2], pad_ref.at[:, :2], sems.at[4]),
     ]
     cells, width = bg_ref.shape
     cols = pad_ref.shape[2]
@@ -324,6 +347,20 @@
     size = 512
     deep = 2 * size
     high = deep // cols
+    blocks = cells // deep
+
+    def load_pad(n):
+        some = pl.ds(n * high + 2, high)
+        return pltpu.make_async_copy(pad_hbm.at[:, some], pad_ref.at[:, some], pad_sems.at[n])
+
+    def load_bg(n):
+        some = pl.ds(pl.multiple_of(n * deep, deep), deep)
+        return pltpu.make_async_copy(bg_hbm.at[some], bg_ref.at[some], bg_sems.at[n])
+
+    for n in range(blocks):
+        load_bg(n).start()
+        load_pad(n).start()
+    loads.append(begin(eg_hbm, eg_ref, sems.at[3]))
     acc_ref[...] = jnp.zeros_like(acc_ref)
     for move in loads[:3]:
         move.wait()
@@ -343,6 +380,10 @@
             at = pl.ds(pl.multiple_of(base, size), size)
             total = dot(mask, embed_ref[...]) + bg_ref[at, :].astype(F32)
             field_ref[at, :] = total.astype(BF)
+            for g in range(size // cols):
+                row = pl.ds(base // cols + g, 1)
+                first32[row, :] = total[g * cols : g * cols + 1]
+                last32[row, :] = total[(g + 1) * cols - 1 : (g + 1) * cols]
         store(n).start()
 
     def correlate(n):
@@ -353,16 +394,16 @@
                 acc_ref[3 * a + b] += dot(field, part, 0, 0)
 
     def step(n, carry):
+        load_bg(n).wait()
         scatter(n)
+        load_pad(n).wait()
         correlate(n)
         return carry
 
-    blocks = cells // deep
-    scatter(0)
+    lax.fori_loop(0, blocks, step, 0)
     loads[3].wait()
-    correlate(0)
-    lax.fori_loop(1, blocks, step, 0)
-    loads[4].wait()
+    last_ref[...] = last32[...].astype(BF)
+    first_ref[...] = first32[...].astype(BF)
     side = me_ref[0] % 2
     taps = acc_ref.shape[0]
     used = taps * width
@@ -449,7 +490,7 @@
     return [bits[i : i + 2] for i in range(0, len(bits), 2)]
 
 
-def reduce_all(me, keeps, gives, taps, width, inputs, beside, encode, unroute):
+def reduce_all(me, keeps, gives, taps, width, inputs, beside, halo_of, encode, unroute):
     count = lax.axis_size("lon") * lax.axis_size("lat")
     terms = [*keeps, *(swap(x, 1) for x in gives)]
     half = width // 2
@@ -465,11 +506,13 @@
         body = functools.partial(split_body, moves=moves, parts=parts)
         own, *send = kernel_call(body, outs, (mine, *terms), smem=(0,))
         if bits is plan[0]:
-            send, back = lax.optimization_barrier((send, beside[0]))
-            found = encode(beside[1])
+            send, edges = lax.optimization_barrier((send, beside[1]))
+            halo = halo_of(edges)
         terms = [own] + [swap(x, m * bits[0]) for m, x in zip(moves, send)]
         if bits is plan[0]:
-            terms, found = lax.optimization_barrier((terms, found))
+            terms, back = lax.optimization_barrier((terms, beside[0]))
+        if bits is plan[-1]:
+            terms, gone = lax.optimization_barrier((terms, unroute(back)))
     body = functools.partial(split_body, moves=[], parts=1)
     (block,) = kernel_call(
         body, [shape(terms[0].shape, BF)], (jnp.zeros((1,), I32), *terms), smem=(0,)
@@ -478,8 +521,10 @@
         ways = 2 ** len(bits)
         mine = (me // bits[0]) % ways
         pieces = [block] + [swap(block, m * bits[0]) for m in range(1, ways)]
+        if bits is plan[-1]:
+            pieces, found = lax.optimization_barrier((pieces, encode(halo, 0, None)))
         if bits is plan[0]:
-            pieces, gone = lax.optimization_barrier((pieces, unroute(back)))
+            pieces, found = lax.optimization_barrier((pieces, encode(halo, 1, found)))
         rows = block.shape[0]
         body = functools.partial(join_body, parts=parts)
         (block,) = kernel_call(body, [shape((rows * ways, half), BF)], (mine, *pieces), smem=(0,))
@@ -516,7 +561,7 @@
         hbm=(1, 2, 3),
         temp=4,
     )
-    sides = side_edges(cotangent)
+    sides = side_edges(cotangent[:, cols - 1], cotangent[:, 0])
     send, sides = lax.optimization_barrier((send, sides))
     ends = end_rows(cotangent, *sides)
     send, ends = lax.optimization_barrier((send, ends))
@@ -555,9 +600,11 @@
     size = 8 * blocks
     total = -(-(taps * width + inputs) // size) * size
     back = lax.all_to_all(grad.reshape(owners, slots, width), AXES, split_axis=0, concat_axis=0, tiled=True)
-    field, keep, give = kernel_call(
+    field, keep, give, last, first = kernel_call(
         field_body,
-        [shape((cells, width), BF)] + [shape((total, width // 2), F32)] * 2,
+        [shape((cells, width), BF)]
+        + [shape((total, width // 2), F32)] * 2
+        + [shape((rows, width), BF)] * 2,
         (me, codes, embed, background.reshape(cells, width), pad, local_eg),
         flops=2 * count * cells * width + 18 * cells * width * width,
         scratch=[
@@ -568,8 +615,11 @@
             pltpu.VMEM((inputs, width), F32),
             pltpu.VMEM((cells, width), BF),
             pltpu.VMEM((taps, width, width), F32),
-            DMA((4,)),
-            DMA,
+            pltpu.VMEM((rows, width), F32),
+            pltpu.VMEM((rows, width), F32),
+            DMA((5,)),
+            DMA((cells // 1024,)),
+            DMA((cells // 1024,)),
             DMA((cells // 1024,)),
         ],
         smem=(0,),
@@ -578,23 +628,26 @@
         temp=8,
     )
     grid = field.reshape(rows, cols, width)
-    sides = side_edges(grid)
-    halo = (*sides, *end_edges(*end_rows(grid, *sides)))
-
-    def encode(halo):
-        return conv(grid, halo, w_conv, False)[0]
+
+    def halo_of(edges):
+        sides = side_edges(*edges)
+        return (*sides, *end_edges(*end_rows(grid, *sides)))
+
+    def encode(halo, part, into):
+        half = rows // 2
+        return conv(grid, halo, w_conv, False, part * half, (part + 1) * half, into)[0]
 
     def unroute(back):
         return kernel_call(
             unroute_body,
             [shape((records, width), BF)],
-            (place.reshape(records, 1), back.reshape(count, width)),
+            (place, back.reshape(count, width)),
             flops=2 * count * records * width,
             temp=4,
         )[0]
 
     (conv_grad, embed_grad), encoded, record_grad = reduce_all(
-        me, (keep,), (give,), taps, width, inputs, (back, halo), encode, unroute
+        me, (keep,), (give,), taps, width, inputs, (back, (last, first)), halo_of, encode, unroute
     )
     return encoded, record_grad, conv_grad, embed_grad
 

time: 118 us -> 112 us (0.949)
  waiting for transfers between devices: 22.6 us -> 16.9 us
  Pallas kernels: 50.1 us -> 51.8 us
  local copies, waits for them, and re-layouts: 4.05 us -> 2.84 us
    all_to_all x1, waiting for transfers between devices: 2.51 us -> 0.01 us  [on_device(): lax.all_to_all(grad.reshape(owners, slots, width), AXES, split_axis=0, co...]
    pallas_call x12 -> x13, Pallas kernels: 50.1 us -> 51.8 us  [kernel_call(): pl.pallas_call(body, out_shape=[pltpu.HBM(o.shape, o.dtype) if i in far e...]
    ppermute x4, waiting for transfers between devices: 1.63 us -> 0.01 us  [side_edges(): return (lax.ppermute(last, 'lon', up), lax.ppermute(first, 'lon', down))]
    ppermute x14, waiting for transfers between devices: 12.9 us -> 11.2 us  [swap(): return lax.ppermute(x, AXES, [(i, i ^ bit) for i in range(count)])]
  transfers between devices with their start and end apart: 24 -> 24, of which waited for: 12 -> 9; matrix products, arithmetic and copies ran while one was open for 3% -> 2% of each run, Pallas kernels for 33% -> 36%
where the time goes in v3:
time: 112 us
  Pallas kernels  51.8 us (46%)
  starting transfers between devices  39.3 us (35%)
  waiting for transfers between devices  16.9 us (15%)
  local copies, waits for them, and re-layouts  2.84 us (3%)
    pallas_call x13, Pallas kernels, kernel_call(): pl.pallas_call(body, out_shape=[pltpu.HBM(o.shape, o.dtype) if i in far e...  51.8 us
    ppermute x14, starting transfers between devices, swap(): return lax.ppermute(x, AXES, [(i, i ^ bit) for i in range(count)])  16.2 us
    ppermute x14, waiting for transfers between devices, swap(): return lax.ppermute(x, AXES, [(i, i ^ bit) for i in range(count)])  11.2 us
    ppermute x4, starting transfers between devices, side_edges(): return (lax.ppermute(last, 'lon', up), lax.ppermute(first, 'lon', down))  10.9 us
    all_to_all x1, starting transfers between devices, on_device(): lax.all_to_all(grad.reshape(owners, slots, width), AXES, split_axis=0, co...  6.18 us
    ppermute x4, waiting for transfers between devices, end_edges(): return (lax.ppermute(last, 'lat', up), lax.ppermute(first, 'lat', down))  5.52 us
    all_to_all x1, starting transfers between devices, on_device(): recv = lax.all_to_all(send, AXES, split_axis=0, concat_axis=0, tiled=True)  3.59 us
    ppermute x4, starting transfers between devices, end_edges(): return (lax.ppermute(last, 'lat', up), lax.ppermute(first, 'lat', down))  2.39 us
  transfers between devices with their start and end apart: 24, of which 9 were waited for; matrix products, arithmetic and copies ran while one was open for 2% of the time, Pallas kernels for 36%

profile of v3, /device:TPU:0, one launch (start us, length us, event | category | flops | bytes accessed | tf_op | source)
XLA Modules:
  0.0 112.0 jit_solution(4801038956408726584)
XLA Ops:
  1.7 3.0 %collective-permute-start = (bf16[32,256]{1,0:T(8,128)(2,1)S(1)}, bf16[32,256]{1,0:T(8,128)(2,1)S(1)}, u32[]{:S(2)}, u32[]{:S(2)}) collective-permute-start(bf16[32,256]{1,0:T(8,128)(2,1)S(1)} %bitcast.22), channel_id=1, source_target_pairs={{0,4},{4,8},{8,12},{12,16},{16,20},{20,24},{24,28},{28,0},{1,5},{5... | collective-permute-start | bytes 49160 | tf_op jit(solution)/shard_map/ppermute | solution.py:213
  4.7 3.1 %collective-permute-start.1 = (bf16[32,256]{1,0:T(8,128)(2,1)S(1)}, bf16[32,256]{1,0:T(8,128)(2,1)S(1)}, u32[]{:S(2)}, u32[]{:S(2)}) collective-permute-start(bf16[32,256]{1,0:T(8,128)(2,1)S(1)} %bitcast.23), channel_id=1, source_target_pairs={{4,0},{8,4},{12,8},{16,12},{20,16},{24,20},{28,24},{0,28},{5,1},{9... | collective-permute-start | bytes 49160 | tf_op jit(solution)/shard_map/ppermute | solution.py:213
  8.7 3.4 %shard_map.102 = (bf16[32,72,128]{2,1,0:T(8,128)(2,1)}, s32[1,1024]{1,0:T(1,128)S(1)}) custom-call(s32[1]{0:T(128)} %bitcast.me_ref, s32[1,1024]{1,0:T(1,128)} %bitcast.27, s32[1,1024]{1,0:T(1,128)} %bitcast.28, bf16[1024,128]{1,0:T(8,128)(2,1)} %feat_hbm.1), custom_call_target="tpu_custom_call" | custom-call | flops 536870912 | bytes 864260 | tf_op jit(solution)/shard_map/pallas_call | solution.py:35
  12.2 3.6 %all-to-all-start = ((bf16[32,72,128]{2,1,0:T(8,128)(2,1)}), bf16[32,72,128]{2,1,0:T(8,128)(2,1)S(1)}, u32[]{:S(2)}, u32[]{:S(2)}) async-start(bf16[32,72,128]{2,1,0:T(8,128)(2,1)} %get-tuple-element.62), calls=%async_computation | async-start | bytes 1179648 | tf_op jit(solution)/shard_map/all_to_all | solution.py:569
  17.7 3.9 %collective-permute-done.2.top_ref = bf16[144,256]{1,0:T(8,128)(2,1)S(1)} collective-permute-done((bf16[144,256]{1,0:T(8,128)(2,1)S(1)}, bf16[144,256]{1,0:T(8,128)(2,1)S(1)}, u32[]{:S(2)}, u32[]{:S(2)}) %collective-permute-start.2) | collective-permute-done | bytes 73760 | tf_op jit(solution)/shard_map/ppermute | solution.py:229
  23.2 9.2 %shard_map.103 = (bf16[32,128,256]{2,1,0:T(8,128)(2,1)}, bf16[3,34,128,256]{3,2,1,0:T(8,128)(2,1)}) custom-call(s32[2]{0:T(128)S(1)} %add_convert_fusion.inside_ref, bf16[32,128,256]{2,1,0:T(8,128)(2,1)} %grid_hbm.1, bf16[32,256]{1,0:T(8,128)(2,1)S(1)} %collective-permute-done.left_ref, bf16[32,256]{1,0:T(8,128)(2,1)S(1)} %collective-permute-done.1.right_ref, ...), custom_call_target="tpu_custom_call" | custom-call | flops 4831838208 | bytes 12238856 | tf_op jit(solution)/shard_map/pallas_call | solution.py:35
  32.5 9.8 %shard_map.104 = (bf16[2048,256]{1,0:T(8,128)(2,1)}, f32[128,256]{1,0:T(8,128)}, bf16[2048,256]{1,0:T(8,128)(2,1)}, f32[16,128]{1,0:T(8,128)}) custom-call(bf16[32,72,128]{2,1,0:T(8,128)(2,1)S(1)} %all-to-all-done.recv_ref, bf16[4096,256]{1,0:T(8,128)(2,1)} %bitcast.29, bf16[128,256]{1,0:T(8,128)(2,1)S(1)} %copy-done.1), custom_call_target="tpu_custom_call" | custom-call | flops 4294967296 | bytes 4988928 | tf_op jit(solution)/shard_map/pallas_call | solution.py:35
  42.3 6.2 %all-to-all-start.1 = ((bf16[32,64,256]{2,1,0:T(8,128)(2,1)}), bf16[32,64,256]{2,1,0:T(8,128)(2,1)S(1)}, u32[]{:S(2)}, u32[]{:S(2)}) async-start(bf16[32,64,256]{2,1,0:T(8,128)(2,1)} %bitcast.21), calls=%async_computation.1 | async-start | bytes 2097152 | tf_op jit(solution)/shard_map/all_to_all | solution.py:602
  48.5 13.6 %shard_map.105 = (bf16[4096,256]{1,0:T(8,128)(2,1)}, f32[2432,128]{1,0:T(8,128)S(1)}, f32[2432,128]{1,0:T(8,128)S(1)}, bf16[32,256]{1,0:T(8,128)(2,1)S(1)}, bf16[32,256]{1,0:T(8,128)(2,1)S(1)}) custom-call(s32[1]{0:T(128)} %bitcast.me_ref, f32[16,128]{1,0:T(8,128)} %get-tuple-element.66.code_hbm, bf16[2048,256]{1,0:T(8,128)(2,1)} %get-tuple-element.67.embed_hbm, ...), custom_call_target="tpu_custom_call" | custom-call | flops 9126805504 | bytes 14589956 | tf_op jit(solution)/shard_map/pallas_call | solution.py:35
  62.3 2.9 %collective-permute-done.4.refs_1_ = f32[2432,128]{1,0:T(8,128)S(1)} collective-permute-done((f32[2432,128]{1,0:T(8,128)S(1)}, f32[2432,128]{1,0:T(8,128)S(1)}, u32[]{:S(2)}, u32[]{:S(2)}) %collective-permute-start.4) | collective-permute-done | bytes 1245216 | tf_op jit(solution)/shard_map/ppermute | solution.py:429
  65.4 1.6 %collective-permute-start.14 = (bf16[32,256]{1,0:T(8,128)(2,1)S(1)}, bf16[32,256]{1,0:T(8,128)(2,1)S(1)}, u32[]{:S(2)}, u32[]{:S(2)}) collective-permute-start(bf16[32,256]{1,0:T(8,128)(2,1)S(1)} %get-tuple-element.97), channel_id=1, source_target_pairs={{0,4},{4,8},{8,12},{12,16},{16,20},{20,24},{24,28},{28,0},{1,5},{5... | collective-permute-start | bytes 49160 | tf_op jit(solution)/shard_map/ppermute | solution.py:213
  67.0 3.1 %collective-permute-start.15 = (bf16[32,256]{1,0:T(8,128)(2,1)S(1)}, bf16[32,256]{1,0:T(8,128)(2,1)S(1)}, u32[]{:S(2)}, u32[]{:S(2)}) collective-permute-start(bf16[32,256]{1,0:T(8,128)(2,1)S(1)} %get-tuple-element.98), channel_id=1, source_target_pairs={{4,0},{8,4},{12,8},{16,12},{20,16},{24,20},{28,24},{0,28},{5,1},{9... | collective-permute-start | bytes 49160 | tf_op jit(solution)/shard_map/ppermute | solution.py:213
  71.0 1.7 %collective-permute-start.5 = (bf16[608,128]{1,0:T(8,128)(2,1)S(1)}, bf16[608,128]{1,0:T(8,128)(2,1)S(1)}, u32[]{:S(2)}, u32[]{:S(2)}) collective-permute-start(bf16[608,128]{1,0:T(8,128)(2,1)S(1)} %get-tuple-element.78), channel_id=1, source_target_pairs={{0,2},{1,3},{2,0},{3,1},{4,6},{5,7},{6,4},{7,5},{8,10},{9,11},{10,... | collective-permute-start | bytes 466952 | tf_op jit(solution)/shard_map/ppermute | solution.py:429
  72.7 1.9 %collective-permute-start.7 = (bf16[608,128]{1,0:T(8,128)(2,1)S(1)}, bf16[608,128]{1,0:T(8,128)(2,1)S(1)}, u32[]{:S(2)}, u32[]{:S(2)}) collective-permute-start(bf16[608,128]{1,0:T(8,128)(2,1)S(1)} %get-tuple-element.80), channel_id=1, source_target_pairs={{0,6},{1,7},{2,4},{3,5},{4,2},{5,3},{6,0},{7,1},{8,14},{9,15},{10,... | collective-permute-start | bytes 466952 | tf_op jit(solution)/shard_map/ppermute | solution.py:429
  75.3 1.6 %collective-permute-done.5.refs_1_ = bf16[608,128]{1,0:T(8,128)(2,1)S(1)} collective-permute-done((bf16[608,128]{1,0:T(8,128)(2,1)S(1)}, bf16[608,128]{1,0:T(8,128)(2,1)S(1)}, u32[]{:S(2)}, u32[]{:S(2)}) %collective-permute-start.5) | collective-permute-done | bytes 155680 | tf_op jit(solution)/shard_map/ppermute | solution.py:429
  76.9 2.7 %collective-permute-done.6.refs_2_ = bf16[608,128]{1,0:T(8,128)(2,1)S(1)} collective-permute-done((bf16[608,128]{1,0:T(8,128)(2,1)S(1)}, bf16[608,128]{1,0:T(8,128)(2,1)S(1)}, u32[]{:S(2)}, u32[]{:S(2)}) %collective-permute-start.6) | collective-permute-done | bytes 155680 | tf_op jit(solution)/shard_map/ppermute | solution.py:429
  79.6 2.0 %collective-permute-done.7.refs_3_ = bf16[608,128]{1,0:T(8,128)(2,1)S(1)} collective-permute-done((bf16[608,128]{1,0:T(8,128)(2,1)S(1)}, bf16[608,128]{1,0:T(8,128)(2,1)S(1)}, u32[]{:S(2)}, u32[]{:S(2)}) %collective-permute-start.7) | collective-permute-done | bytes 155680 | tf_op jit(solution)/shard_map/ppermute | solution.py:429
  83.7 2.4 %collective-permute-start.9 = (bf16[152,128]{1,0:T(8,128)(2,1)S(1)}, bf16[152,128]{1,0:T(8,128)(2,1)S(1)}, u32[]{:S(2)}, u32[]{:S(2)}) collective-permute-start(bf16[152,128]{1,0:T(8,128)(2,1)S(1)} %get-tuple-element.88), channel_id=1, source_target_pairs={{0,16},{1,17},{2,18},{3,19},{4,20},{5,21},{6,22},{7,23},{8,24},{9,... | collective-permute-start | bytes 116744 | tf_op jit(solution)/shard_map/ppermute | solution.py:429
  86.1 2.4 %shard_map.108 = bf16[1024,256]{1,0:T(8,128)(2,1)} custom-call(s32[1,1024]{1,0:T(1,128)S(1)} %get-tuple-element.90.place_ref, bf16[2048,256]{1,0:T(8,128)(2,1)S(1)} %bitcast.20), custom_call_target="tpu_custom_call" | custom-call | flops 1073741824 | bytes 1576960 | tf_op jit(solution)/shard_map/pallas_call | solution.py:35
  91.2 1.9 %collective-permute-start.13 = (bf16[152,128]{1,0:T(8,128)(2,1)S(1)}, bf16[152,128]{1,0:T(8,128)(2,1)S(1)}, u32[]{:S(2)}, u32[]{:S(2)}) collective-permute-start(bf16[152,128]{1,0:T(8,128)(2,1)S(1)} %shard_map.109.refs_0_), channel_id=1, source_target_pairs={{0,24},{1,25},{2,26},{3,27},{4,28},{5,29},{6,30},{7,31},{8,16},{9,... | collective-permute-start | bytes 116744 | tf_op jit(solution)/shard_map/ppermute | solution.py:429
  93.1 5.7 %shard_map.110.refs_0_ = bf16[32,128,256]{2,1,0:T(8,128)(2,1)} custom-call(s32[2]{0:T(128)S(1)} %add_convert_fusion.inside_ref, bf16[32,128,256]{2,1,0:T(8,128)(2,1)} %bitcast.24, bf16[32,256]{1,0:T(8,128)(2,1)S(1)} %collective-permute-done.14.left_ref, bf16[32,256]{1,0:T(8,128)(2,1)S(1)} %collective-permute-done.15.right_ref, ...), custom_call_target="tpu_custom_call" | custom-call | flops 2415919104 | bytes 5554184 | tf_op jit(solution)/shard_map/pallas_call | solution.py:35
  100.8 1.7 %collective-permute-start.20 = (bf16[608,128]{1,0:T(8,128)(2,1)S(1)}, bf16[608,128]{1,0:T(8,128)(2,1)S(1)}, u32[]{:S(2)}, u32[]{:S(2)}) collective-permute-start(bf16[608,128]{1,0:T(8,128)(2,1)S(1)} %shard_map.111.refs_0_), channel_id=1, source_target_pairs={{0,6},{1,7},{2,4},{3,5},{4,2},{5,3},{6,0},{7,1},{8,14},{9,15},{10,... | collective-permute-start | bytes 466952 | tf_op jit(solution)/shard_map/ppermute | solution.py:429
  102.4 5.7 %shard_map.112 = bf16[32,128,256]{2,1,0:T(8,128)(2,1)} custom-call(s32[2]{0:T(128)S(1)} %add_convert_fusion.inside_ref, bf16[32,128,256]{2,1,0:T(8,128)(2,1)} %bitcast.25, bf16[32,256]{1,0:T(8,128)(2,1)S(1)} %collective-permute-done.14.left_ref, bf16[32,256]{1,0:T(8,128)(2,1)S(1)} %collective-permute-done.15.right_ref, ...), custom_call_target="tpu_custom_call", output_to_operand_aliasing={{}: (7, {})} | custom-call | flops 2415919104 | bytes 7651336 | tf_op jit(solution)/shard_map/pallas_call | solution.py:35
  108.3 2.0 %collective-permute-done.21.other_ref = bf16[2432,128]{1,0:T(8,128)(2,1)S(1)} collective-permute-done((bf16[2432,128]{1,0:T(8,128)(2,1)S(1)}, bf16[2432,128]{1,0:T(8,128)(2,1)S(1)}, u32[]{:S(2)}, u32[]{:S(2)}) %collective-permute-start.21) | collective-permute-done | bytes 622624 | tf_op jit(solution)/shard_map/ppermute | solution.py:429
  (58 shorter events, 16.0 us)
Async XLA Ops:
  1.7 10.4 %collective-permute-start = (bf16[32,256]{1,0:T(8,128)(2,1)S(1)}, bf16[32,256]{1,0:T(8,128)(2,1)S(1)}, u32[]{:S(2)}, u32[]{:S(2)}) collective-permute-start(bf16[32,256]{1,0:T(8,128)(2,1)S(1)} %bitcast.22), channel_id=1, source_target_pairs={{0,4},{4,8},{8,12},{12,16},{16,20},{20,24},{24,28},{28,0},{1,5},{5... | collective-permute-start | bytes 49160 | tf_op jit(solution)/shard_map/ppermute | solution.py:213
  4.7 7.4 %collective-permute-start.1 = (bf16[32,256]{1,0:T(8,128)(2,1)S(1)}, bf16[32,256]{1,0:T(8,128)(2,1)S(1)}, u32[]{:S(2)}, u32[]{:S(2)}) collective-permute-start(bf16[32,256]{1,0:T(8,128)(2,1)S(1)} %bitcast.23), channel_id=1, source_target_pairs={{4,0},{8,4},{12,8},{16,12},{20,16},{24,20},{28,24},{0,28},{5,1},{9... | collective-permute-start | bytes 49160 | tf_op jit(solution)/shard_map/ppermute | solution.py:213
  12.2 20.3 %all-to-all-start = ((bf16[32,72,128]{2,1,0:T(8,128)(2,1)}), bf16[32,72,128]{2,1,0:T(8,128)(2,1)S(1)}, u32[]{:S(2)}, u32[]{:S(2)}) async-start(bf16[32,72,128]{2,1,0:T(8,128)(2,1)} %get-tuple-element.62), calls=%async_computation | async-start | bytes 1179648 | tf_op jit(solution)/shard_map/all_to_all | solution.py:569
  15.8 5.8 %collective-permute-start.2 = (bf16[144,256]{1,0:T(8,128)(2,1)S(1)}, bf16[144,256]{1,0:T(8,128)(2,1)S(1)}, u32[]{:S(2)}, u32[]{:S(2)}) collective-permute-start(bf16[144,256]{1,0:T(8,128)(2,1)S(1)} %get-tuple-element.63), channel_id=1, source_target_pairs={{0,1},{1,2},{2,3},{3,0},{4,5},{5,6},{6,7},{7,4},{8,9},{9,10},{10,1... | collective-permute-start | bytes 221192 | tf_op jit(solution)/shard_map/ppermute | solution.py:229
  16.1 7.1 %collective-permute-start.3 = (bf16[144,256]{1,0:T(8,128)(2,1)S(1)}, bf16[144,256]{1,0:T(8,128)(2,1)S(1)}, u32[]{:S(2)}, u32[]{:S(2)}) collective-permute-start(bf16[144,256]{1,0:T(8,128)(2,1)S(1)} %get-tuple-element.64), channel_id=1, source_target_pairs={{1,0},{2,1},{3,2},{0,3},{5,4},{6,5},{7,6},{4,7},{9,8},{10,9},{11,1... | collective-permute-start | bytes 221192 | tf_op jit(solution)/shard_map/ppermute | solution.py:229
  42.3 39.2 %all-to-all-start.1 = ((bf16[32,64,256]{2,1,0:T(8,128)(2,1)}), bf16[32,64,256]{2,1,0:T(8,128)(2,1)S(1)}, u32[]{:S(2)}, u32[]{:S(2)}) async-start(bf16[32,64,256]{2,1,0:T(8,128)(2,1)} %bitcast.21), calls=%async_computation.1 | async-start | bytes 2097152 | tf_op jit(solution)/shard_map/all_to_all | solution.py:602
  62.1 3.0 %collective-permute-start.4 = (f32[2432,128]{1,0:T(8,128)S(1)}, f32[2432,128]{1,0:T(8,128)S(1)}, u32[]{:S(2)}, u32[]{:S(2)}) collective-permute-start(f32[2432,128]{1,0:T(8,128)S(1)} %get-tuple-element.71), channel_id=1, source_target_pairs={{0,1},{1,0},{2,3},{3,2},{4,5},{5,4},{6,7},{7,6},{8,9},{9,8},{10,11... | collective-permute-start | bytes 3735560 | tf_op jit(solution)/shard_map/ppermute | solution.py:429
  65.4 9.2 %collective-permute-start.14 = (bf16[32,256]{1,0:T(8,128)(2,1)S(1)}, bf16[32,256]{1,0:T(8,128)(2,1)S(1)}, u32[]{:S(2)}, u32[]{:S(2)}) collective-permute-start(bf16[32,256]{1,0:T(8,128)(2,1)S(1)} %get-tuple-element.97), channel_id=1, source_target_pairs={{0,4},{4,8},{8,12},{12,16},{16,20},{20,24},{24,28},{28,0},{1,5},{5... | collective-permute-start | bytes 49160 | tf_op jit(solution)/shard_map/ppermute | solution.py:213
  67.0 7.6 %collective-permute-start.15 = (bf16[32,256]{1,0:T(8,128)(2,1)S(1)}, bf16[32,256]{1,0:T(8,128)(2,1)S(1)}, u32[]{:S(2)}, u32[]{:S(2)}) collective-permute-start(bf16[32,256]{1,0:T(8,128)(2,1)S(1)} %get-tuple-element.98), channel_id=1, source_target_pairs={{4,0},{8,4},{12,8},{16,12},{20,16},{24,20},{28,24},{0,28},{5,1},{9... | collective-permute-start | bytes 49160 | tf_op jit(solution)/shard_map/ppermute | solution.py:213
  71.0 5.9 %collective-permute-start.5 = (bf16[608,128]{1,0:T(8,128)(2,1)S(1)}, bf16[608,128]{1,0:T(8,128)(2,1)S(1)}, u32[]{:S(2)}, u32[]{:S(2)}) collective-permute-start(bf16[608,128]{1,0:T(8,128)(2,1)S(1)} %get-tuple-element.78), channel_id=1, source_target_pairs={{0,2},{1,3},{2,0},{3,1},{4,6},{5,7},{6,4},{7,5},{8,10},{9,11},{10,... | collective-permute-start | bytes 466952 | tf_op jit(solution)/shard_map/ppermute | solution.py:429
  72.7 6.9 %collective-permute-start.6 = (bf16[608,128]{1,0:T(8,128)(2,1)S(1)}, bf16[608,128]{1,0:T(8,128)(2,1)S(1)}, u32[]{:S(2)}, u32[]{:S(2)}) collective-permute-start(bf16[608,128]{1,0:T(8,128)(2,1)S(1)} %get-tuple-element.79), channel_id=1, source_target_pairs={{0,4},{1,5},{2,6},{3,7},{4,0},{5,1},{6,2},{7,3},{8,12},{9,13},{10,... | collective-permute-start | bytes 466952 | tf_op jit(solution)/shard_map/ppermute | solution.py:429
  72.7 8.9 %collective-permute-start.7 = (bf16[608,128]{1,0:T(8,128)(2,1)S(1)}, bf16[608,128]{1,0:T(8,128)(2,1)S(1)}, u32[]{:S(2)}, u32[]{:S(2)}) collective-permute-start(bf16[608,128]{1,0:T(8,128)(2,1)S(1)} %get-tuple-element.80), channel_id=1, source_target_pairs={{0,6},{1,7},{2,4},{3,5},{4,2},{5,3},{6,0},{7,1},{8,14},{9,15},{10,... | collective-permute-start | bytes 466952 | tf_op jit(solution)/shard_map/ppermute | solution.py:429
  74.7 18.4 %collective-permute-start.17 = (bf16[144,256]{1,0:T(8,128)(2,1)S(1)}, bf16[144,256]{1,0:T(8,128)(2,1)S(1)}, u32[]{:S(2)}, u32[]{:S(2)}) collective-permute-start(bf16[144,256]{1,0:T(8,128)(2,1)S(1)} %pad_maximum_fusion.1), channel_id=1, source_target_pairs={{1,0},{2,1},{3,2},{0,3},{5,4},{6,5},{7,6},{4,7},{9,8},{10,9},{11,1... | collective-permute-start | bytes 221192 | tf_op jit(solution)/shard_map/ppermute | solution.py:229
  74.8 18.3 %collective-permute-start.16 = (bf16[144,256]{1,0:T(8,128)(2,1)S(1)}, bf16[144,256]{1,0:T(8,128)(2,1)S(1)}, u32[]{:S(2)}, u32[]{:S(2)}) collective-permute-start(bf16[144,256]{1,0:T(8,128)(2,1)S(1)} %fusion.8), channel_id=1, source_target_pairs={{0,1},{1,2},{2,3},{3,0},{4,5},{5,6},{6,7},{7,4},{8,9},{9,10},{10,1... | collective-permute-start | bytes 221192 | tf_op jit(solution)/shard_map/ppermute | solution.py:229
  81.6 6.8 %collective-permute-start.10 = (bf16[152,128]{1,0:T(8,128)(2,1)S(1)}, bf16[152,128]{1,0:T(8,128)(2,1)S(1)}, u32[]{:S(2)}, u32[]{:S(2)}) collective-permute-start(bf16[152,128]{1,0:T(8,128)(2,1)S(1)} %get-tuple-element.89), channel_id=1, source_target_pairs={{0,24},{1,25},{2,26},{3,27},{4,28},{5,29},{6,30},{7,31},{8,16},{9,... | collective-permute-start | bytes 116744 | tf_op jit(solution)/shard_map/ppermute | solution.py:429
  83.0 5.5 %collective-permute-start.8 = (bf16[152,128]{1,0:T(8,128)(2,1)S(1)}, bf16[152,128]{1,0:T(8,128)(2,1)S(1)}, u32[]{:S(2)}, u32[]{:S(2)}) collective-permute-start(bf16[152,128]{1,0:T(8,128)(2,1)S(1)} %get-tuple-element.87), channel_id=1, source_target_pairs={{0,8},{1,9},{2,10},{3,11},{4,12},{5,13},{6,14},{7,15},{8,0},{9,1},... | collective-permute-start | bytes 116744 | tf_op jit(solution)/shard_map/ppermute | solution.py:429
  83.7 4.9 %collective-permute-start.9 = (bf16[152,128]{1,0:T(8,128)(2,1)S(1)}, bf16[152,128]{1,0:T(8,128)(2,1)S(1)}, u32[]{:S(2)}, u32[]{:S(2)}) collective-permute-start(bf16[152,128]{1,0:T(8,128)(2,1)S(1)} %get-tuple-element.88), channel_id=1, source_target_pairs={{0,16},{1,17},{2,18},{3,19},{4,20},{5,21},{6,22},{7,23},{8,24},{9,... | collective-permute-start | bytes 116744 | tf_op jit(solution)/shard_map/ppermute | solution.py:429
  88.6 10.2 %collective-permute-start.11 = (bf16[152,128]{1,0:T(8,128)(2,1)S(1)}, bf16[152,128]{1,0:T(8,128)(2,1)S(1)}, u32[]{:S(2)}, u32[]{:S(2)}) collective-permute-start(bf16[152,128]{1,0:T(8,128)(2,1)S(1)} %shard_map.109.refs_0_), channel_id=1, source_target_pairs={{0,8},{1,9},{2,10},{3,11},{4,12},{5,13},{6,14},{7,15},{8,0},{9,1},... | collective-permute-start | bytes 116744 | tf_op jit(solution)/shard_map/ppermute | solution.py:429
  90.0 8.9 %collective-permute-start.12 = (bf16[152,128]{1,0:T(8,128)(2,1)S(1)}, bf16[152,128]{1,0:T(8,128)(2,1)S(1)}, u32[]{:S(2)}, u32[]{:S(2)}) collective-permute-start(bf16[152,128]{1,0:T(8,128)(2,1)S(1)} %shard_map.109.refs_0_), channel_id=1, source_target_pairs={{0,16},{1,17},{2,18},{3,19},{4,20},{5,21},{6,22},{7,23},{8,24},{9,... | collective-permute-start | bytes 116744 | tf_op jit(solution)/shard_map/ppermute | solution.py:429
  91.2 7.7 %collective-permute-start.13 = (bf16[152,128]{1,0:T(8,128)(2,1)S(1)}, bf16[152,128]{1,0:T(8,128)(2,1)S(1)}, u32[]{:S(2)}, u32[]{:S(2)}) collective-permute-start(bf16[152,128]{1,0:T(8,128)(2,1)S(1)} %shard_map.109.refs_0_), channel_id=1, source_target_pairs={{0,24},{1,25},{2,26},{3,27},{4,28},{5,29},{6,30},{7,31},{8,16},{9,... | collective-permute-start | bytes 116744 | tf_op jit(solution)/shard_map/ppermute | solution.py:429
  98.9 9.3 %collective-permute-start.18 = (bf16[608,128]{1,0:T(8,128)(2,1)S(1)}, bf16[608,128]{1,0:T(8,128)(2,1)S(1)}, u32[]{:S(2)}, u32[]{:S(2)}) collective-permute-start(bf16[608,128]{1,0:T(8,128)(2,1)S(1)} %shard_map.111.refs_0_), channel_id=1, source_target_pairs={{0,2},{1,3},{2,0},{3,1},{4,6},{5,7},{6,4},{7,5},{8,10},{9,11},{10,... | collective-permute-start | bytes 466952 | tf_op jit(solution)/shard_map/ppermute | solution.py:429
  100.1 8.1 %collective-permute-start.19 = (bf16[608,128]{1,0:T(8,128)(2,1)S(1)}, bf16[608,128]{1,0:T(8,128)(2,1)S(1)}, u32[]{:S(2)}, u32[]{:S(2)}) collective-permute-start(bf16[608,128]{1,0:T(8,128)(2,1)S(1)} %shard_map.111.refs_0_), channel_id=1, source_target_pairs={{0,4},{1,5},{2,6},{3,7},{4,0},{5,1},{6,2},{7,3},{8,12},{9,13},{10,... | collective-permute-start | bytes 466952 | tf_op jit(solution)/shard_map/ppermute | solution.py:429
  100.8 7.4 %collective-permute-start.20 = (bf16[608,128]{1,0:T(8,128)(2,1)S(1)}, bf16[608,128]{1,0:T(8,128)(2,1)S(1)}, u32[]{:S(2)}, u32[]{:S(2)}) collective-permute-start(bf16[608,128]{1,0:T(8,128)(2,1)S(1)} %shard_map.111.refs_0_), channel_id=1, source_target_pairs={{0,6},{1,7},{2,4},{3,5},{4,2},{5,3},{6,0},{7,1},{8,14},{9,15},{10,... | collective-permute-start | bytes 466952 | tf_op jit(solution)/shard_map/ppermute | solution.py:429
  108.3 2.1 %collective-permute-start.21 = (bf16[2432,128]{1,0:T(8,128)(2,1)S(1)}, bf16[2432,128]{1,0:T(8,128)(2,1)S(1)}, u32[]{:S(2)}, u32[]{:S(2)}) collective-permute-start(bf16[2432,128]{1,0:T(8,128)(2,1)S(1)} %shard_map.113.own_ref), channel_id=1, source_target_pairs={{0,1},{1,0},{2,3},{3,2},{4,5},{5,4},{6,7},{7,6},{8,9},{9,8},{10,11... | collective-permute-start | bytes 1867784 | tf_op jit(solution)/shard_map/ppermute | solution.py:429
  (3 other events, 33.3 us)

commit v4 on v3

--- a/solution.py
+++ b/solution.py
@@ -131,19 +131,22 @@
     if back:
         out_hbm, pad_hbm, grid_ref, w_ref, pad_ref, out_ref, left32, right32, in_sem, w_sem, out_sem, pad_sem = refs
     else:
-        out_hbm, grid_ref, pad_ref, out_ref, left32, right32, in_sem, out_sem = refs[-8:]
+        out_hbm, pad_ref, out_ref, left32, right32, out_sem = refs[-6:]
         w_ref = w_hbm
     rows, cols, width = out_ref.shape
-    held = grid_ref.shape[0]
     base = max(start - 1, 0)
+    held = min(start + rows + 1, total) - base
+    if not back:
+        grid_ref = grid_hbm.at[base : base + held]
     high = 8
     blocks = rows // high
     cuts = [*range(0, held - 1, high), held]
-    loads = [
-        begin(grid_hbm.at[base + i : base + j], grid_ref.at[i:j], in_sem.at[n])
-        for n, (i, j) in enumerate(zip(cuts[:-1], cuts[1:]))
-    ]
+    loads = []
     if back:
+        loads = [
+            begin(grid_hbm.at[base + i : base + j], grid_ref.at[i:j], in_sem.at[n])
+            for n, (i, j) in enumerate(zip(cuts[:-1], cuts[1:]))
+        ]
         load_w = begin(w_hbm, w_ref, w_sem)
     left32[...] = left_ref[...].astype(F32)
     right32[...] = right_ref[...].astype(F32)
@@ -177,6 +180,8 @@
     for load, i, j in zip(loads, cuts[:-1], cuts[1:]):
         load.wait()
         lax.fori_loop(i, j, fill, 0)
+    if not back:
+        lax.fori_loop(0, held, fill, 0)
     stores = []
     if back:
         stores += [begin(pad_ref.at[b], pad_hbm.at[b], pad_sem.at[b]) for b in range(3)]
@@ -238,19 +243,23 @@
     pad = (3, rows + 2, cols, width)
     blocks = rows // 8
     scratch = [
-        pltpu.VMEM((held, cols, width), BF),
         pltpu.VMEM(pad, BF),
         pltpu.VMEM((rows, cols, width), BF),
         pltpu.VMEM((total, width), F32),
         pltpu.VMEM((total, width), F32),
-        DMA((blocks + 1,)),
         DMA((blocks,)),
     ]
     if back:
         outs.append(shape(pad, BF))
-        scratch.insert(1, pltpu.VMEM(w.shape, BF))
-        scratch.insert(7, DMA)
-        scratch.append(DMA((3,)))
+        scratch = [
+            pltpu.VMEM((held, cols, width), BF),
+            pltpu.VMEM(w.shape, BF),
+            *scratch[:4],
+            DMA((blocks + 1,)),
+            DMA,
+            DMA((blocks,)),
+            DMA((3,)),
+        ]
     flops = 18 * rows * cols * width * width
     body = functools.partial(conv_body, back=back, start=start, total=total)
     at = lax.axis_index("lat")
@@ -261,7 +270,7 @@
         alias = {len(args): 0}
         args.append(into)
     return kernel_call(
-        body, outs, args, flops, scratch, smem=(0,), hbm=(1, 6 if back else 7), far=(0, 1), temp=8, alias=alias
+        body, outs, args, flops, scratch, smem=(0,), hbm=(1, 6) if back else (7,), far=(0, 1), temp=8, alias=alias
     )
 
 
@@ -291,7 +300,7 @@
 
 def gather_body(
     recv_ref, dfield_hbm, w_ref, grad_hbm, eg_hbm, embed_hbm, code_hbm,
-    dfield_ref, grad_ref, eg_ref, embed_ref, code_ref, slope_ref, in_sem, grad_sem, out_sem, *, slots,
+    dfield_ref, grad_ref, eg_ref, embed_ref, code_ref, column_ref, slope_ref, in_sem, grad_sem, out_sem, *, slots,
 ):
     owners = recv_ref.shape[0]
     cells = dfield_ref.shape[0]
@@ -305,29 +314,43 @@
     def features(blk):
         return jnp.concatenate([recv_ref[blk * group + q, :slots, :] for q in range(group)], axis=0)
 
-    for blk in range(blocks):
-        at = slice(blk * size, (blk + 1) * size)
+    codes = code_ref[...].T.astype(I32)
+    for p in range(codes.shape[1]):
+        column_ref[p * 128 : (p + 1) * 128, :] = codes[:, p : p + 1]
+
+    def activate(blk, carry):
+        at = pl.ds(pl.multiple_of(blk * size, size), size)
         value, slope = gelu_parts(dot(features(blk), w_ref[...]))
         embed_ref[at, :] = value.astype(BF)
         slope_ref[at, :] = slope
+        return carry
+
+    lax.fori_loop(0, blocks, activate, 0)
     stores.append(begin(embed_ref, embed_hbm, out_sem.at[1]))
-    codes = code_ref[...].T.astype(I32)
-    total = jnp.zeros(eg_ref.shape, F32)
+    eg_ref[...] = jnp.zeros_like(eg_ref)
     load.wait()
-    for blk in range(blocks):
-        at = slice(blk * size, (blk + 1) * size)
-        code = jnp.concatenate([codes[:, blk * 4 + q : blk * 4 + q + 1] for q in range(4)], axis=0)
-        mask = (iota((size, cells), 1) == code).astype(BF)
+
+    def store(blk):
+        at = pl.ds(pl.multiple_of(blk * size, size), size)
+        return pltpu.make_async_copy(grad_ref.at[at], grad_hbm.at[at], grad_sem.at[blk])
+
+    def pick(blk, carry):
+        at = pl.ds(pl.multiple_of(blk * size, size), size)
+        mask = (iota((size, cells), 1) == column_ref[at, :]).astype(BF)
         rows = dot(mask, dfield_ref[...]).astype(BF)
         grad_ref[at, :] = rows
-        stores.append(begin(grad_ref.at[at], grad_hbm.at[at], grad_sem.at[blk]))
+        store(blk).start()
         dh = rows.astype(F32) * slope_ref[at, :]
         part = dh.astype(BF)
         rest = (dh - part.astype(F32)).astype(BF)
         feat = features(blk)
-        total = total + dot(feat, part, 0, 0) + dot(feat, rest, 0, 0)
-    eg_ref[...] = total
+        eg_ref[...] += dot(feat, part, 0, 0) + dot(feat, rest, 0, 0)
+        return carry
+
+    lax.fori_loop(0, blocks, pick, 0)
     stores.append(begin(eg_ref, eg_hbm, out_sem.at[2]))
+    for blk in range(blocks):
+        store(blk).wait()
     for move in stores:
         move.wait()
 
@@ -510,9 +533,9 @@
             halo = halo_of(edges)
         terms = [own] + [swap(x, m * bits[0]) for m, x in zip(moves, send)]
         if bits is plan[0]:
-            terms, back = lax.optimization_barrier((terms, beside[0]))
+            terms, gone = lax.optimization_barrier((terms, unroute(beside[0])))
         if bits is plan[-1]:
-            terms, gone = lax.optimization_barrier((terms, unroute(back)))
+            terms, found = lax.optimization_barrier((terms, encode(halo, 0, None)))
     body = functools.partial(split_body, moves=[], parts=1)
     (block,) = kernel_call(
         body, [shape(terms[0].shape, BF)], (jnp.zeros((1,), I32), *terms), smem=(0,)
@@ -522,9 +545,9 @@
         mine = (me // bits[0]) % ways
         pieces = [block] + [swap(block, m * bits[0]) for m in range(1, ways)]
         if bits is plan[-1]:
-            pieces, found = lax.optimization_barrier((pieces, encode(halo, 0, None)))
+            pieces, found = lax.optimization_barrier((pieces, encode(halo, 1, found)))
         if bits is plan[0]:
-            pieces, found = lax.optimization_barrier((pieces, encode(halo, 1, found)))
+            pieces, found = lax.optimization_barrier((pieces, encode(halo, 2, found)))
         rows = block.shape[0]
         body = functools.partial(join_body, parts=parts)
         (block,) = kernel_call(body, [shape((rows * ways, half), BF)], (mine, *pieces), smem=(0,))
@@ -587,6 +610,7 @@
             pltpu.VMEM((inputs, width), F32),
             pltpu.VMEM((count, width), BF),
             pltpu.VMEM((count // 128, 128), F32),
+            pltpu.VMEM((count, 1), I32),
             pltpu.VMEM((count, width), F32),
             DMA,
             DMA((count // 512,)),
@@ -634,8 +658,8 @@
         return (*sides, *end_edges(*end_rows(grid, *sides)))
 
     def encode(halo, part, into):
-        half = rows // 2
-        return conv(grid, halo, w_conv, False, part * half, (part + 1) * half, into)[0]
+        cuts = (0, rows // 4, rows // 2, rows)
+        return conv(grid, halo, w_conv, False, cuts[part], cuts[part + 1], into)[0]
 
     def unroute(back):
         return kernel_call(

time: 112 us -> 111 us (level)
  waiting for transfers between devices: 16.9 us -> 13.5 us
  Pallas kernels: 51.8 us -> 53.9 us
  other arithmetic: 0.25 us -> 1.52 us
    ppermute x14, waiting for transfers between devices: 11.2 us -> 7.87 us  [swap(): return lax.ppermute(x, AXES, [(i, i ^ bit) for i in range(count)])]
    pallas_call x13 -> x14, Pallas kernels: 51.8 us -> 53.9 us  [kernel_call(): pl.pallas_call(body, out_shape=[pltpu.HBM(o.shape, o.dtype) if i in far e...]
    concatenate x3, other arithmetic: 0.03 us -> 1.29 us  [row(): jnp.concatenate([grid[i], jnp.pad(left[i][None], pad), jnp.pad(right[i][N...]
  transfers between devices with their start and end apart: 24 -> 24, of which waited for: 9 -> 7; matrix products, arithmetic and copies ran while one was open for 2% -> 2% of each run, Pallas kernels for 36% -> 38%
where the time goes in v4:
time: 111 us
  Pallas kernels  53.9 us (49%)
  starting transfers between devices  39.1 us (35%)
  waiting for transfers between devices  13.5 us (12%)
  local copies, waits for them, and re-layouts  1.99 us (2%)
  other arithmetic  1.52 us (1%)
    pallas_call x14, Pallas kernels, kernel_call(): pl.pallas_call(body, out_shape=[pltpu.HBM(o.shape, o.dtype) if i in far e...  53.9 us
    ppermute x14, starting transfers between devices, swap(): return lax.ppermute(x, AXES, [(i, i ^ bit) for i in range(count)])  16.4 us
    ppermute x4, starting transfers between devices, side_edges(): return (lax.ppermute(last, 'lon', up), lax.ppermute(first, 'lon', down))  10.8 us
    ppermute x14, waiting for transfers between devices, swap(): return lax.ppermute(x, AXES, [(i, i ^ bit) for i in range(count)])  7.87 us
    all_to_all x1, starting transfers between devices, on_device(): lax.all_to_all(grad.reshape(owners, slots, width), AXES, split_axis=0, co...  5.99 us
    ppermute x4, waiting for transfers between devices, end_edges(): return (lax.ppermute(last, 'lat', up), lax.ppermute(first, 'lat', down))  5.52 us
    all_to_all x1, starting transfers between devices, on_device(): recv = lax.all_to_all(send, AXES, split_axis=0, concat_axis=0, tiled=True)  3.59 us
    ppermute x4, starting transfers between devices, end_edges(): return (lax.ppermute(last, 'lat', up), lax.ppermute(first, 'lat', down))  2.31 us
  transfers between devices with their start and end apart: 24, of which 7 were waited for; matrix products, arithmetic and copies ran while one was open for 2% of the time, Pallas kernels for 38%

profile of v4, /device:TPU:0, one launch (start us, length us, event | category | flops | bytes accessed | tf_op | source)
XLA Modules:
  0.0 111.0 jit_solution(7082206583370962348)
XLA Ops:
  1.7 3.0 %collective-permute-start = (bf16[32,256]{1,0:T(8,128)(2,1)S(1)}, bf16[32,256]{1,0:T(8,128)(2,1)S(1)}, u32[]{:S(2)}, u32[]{:S(2)}) collective-permute-start(bf16[32,256]{1,0:T(8,128)(2,1)S(1)} %bitcast.25), channel_id=1, source_target_pairs={{0,4},{4,8},{8,12},{12,16},{16,20},{20,24},{24,28},{28,0},{1,5},{5... | collective-permute-start | bytes 49160 | tf_op jit(solution)/shard_map/ppermute | solution.py:218
  4.7 3.1 %collective-permute-start.1 = (bf16[32,256]{1,0:T(8,128)(2,1)S(1)}, bf16[32,256]{1,0:T(8,128)(2,1)S(1)}, u32[]{:S(2)}, u32[]{:S(2)}) collective-permute-start(bf16[32,256]{1,0:T(8,128)(2,1)S(1)} %bitcast.26), channel_id=1, source_target_pairs={{4,0},{8,4},{12,8},{16,12},{20,16},{24,20},{28,24},{0,28},{5,1},{9... | collective-permute-start | bytes 49160 | tf_op jit(solution)/shard_map/ppermute | solution.py:218
  8.7 3.4 %shard_map.102 = (bf16[32,72,128]{2,1,0:T(8,128)(2,1)}, s32[1,1024]{1,0:T(1,128)S(1)}) custom-call(s32[1]{0:T(128)} %bitcast.me_ref, s32[1,1024]{1,0:T(1,128)} %bitcast.28, s32[1,1024]{1,0:T(1,128)} %bitcast.29, bf16[1024,128]{1,0:T(8,128)(2,1)} %feat_hbm.1), custom_call_target="tpu_custom_call" | custom-call | flops 536870912 | bytes 864260 | tf_op jit(solution)/shard_map/pallas_call | solution.py:35
  12.2 3.6 %all-to-all-start = ((bf16[32,72,128]{2,1,0:T(8,128)(2,1)}), bf16[32,72,128]{2,1,0:T(8,128)(2,1)S(1)}, u32[]{:S(2)}, u32[]{:S(2)}) async-start(bf16[32,72,128]{2,1,0:T(8,128)(2,1)} %get-tuple-element.62), calls=%async_computation | async-start | bytes 1179648 | tf_op jit(solution)/shard_map/all_to_all | solution.py:592
  17.7 3.9 %collective-permute-done.2.top_ref = bf16[144,256]{1,0:T(8,128)(2,1)S(1)} collective-permute-done((bf16[144,256]{1,0:T(8,128)(2,1)S(1)}, bf16[144,256]{1,0:T(8,128)(2,1)S(1)}, u32[]{:S(2)}, u32[]{:S(2)}) %collective-permute-start.2) | collective-permute-done | bytes 73760 | tf_op jit(solution)/shard_map/ppermute | solution.py:234
  23.2 9.2 %shard_map.103 = (bf16[32,128,256]{2,1,0:T(8,128)(2,1)}, bf16[3,34,128,256]{3,2,1,0:T(8,128)(2,1)}) custom-call(s32[2]{0:T(128)S(1)} %add_convert_fusion.inside_ref, bf16[32,128,256]{2,1,0:T(8,128)(2,1)} %grid_hbm.1, bf16[32,256]{1,0:T(8,128)(2,1)S(1)} %collective-permute-done.left_ref, bf16[32,256]{1,0:T(8,128)(2,1)S(1)} %collective-permute-done.1.right_ref, ...), custom_call_target="tpu_custom_call" | custom-call | flops 4831838208 | bytes 12238856 | tf_op jit(solution)/shard_map/pallas_call | solution.py:35
  32.5 9.4 %shard_map.104 = (bf16[2048,256]{1,0:T(8,128)(2,1)}, f32[128,256]{1,0:T(8,128)}, bf16[2048,256]{1,0:T(8,128)(2,1)}, f32[16,128]{1,0:T(8,128)}) custom-call(bf16[32,72,128]{2,1,0:T(8,128)(2,1)S(1)} %all-to-all-done.recv_ref, bf16[4096,256]{1,0:T(8,128)(2,1)} %bitcast.30, bf16[128,256]{1,0:T(8,128)(2,1)S(1)} %copy-done.4), custom_call_target="tpu_custom_call" | custom-call | flops 4294967296 | bytes 4988928 | tf_op jit(solution)/shard_map/pallas_call | solution.py:35
  42.0 6.0 %all-to-all-start.1 = ((bf16[32,64,256]{2,1,0:T(8,128)(2,1)}), bf16[32,64,256]{2,1,0:T(8,128)(2,1)S(1)}, u32[]{:S(2)}, u32[]{:S(2)}) async-start(bf16[32,64,256]{2,1,0:T(8,128)(2,1)} %bitcast.24), calls=%async_computation.1 | async-start | bytes 2097152 | tf_op jit(solution)/shard_map/all_to_all | solution.py:626
  48.0 13.6 %shard_map.105 = (bf16[4096,256]{1,0:T(8,128)(2,1)}, f32[2432,128]{1,0:T(8,128)S(1)}, f32[2432,128]{1,0:T(8,128)S(1)}, bf16[32,256]{1,0:T(8,128)(2,1)S(1)}, bf16[32,256]{1,0:T(8,128)(2,1)S(1)}) custom-call(s32[1]{0:T(128)} %bitcast.me_ref, f32[16,128]{1,0:T(8,128)} %get-tuple-element.66.code_hbm, bf16[2048,256]{1,0:T(8,128)(2,1)} %get-tuple-element.67.embed_hbm, ...), custom_call_target="tpu_custom_call" | custom-call | flops 9126805504 | bytes 14589956 | tf_op jit(solution)/shard_map/pallas_call | solution.py:35
  61.9 2.7 %collective-permute-done.4.refs_1_ = f32[2432,128]{1,0:T(8,128)S(1)} collective-permute-done((f32[2432,128]{1,0:T(8,128)S(1)}, f32[2432,128]{1,0:T(8,128)S(1)}, u32[]{:S(2)}, u32[]{:S(2)}) %collective-permute-start.4) | collective-permute-done | bytes 1245216 | tf_op jit(solution)/shard_map/ppermute | solution.py:452
  65.6 1.8 %collective-permute-start.11 = (bf16[32,256]{1,0:T(8,128)(2,1)S(1)}, bf16[32,256]{1,0:T(8,128)(2,1)S(1)}, u32[]{:S(2)}, u32[]{:S(2)}) collective-permute-start(bf16[32,256]{1,0:T(8,128)(2,1)S(1)} %get-tuple-element.92), channel_id=1, source_target_pairs={{0,4},{4,8},{8,12},{12,16},{16,20},{20,24},{24,28},{28,0},{1,5},{5... | collective-permute-start | bytes 49160 | tf_op jit(solution)/shard_map/ppermute | solution.py:218
  67.3 3.0 %collective-permute-start.12 = (bf16[32,256]{1,0:T(8,128)(2,1)S(1)}, bf16[32,256]{1,0:T(8,128)(2,1)S(1)}, u32[]{:S(2)}, u32[]{:S(2)}) collective-permute-start(bf16[32,256]{1,0:T(8,128)(2,1)S(1)} %get-tuple-element.93), channel_id=1, source_target_pairs={{4,0},{8,4},{12,8},{16,12},{20,16},{24,20},{28,24},{0,28},{5,1},{9... | collective-permute-start | bytes 49160 | tf_op jit(solution)/shard_map/ppermute | solution.py:218
  70.3 1.8 %collective-permute-start.5 = (bf16[608,128]{1,0:T(8,128)(2,1)}, bf16[608,128]{1,0:T(8,128)(2,1)}, u32[]{:S(2)}, u32[]{:S(2)}) collective-permute-start(bf16[608,128]{1,0:T(8,128)(2,1)} %get-tuple-element.78), channel_id=1, source_target_pairs={{0,2},{1,3},{2,0},{3,1},{4,6},{5,7},{6,4},{7,5},{8,10},{9,11},{10,... | collective-permute-start | bytes 466952 | tf_op jit(solution)/shard_map/ppermute | solution.py:452
  72.2 1.7 %collective-permute-start.7 = (bf16[608,128]{1,0:T(8,128)(2,1)}, bf16[608,128]{1,0:T(8,128)(2,1)}, u32[]{:S(2)}, u32[]{:S(2)}) collective-permute-start(bf16[608,128]{1,0:T(8,128)(2,1)} %get-tuple-element.80), channel_id=1, source_target_pairs={{0,6},{1,7},{2,4},{3,5},{4,2},{5,3},{6,0},{7,1},{8,14},{9,15},{10,... | collective-permute-start | bytes 466952 | tf_op jit(solution)/shard_map/ppermute | solution.py:452
  75.8 2.4 %shard_map.107 = bf16[1024,256]{1,0:T(8,128)(2,1)} custom-call(s32[1,1024]{1,0:T(1,128)S(1)} %get-tuple-element.81.place_ref, bf16[2048,256]{1,0:T(8,128)(2,1)S(1)} %bitcast.23), custom_call_target="tpu_custom_call" | custom-call | flops 1073741824 | bytes 1576960 | tf_op jit(solution)/shard_map/pallas_call | solution.py:35
  79.4 1.9 %collective-permute-done.7.refs_3_ = bf16[608,128]{1,0:T(8,128)(2,1)} collective-permute-done((bf16[608,128]{1,0:T(8,128)(2,1)}, bf16[608,128]{1,0:T(8,128)(2,1)}, u32[]{:S(2)}, u32[]{:S(2)}) %collective-permute-start.7) | collective-permute-done | bytes 155680 | tf_op jit(solution)/shard_map/ppermute | solution.py:452
  84.6 2.3 %collective-permute-start.9 = (bf16[152,128]{1,0:T(8,128)(2,1)S(1)}, bf16[152,128]{1,0:T(8,128)(2,1)S(1)}, u32[]{:S(2)}, u32[]{:S(2)}) collective-permute-start(bf16[152,128]{1,0:T(8,128)(2,1)S(1)} %get-tuple-element.89), channel_id=1, source_target_pairs={{0,16},{1,17},{2,18},{3,19},{4,20},{5,21},{6,22},{7,23},{8,24},{9,... | collective-permute-start | bytes 116744 | tf_op jit(solution)/shard_map/ppermute | solution.py:452
  86.9 3.6 %shard_map.109.refs_0_ = bf16[32,128,256]{2,1,0:T(8,128)(2,1)} custom-call(s32[2]{0:T(128)S(1)} %add_convert_fusion.inside_ref, bf16[32,128,256]{2,1,0:T(8,128)(2,1)S(1)} %bitcast.20, bf16[32,256]{1,0:T(8,128)(2,1)S(1)} %collective-permute-done.11.left_ref, bf16[32,256]{1,0:T(8,128)(2,1)S(1)} %copy-done.3, bf16[144,256]{1,0:T(8,128)(2,1)} %collective-permute-done.13.top_ref, ...), custom_call_target="tpu_custom_call" | custom-call | flops 1207959552 | bytes 5554184 | tf_op jit(solution)/shard_map/pallas_call | solution.py:35
  90.8 1.7 %collective-permute-start.16 = (bf16[152,128]{1,0:T(8,128)(2,1)S(1)}, bf16[152,128]{1,0:T(8,128)(2,1)S(1)}, u32[]{:S(2)}, u32[]{:S(2)}) collective-permute-start(bf16[152,128]{1,0:T(8,128)(2,1)S(1)} %shard_map.110.refs_0_), channel_id=1, source_target_pairs={{0,16},{1,17},{2,18},{3,19},{4,20},{5,21},{6,22},{7,23},{8,24},{9,... | collective-permute-start | bytes 116744 | tf_op jit(solution)/shard_map/ppermute | solution.py:452
  92.5 2.5 %collective-permute-start.17 = (bf16[152,128]{1,0:T(8,128)(2,1)S(1)}, bf16[152,128]{1,0:T(8,128)(2,1)S(1)}, u32[]{:S(2)}, u32[]{:S(2)}) collective-permute-start(bf16[152,128]{1,0:T(8,128)(2,1)S(1)} %shard_map.110.refs_0_), channel_id=1, source_target_pairs={{0,24},{1,25},{2,26},{3,27},{4,28},{5,29},{6,30},{7,31},{8,16},{9,... | collective-permute-start | bytes 116744 | tf_op jit(solution)/shard_map/ppermute | solution.py:452
  95.0 3.4 %shard_map.111.refs_0_ = bf16[32,128,256]{2,1,0:T(8,128)(2,1)} custom-call(s32[2]{0:T(128)S(1)} %add_convert_fusion.inside_ref, bf16[32,128,256]{2,1,0:T(8,128)(2,1)S(1)} %bitcast.21, bf16[32,256]{1,0:T(8,128)(2,1)S(1)} %collective-permute-done.11.left_ref, bf16[32,256]{1,0:T(8,128)(2,1)S(1)} %copy-done.3, ...), custom_call_target="tpu_custom_call", output_to_operand_aliasing={{}: (7, {})} | custom-call | flops 1207959552 | bytes 7651336 | tf_op jit(solution)/shard_map/pallas_call | solution.py:35
  102.1 5.1 %shard_map.113 = bf16[32,128,256]{2,1,0:T(8,128)(2,1)} custom-call(s32[2]{0:T(128)S(1)} %add_convert_fusion.inside_ref, bf16[32,128,256]{2,1,0:T(8,128)(2,1)S(1)} %bitcast.22, bf16[32,256]{1,0:T(8,128)(2,1)S(1)} %collective-permute-done.11.left_ref, bf16[32,256]{1,0:T(8,128)(2,1)S(1)} %copy-done.3, ...), custom_call_target="tpu_custom_call", output_to_operand_aliasing={{}: (7, {})} | custom-call | flops 2415919104 | bytes 7651336 | tf_op jit(solution)/shard_map/pallas_call | solution.py:35
  107.3 2.0 %collective-permute-done.21.other_ref = bf16[2432,128]{1,0:T(8,128)(2,1)S(1)} collective-permute-done((bf16[2432,128]{1,0:T(8,128)(2,1)S(1)}, bf16[2432,128]{1,0:T(8,128)(2,1)S(1)}, u32[]{:S(2)}, u32[]{:S(2)}) %collective-permute-start.21) | collective-permute-done | bytes 622624 | tf_op jit(solution)/shard_map/ppermute | solution.py:452
  109.4 1.6 %shard_map.115 = (f32[9,256,256]{2,1,0:T(8,128)}, f32[128,256]{1,0:T(8,128)}) custom-call(s32[1]{0:T(128)S(6)} %select_n.33.mine_ref, bf16[2432,128]{1,0:T(8,128)(2,1)S(1)} %shard_map.114.own_ref, bf16[2432,128]{1,0:T(8,128)(2,1)S(1)} %collective-permute-done.21.other_ref), custom_call_target="tpu_custom_call" | custom-call | bytes 3735556 | tf_op jit(solution)/shard_map/pallas_call | solution.py:35
  (67 shorter events, 17.3 us)
Async XLA Ops:
  1.7 10.4 %collective-permute-start = (bf16[32,256]{1,0:T(8,128)(2,1)S(1)}, bf16[32,256]{1,0:T(8,128)(2,1)S(1)}, u32[]{:S(2)}, u32[]{:S(2)}) collective-permute-start(bf16[32,256]{1,0:T(8,128)(2,1)S(1)} %bitcast.25), channel_id=1, source_target_pairs={{0,4},{4,8},{8,12},{12,16},{16,20},{20,24},{24,28},{28,0},{1,5},{5... | collective-permute-start | bytes 49160 | tf_op jit(solution)/shard_map/ppermute | solution.py:218
  4.7 7.4 %collective-permute-start.1 = (bf16[32,256]{1,0:T(8,128)(2,1)S(1)}, bf16[32,256]{1,0:T(8,128)(2,1)S(1)}, u32[]{:S(2)}, u32[]{:S(2)}) collective-permute-start(bf16[32,256]{1,0:T(8,128)(2,1)S(1)} %bitcast.26), channel_id=1, source_target_pairs={{4,0},{8,4},{12,8},{16,12},{20,16},{24,20},{28,24},{0,28},{5,1},{9... | collective-permute-start | bytes 49160 | tf_op jit(solution)/shard_map/ppermute | solution.py:218
  12.2 20.3 %all-to-all-start = ((bf16[32,72,128]{2,1,0:T(8,128)(2,1)}), bf16[32,72,128]{2,1,0:T(8,128)(2,1)S(1)}, u32[]{:S(2)}, u32[]{:S(2)}) async-start(bf16[32,72,128]{2,1,0:T(8,128)(2,1)} %get-tuple-element.62), calls=%async_computation | async-start | bytes 1179648 | tf_op jit(solution)/shard_map/all_to_all | solution.py:592
  15.8 5.8 %collective-permute-start.2 = (bf16[144,256]{1,0:T(8,128)(2,1)S(1)}, bf16[144,256]{1,0:T(8,128)(2,1)S(1)}, u32[]{:S(2)}, u32[]{:S(2)}) collective-permute-start(bf16[144,256]{1,0:T(8,128)(2,1)S(1)} %get-tuple-element.63), channel_id=1, source_target_pairs={{0,1},{1,2},{2,3},{3,0},{4,5},{5,6},{6,7},{7,4},{8,9},{9,10},{10,1... | collective-permute-start | bytes 221192 | tf_op jit(solution)/shard_map/ppermute | solution.py:234
  16.1 7.1 %collective-permute-start.3 = (bf16[144,256]{1,0:T(8,128)(2,1)S(1)}, bf16[144,256]{1,0:T(8,128)(2,1)S(1)}, u32[]{:S(2)}, u32[]{:S(2)}) collective-permute-start(bf16[144,256]{1,0:T(8,128)(2,1)S(1)} %get-tuple-element.64), channel_id=1, source_target_pairs={{1,0},{2,1},{3,2},{0,3},{5,4},{6,5},{7,6},{4,7},{9,8},{10,9},{11,1... | collective-permute-start | bytes 221192 | tf_op jit(solution)/shard_map/ppermute | solution.py:234
  42.0 33.8 %all-to-all-start.1 = ((bf16[32,64,256]{2,1,0:T(8,128)(2,1)}), bf16[32,64,256]{2,1,0:T(8,128)(2,1)S(1)}, u32[]{:S(2)}, u32[]{:S(2)}) async-start(bf16[32,64,256]{2,1,0:T(8,128)(2,1)} %bitcast.24), calls=%async_computation.1 | async-start | bytes 2097152 | tf_op jit(solution)/shard_map/all_to_all | solution.py:626
  61.6 3.0 %collective-permute-start.4 = (f32[2432,128]{1,0:T(8,128)S(1)}, f32[2432,128]{1,0:T(8,128)S(1)}, u32[]{:S(2)}, u32[]{:S(2)}) collective-permute-start(f32[2432,128]{1,0:T(8,128)S(1)} %get-tuple-element.71), channel_id=1, source_target_pairs={{0,1},{1,0},{2,3},{3,2},{4,5},{5,4},{6,7},{7,6},{8,9},{9,8},{10,11... | collective-permute-start | bytes 3735560 | tf_op jit(solution)/shard_map/ppermute | solution.py:452
  65.6 8.3 %collective-permute-start.11 = (bf16[32,256]{1,0:T(8,128)(2,1)S(1)}, bf16[32,256]{1,0:T(8,128)(2,1)S(1)}, u32[]{:S(2)}, u32[]{:S(2)}) collective-permute-start(bf16[32,256]{1,0:T(8,128)(2,1)S(1)} %get-tuple-element.92), channel_id=1, source_target_pairs={{0,4},{4,8},{8,12},{12,16},{16,20},{20,24},{24,28},{28,0},{1,5},{5... | collective-permute-start | bytes 49160 | tf_op jit(solution)/shard_map/ppermute | solution.py:218
  67.3 6.5 %collective-permute-start.12 = (bf16[32,256]{1,0:T(8,128)(2,1)S(1)}, bf16[32,256]{1,0:T(8,128)(2,1)S(1)}, u32[]{:S(2)}, u32[]{:S(2)}) collective-permute-start(bf16[32,256]{1,0:T(8,128)(2,1)S(1)} %get-tuple-element.93), channel_id=1, source_target_pairs={{4,0},{8,4},{12,8},{16,12},{20,16},{24,20},{28,24},{0,28},{5,1},{9... | collective-permute-start | bytes 49160 | tf_op jit(solution)/shard_map/ppermute | solution.py:218
  70.3 7.9 %collective-permute-start.5 = (bf16[608,128]{1,0:T(8,128)(2,1)}, bf16[608,128]{1,0:T(8,128)(2,1)}, u32[]{:S(2)}, u32[]{:S(2)}) collective-permute-start(bf16[608,128]{1,0:T(8,128)(2,1)} %get-tuple-element.78), channel_id=1, source_target_pairs={{0,2},{1,3},{2,0},{3,1},{4,6},{5,7},{6,4},{7,5},{8,10},{9,11},{10,... | collective-permute-start | bytes 466952 | tf_op jit(solution)/shard_map/ppermute | solution.py:452
  72.2 7.2 %collective-permute-start.6 = (bf16[608,128]{1,0:T(8,128)(2,1)}, bf16[608,128]{1,0:T(8,128)(2,1)}, u32[]{:S(2)}, u32[]{:S(2)}) collective-permute-start(bf16[608,128]{1,0:T(8,128)(2,1)} %get-tuple-element.79), channel_id=1, source_target_pairs={{0,4},{1,5},{2,6},{3,7},{4,0},{5,1},{6,2},{7,3},{8,12},{9,13},{10,... | collective-permute-start | bytes 466952 | tf_op jit(solution)/shard_map/ppermute | solution.py:452
  72.2 9.1 %collective-permute-start.7 = (bf16[608,128]{1,0:T(8,128)(2,1)}, bf16[608,128]{1,0:T(8,128)(2,1)}, u32[]{:S(2)}, u32[]{:S(2)}) collective-permute-start(bf16[608,128]{1,0:T(8,128)(2,1)} %get-tuple-element.80), channel_id=1, source_target_pairs={{0,6},{1,7},{2,4},{3,5},{4,2},{5,3},{6,0},{7,1},{8,14},{9,15},{10,... | collective-permute-start | bytes 466952 | tf_op jit(solution)/shard_map/ppermute | solution.py:452
  74.6 12.3 %collective-permute-start.14 = (bf16[144,256]{1,0:T(8,128)(2,1)}, bf16[144,256]{1,0:T(8,128)(2,1)S(1)}, u32[]{:S(2)}, u32[]{:S(2)}) collective-permute-start(bf16[144,256]{1,0:T(8,128)(2,1)} %pad_maximum_fusion.1), channel_id=1, source_target_pairs={{1,0},{2,1},{3,2},{0,3},{5,4},{6,5},{7,6},{4,7},{9,8},{10,9},{11,1... | collective-permute-start | bytes 221192 | tf_op jit(solution)/shard_map/ppermute | solution.py:234
  75.4 11.5 %collective-permute-start.13 = (bf16[144,256]{1,0:T(8,128)(2,1)}, bf16[144,256]{1,0:T(8,128)(2,1)}, u32[]{:S(2)}, u32[]{:S(2)}) collective-permute-start(bf16[144,256]{1,0:T(8,128)(2,1)} %fusion.8), channel_id=1, source_target_pairs={{0,1},{1,2},{2,3},{3,0},{4,5},{5,6},{6,7},{7,4},{8,9},{9,10},{10,1... | collective-permute-start | bytes 221192 | tf_op jit(solution)/shard_map/ppermute | solution.py:234
  82.5 8.1 %collective-permute-start.10 = (bf16[152,128]{1,0:T(8,128)(2,1)S(1)}, bf16[152,128]{1,0:T(8,128)(2,1)S(1)}, u32[]{:S(2)}, u32[]{:S(2)}) collective-permute-start(bf16[152,128]{1,0:T(8,128)(2,1)S(1)} %get-tuple-element.90), channel_id=1, source_target_pairs={{0,24},{1,25},{2,26},{3,27},{4,28},{5,29},{6,30},{7,31},{8,16},{9,... | collective-permute-start | bytes 116744 | tf_op jit(solution)/shard_map/ppermute | solution.py:452
  83.8 6.7 %collective-permute-start.8 = (bf16[152,128]{1,0:T(8,128)(2,1)S(1)}, bf16[152,128]{1,0:T(8,128)(2,1)S(1)}, u32[]{:S(2)}, u32[]{:S(2)}) collective-permute-start(bf16[152,128]{1,0:T(8,128)(2,1)S(1)} %get-tuple-element.88), channel_id=1, source_target_pairs={{0,8},{1,9},{2,10},{3,11},{4,12},{5,13},{6,14},{7,15},{8,0},{9,1},... | collective-permute-start | bytes 116744 | tf_op jit(solution)/shard_map/ppermute | solution.py:452
  84.6 6.0 %collective-permute-start.9 = (bf16[152,128]{1,0:T(8,128)(2,1)S(1)}, bf16[152,128]{1,0:T(8,128)(2,1)S(1)}, u32[]{:S(2)}, u32[]{:S(2)}) collective-permute-start(bf16[152,128]{1,0:T(8,128)(2,1)S(1)} %get-tuple-element.89), channel_id=1, source_target_pairs={{0,16},{1,17},{2,18},{3,19},{4,20},{5,21},{6,22},{7,23},{8,24},{9,... | collective-permute-start | bytes 116744 | tf_op jit(solution)/shard_map/ppermute | solution.py:452
  90.6 7.9 %collective-permute-start.15 = (bf16[152,128]{1,0:T(8,128)(2,1)S(1)}, bf16[152,128]{1,0:T(8,128)(2,1)S(1)}, u32[]{:S(2)}, u32[]{:S(2)}) collective-permute-start(bf16[152,128]{1,0:T(8,128)(2,1)S(1)} %shard_map.110.refs_0_), channel_id=1, source_target_pairs={{0,8},{1,9},{2,10},{3,11},{4,12},{5,13},{6,14},{7,15},{8,0},{9,1},... | collective-permute-start | bytes 116744 | tf_op jit(solution)/shard_map/ppermute | solution.py:452
  90.8 7.6 %collective-permute-start.16 = (bf16[152,128]{1,0:T(8,128)(2,1)S(1)}, bf16[152,128]{1,0:T(8,128)(2,1)S(1)}, u32[]{:S(2)}, u32[]{:S(2)}) collective-permute-start(bf16[152,128]{1,0:T(8,128)(2,1)S(1)} %shard_map.110.refs_0_), channel_id=1, source_target_pairs={{0,16},{1,17},{2,18},{3,19},{4,20},{5,21},{6,22},{7,23},{8,24},{9,... | collective-permute-start | bytes 116744 | tf_op jit(solution)/shard_map/ppermute | solution.py:452
  92.5 6.0 %collective-permute-start.17 = (bf16[152,128]{1,0:T(8,128)(2,1)S(1)}, bf16[152,128]{1,0:T(8,128)(2,1)S(1)}, u32[]{:S(2)}, u32[]{:S(2)}) collective-permute-start(bf16[152,128]{1,0:T(8,128)(2,1)S(1)} %shard_map.110.refs_0_), channel_id=1, source_target_pairs={{0,24},{1,25},{2,26},{3,27},{4,28},{5,29},{6,30},{7,31},{8,16},{9,... | collective-permute-start | bytes 116744 | tf_op jit(solution)/shard_map/ppermute | solution.py:452
  98.5 8.6 %collective-permute-start.18 = (bf16[608,128]{1,0:T(8,128)(2,1)S(1)}, bf16[608,128]{1,0:T(8,128)(2,1)S(1)}, u32[]{:S(2)}, u32[]{:S(2)}) collective-permute-start(bf16[608,128]{1,0:T(8,128)(2,1)S(1)} %shard_map.112.refs_0_), channel_id=1, source_target_pairs={{0,2},{1,3},{2,0},{3,1},{4,6},{5,7},{6,4},{7,5},{8,10},{9,11},{10,... | collective-permute-start | bytes 466952 | tf_op jit(solution)/shard_map/ppermute | solution.py:452
  99.9 7.3 %collective-permute-start.19 = (bf16[608,128]{1,0:T(8,128)(2,1)S(1)}, bf16[608,128]{1,0:T(8,128)(2,1)S(1)}, u32[]{:S(2)}, u32[]{:S(2)}) collective-permute-start(bf16[608,128]{1,0:T(8,128)(2,1)S(1)} %shard_map.112.refs_0_), channel_id=1, source_target_pairs={{0,4},{1,5},{2,6},{3,7},{4,0},{5,1},{6,2},{7,3},{8,12},{9,13},{10,... | collective-permute-start | bytes 466952 | tf_op jit(solution)/shard_map/ppermute | solution.py:452
  100.8 6.4 %collective-permute-start.20 = (bf16[608,128]{1,0:T(8,128)(2,1)S(1)}, bf16[608,128]{1,0:T(8,128)(2,1)S(1)}, u32[]{:S(2)}, u32[]{:S(2)}) collective-permute-start(bf16[608,128]{1,0:T(8,128)(2,1)S(1)} %shard_map.112.refs_0_), channel_id=1, source_target_pairs={{0,6},{1,7},{2,4},{3,5},{4,2},{5,3},{6,0},{7,1},{8,14},{9,15},{10,... | collective-permute-start | bytes 466952 | tf_op jit(solution)/shard_map/ppermute | solution.py:452
  107.3 2.1 %collective-permute-start.21 = (bf16[2432,128]{1,0:T(8,128)(2,1)S(1)}, bf16[2432,128]{1,0:T(8,128)(2,1)S(1)}, u32[]{:S(2)}, u32[]{:S(2)}) collective-permute-start(bf16[2432,128]{1,0:T(8,128)(2,1)S(1)} %shard_map.114.own_ref), channel_id=1, source_target_pairs={{0,1},{1,0},{2,3},{3,2},{4,5},{5,4},{6,7},{7,6},{8,9},{9,8},{10,11... | collective-permute-start | bytes 1867784 | tf_op jit(solution)/shard_map/ppermute | solution.py:452
  (7 other events, 71.1 us)

commit v5 on v4

--- a/solution.py
+++ b/solution.py
@@ -533,9 +533,9 @@
             halo = halo_of(edges)
         terms = [own] + [swap(x, m * bits[0]) for m, x in zip(moves, send)]
         if bits is plan[0]:
-            terms, gone = lax.optimization_barrier((terms, unroute(beside[0])))
+            terms, back = lax.optimization_barrier((terms, beside[0]))
         if bits is plan[-1]:
-            terms, found = lax.optimization_barrier((terms, encode(halo, 0, None)))
+            terms, gone = lax.optimization_barrier((terms, unroute(back)))
     body = functools.partial(split_body, moves=[], parts=1)
     (block,) = kernel_call(
         body, [shape(terms[0].shape, BF)], (jnp.zeros((1,), I32), *terms), smem=(0,)
@@ -545,9 +545,9 @@
         mine = (me // bits[0]) % ways
         pieces = [block] + [swap(block, m * bits[0]) for m in range(1, ways)]
         if bits is plan[-1]:
+            pieces, found = lax.optimization_barrier((pieces, encode(halo, 0, None)))
+        if bits is plan[0]:
             pieces, found = lax.optimization_barrier((pieces, encode(halo, 1, found)))
-        if bits is plan[0]:
-            pieces, found = lax.optimization_barrier((pieces, encode(halo, 2, found)))
         rows = block.shape[0]
         body = functools.partial(join_body, parts=parts)
         (block,) = kernel_call(body, [shape((rows * ways, half), BF)], (mine, *pieces), smem=(0,))
@@ -658,7 +658,7 @@
         return (*sides, *end_edges(*end_rows(grid, *sides)))
 
     def encode(halo, part, into):
-        cuts = (0, rows // 4, rows // 2, rows)
+        cuts = (0, rows // 2, rows)
         return conv(grid, halo, w_conv, False, cuts[part], cuts[part + 1], into)[0]
 
     def unroute(back):

time: 111 us -> 110 us (level)
  Pallas kernels: 53.9 us -> 49.4 us
  waiting for transfers between devices: 13.5 us -> 17 us
  other arithmetic: 1.52 us -> 0.25 us
    pallas_call x14 -> x13, Pallas kernels: 53.9 us -> 49.4 us  [kernel_call(): pl.pallas_call(body, out_shape=[pltpu.HBM(o.shape, o.dtype) if i in far e...]
    ppermute x14, waiting for transfers between devices: 7.87 us -> 11.4 us  [swap(): return lax.ppermute(x, AXES, [(i, i ^ bit) for i in range(count)])]
    concatenate x3, other arithmetic: 1.29 us -> 0.03 us  [row(): jnp.concatenate([grid[i], jnp.pad(left[i][None], pad), jnp.pad(right[i][N...]
  transfers between devices with their start and end apart: 24 -> 24, of which waited for: 7 -> 10; matrix products, arithmetic and copies ran while one was open for 2% -> 2% of each run, Pallas kernels for 38% -> 35%
where the time goes in v5:
time: 110 us
  Pallas kernels  49.4 us (45%)
  starting transfers between devices  39.3 us (36%)
  waiting for transfers between devices  17 us (15%)
  local copies, waits for them, and re-layouts  2.84 us (3%)
    pallas_call x13, Pallas kernels, kernel_call(): pl.pallas_call(body, out_shape=[pltpu.HBM(o.shape, o.dtype) if i in far e...  49.4 us
    ppermute x14, starting transfers between devices, swap(): return lax.ppermute(x, AXES, [(i, i ^ bit) for i in range(count)])  16.4 us
    ppermute x14, waiting for transfers between devices, swap(): return lax.ppermute(x, AXES, [(i, i ^ bit) for i in range(count)])  11.4 us
    ppermute x4, starting transfers between devices, side_edges(): return (lax.ppermute(last, 'lon', up), lax.ppermute(first, 'lon', down))  10.9 us
    all_to_all x1, starting transfers between devices, on_device(): lax.all_to_all(grad.reshape(owners, slots, width), AXES, split_axis=0, co...  5.99 us
    ppermute x4, waiting for transfers between devices, end_edges(): return (lax.ppermute(last, 'lat', up), lax.ppermute(first, 'lat', down))  5.52 us
    all_to_all x1, starting transfers between devices, on_device(): recv = lax.all_to_all(send, AXES, split_axis=0, concat_axis=0, tiled=True)  3.6 us
    ppermute x4, starting transfers between devices, end_edges(): return (lax.ppermute(last, 'lat', up), lax.ppermute(first, 'lat', down))  2.41 us
  transfers between devices with their start and end apart: 24, of which 10 were waited for; matrix products, arithmetic and copies ran while one was open for 2% of the time, Pallas kernels for 35%

profile of v5, /device:TPU:0, one launch (start us, length us, event | category | flops | bytes accessed | tf_op | source)
XLA Modules:
  0.0 109.7 jit_solution(9087315495856478722)
XLA Ops:
  1.7 3.0 %collective-permute-start = (bf16[32,256]{1,0:T(8,128)(2,1)S(1)}, bf16[32,256]{1,0:T(8,128)(2,1)S(1)}, u32[]{:S(2)}, u32[]{:S(2)}) collective-permute-start(bf16[32,256]{1,0:T(8,128)(2,1)S(1)} %bitcast.24), channel_id=1, source_target_pairs={{0,4},{4,8},{8,12},{12,16},{16,20},{20,24},{24,28},{28,0},{1,5},{5... | collective-permute-start | bytes 49160 | tf_op jit(solution)/shard_map/ppermute | solution.py:218
  4.7 3.1 %collective-permute-start.1 = (bf16[32,256]{1,0:T(8,128)(2,1)S(1)}, bf16[32,256]{1,0:T(8,128)(2,1)S(1)}, u32[]{:S(2)}, u32[]{:S(2)}) collective-permute-start(bf16[32,256]{1,0:T(8,128)(2,1)S(1)} %bitcast.25), channel_id=1, source_target_pairs={{4,0},{8,4},{12,8},{16,12},{20,16},{24,20},{28,24},{0,28},{5,1},{9... | collective-permute-start | bytes 49160 | tf_op jit(solution)/shard_map/ppermute | solution.py:218
  8.7 3.4 %shard_map.102 = (bf16[32,72,128]{2,1,0:T(8,128)(2,1)}, s32[1,1024]{1,0:T(1,128)S(1)}) custom-call(s32[1]{0:T(128)} %bitcast.me_ref, s32[1,1024]{1,0:T(1,128)} %bitcast.27, s32[1,1024]{1,0:T(1,128)} %bitcast.28, bf16[1024,128]{1,0:T(8,128)(2,1)} %feat_hbm.1), custom_call_target="tpu_custom_call" | custom-call | flops 536870912 | bytes 864260 | tf_op jit(solution)/shard_map/pallas_call | solution.py:35
  12.2 3.6 %all-to-all-start = ((bf16[32,72,128]{2,1,0:T(8,128)(2,1)}), bf16[32,72,128]{2,1,0:T(8,128)(2,1)S(1)}, u32[]{:S(2)}, u32[]{:S(2)}) async-start(bf16[32,72,128]{2,1,0:T(8,128)(2,1)} %get-tuple-element.62), calls=%async_computation | async-start | bytes 1179648 | tf_op jit(solution)/shard_map/all_to_all | solution.py:592
  17.7 3.9 %collective-permute-done.2.top_ref = bf16[144,256]{1,0:T(8,128)(2,1)S(1)} collective-permute-done((bf16[144,256]{1,0:T(8,128)(2,1)S(1)}, bf16[144,256]{1,0:T(8,128)(2,1)S(1)}, u32[]{:S(2)}, u32[]{:S(2)}) %collective-permute-start.2) | collective-permute-done | bytes 73760 | tf_op jit(solution)/shard_map/ppermute | solution.py:234
  23.2 9.2 %shard_map.103 = (bf16[32,128,256]{2,1,0:T(8,128)(2,1)}, bf16[3,34,128,256]{3,2,1,0:T(8,128)(2,1)}) custom-call(s32[2]{0:T(128)S(1)} %add_convert_fusion.inside_ref, bf16[32,128,256]{2,1,0:T(8,128)(2,1)} %grid_hbm.1, bf16[32,256]{1,0:T(8,128)(2,1)S(1)} %collective-permute-done.left_ref, bf16[32,256]{1,0:T(8,128)(2,1)S(1)} %collective-permute-done.1.right_ref, ...), custom_call_target="tpu_custom_call" | custom-call | flops 4831838208 | bytes 12238856 | tf_op jit(solution)/shard_map/pallas_call | solution.py:35
  32.5 9.4 %shard_map.104 = (bf16[2048,256]{1,0:T(8,128)(2,1)}, f32[128,256]{1,0:T(8,128)}, bf16[2048,256]{1,0:T(8,128)(2,1)}, f32[16,128]{1,0:T(8,128)}) custom-call(bf16[32,72,128]{2,1,0:T(8,128)(2,1)S(1)} %all-to-all-done.recv_ref, bf16[4096,256]{1,0:T(8,128)(2,1)} %bitcast.29, bf16[128,256]{1,0:T(8,128)(2,1)S(1)} %copy-done.2), custom_call_target="tpu_custom_call" | custom-call | flops 4294967296 | bytes 4988928 | tf_op jit(solution)/shard_map/pallas_call | solution.py:35
  42.0 6.0 %all-to-all-start.1 = ((bf16[32,64,256]{2,1,0:T(8,128)(2,1)}), bf16[32,64,256]{2,1,0:T(8,128)(2,1)S(1)}, u32[]{:S(2)}, u32[]{:S(2)}) async-start(bf16[32,64,256]{2,1,0:T(8,128)(2,1)} %bitcast.23), calls=%async_computation.1 | async-start | bytes 2097152 | tf_op jit(solution)/shard_map/all_to_all | solution.py:626
  48.0 13.6 %shard_map.105 = (bf16[4096,256]{1,0:T(8,128)(2,1)}, f32[2432,128]{1,0:T(8,128)S(1)}, f32[2432,128]{1,0:T(8,128)S(1)}, bf16[32,256]{1,0:T(8,128)(2,1)S(1)}, bf16[32,256]{1,0:T(8,128)(2,1)S(1)}) custom-call(s32[1]{0:T(128)} %bitcast.me_ref, f32[16,128]{1,0:T(8,128)} %get-tuple-element.66.code_hbm, bf16[2048,256]{1,0:T(8,128)(2,1)} %get-tuple-element.67.embed_hbm, ...), custom_call_target="tpu_custom_call" | custom-call | flops 9126805504 | bytes 14589956 | tf_op jit(solution)/shard_map/pallas_call | solution.py:35
  61.9 2.7 %collective-permute-done.4.refs_1_ = f32[2432,128]{1,0:T(8,128)S(1)} collective-permute-done((f32[2432,128]{1,0:T(8,128)S(1)}, f32[2432,128]{1,0:T(8,128)S(1)}, u32[]{:S(2)}, u32[]{:S(2)}) %collective-permute-start.4) | collective-permute-done | bytes 1245216 | tf_op jit(solution)/shard_map/ppermute | solution.py:452
  64.8 1.8 %collective-permute-start.14 = (bf16[32,256]{1,0:T(8,128)(2,1)S(1)}, bf16[32,256]{1,0:T(8,128)(2,1)S(1)}, u32[]{:S(2)}, u32[]{:S(2)}) collective-permute-start(bf16[32,256]{1,0:T(8,128)(2,1)S(1)} %get-tuple-element.97), channel_id=1, source_target_pairs={{0,4},{4,8},{8,12},{12,16},{16,20},{20,24},{24,28},{28,0},{1,5},{5... | collective-permute-start | bytes 49160 | tf_op jit(solution)/shard_map/ppermute | solution.py:218
  66.6 3.0 %collective-permute-start.15 = (bf16[32,256]{1,0:T(8,128)(2,1)S(1)}, bf16[32,256]{1,0:T(8,128)(2,1)S(1)}, u32[]{:S(2)}, u32[]{:S(2)}) collective-permute-start(bf16[32,256]{1,0:T(8,128)(2,1)S(1)} %get-tuple-element.98), channel_id=1, source_target_pairs={{4,0},{8,4},{12,8},{16,12},{20,16},{24,20},{28,24},{0,28},{5,1},{9... | collective-permute-start | bytes 49160 | tf_op jit(solution)/shard_map/ppermute | solution.py:218
  70.5 1.8 %collective-permute-start.5 = (bf16[608,128]{1,0:T(8,128)(2,1)S(1)}, bf16[608,128]{1,0:T(8,128)(2,1)S(1)}, u32[]{:S(2)}, u32[]{:S(2)}) collective-permute-start(bf16[608,128]{1,0:T(8,128)(2,1)S(1)} %get-tuple-element.78), channel_id=1, source_target_pairs={{0,2},{1,3},{2,0},{3,1},{4,6},{5,7},{6,4},{7,5},{8,10},{9,11},{10,... | collective-permute-start | bytes 466952 | tf_op jit(solution)/shard_map/ppermute | solution.py:452
  72.3 1.7 %collective-permute-start.7 = (bf16[608,128]{1,0:T(8,128)(2,1)S(1)}, bf16[608,128]{1,0:T(8,128)(2,1)S(1)}, u32[]{:S(2)}, u32[]{:S(2)}) collective-permute-start(bf16[608,128]{1,0:T(8,128)(2,1)S(1)} %get-tuple-element.80), channel_id=1, source_target_pairs={{0,6},{1,7},{2,4},{3,5},{4,2},{5,3},{6,0},{7,1},{8,14},{9,15},{10,... | collective-permute-start | bytes 466952 | tf_op jit(solution)/shard_map/ppermute | solution.py:452
  74.8 1.7 %collective-permute-done.5.refs_1_ = bf16[608,128]{1,0:T(8,128)(2,1)S(1)} collective-permute-done((bf16[608,128]{1,0:T(8,128)(2,1)S(1)}, bf16[608,128]{1,0:T(8,128)(2,1)S(1)}, u32[]{:S(2)}, u32[]{:S(2)}) %collective-permute-start.5) | collective-permute-done | bytes 155680 | tf_op jit(solution)/shard_map/ppermute | solution.py:452
  76.5 2.8 %collective-permute-done.6.refs_2_ = bf16[608,128]{1,0:T(8,128)(2,1)S(1)} collective-permute-done((bf16[608,128]{1,0:T(8,128)(2,1)S(1)}, bf16[608,128]{1,0:T(8,128)(2,1)S(1)}, u32[]{:S(2)}, u32[]{:S(2)}) %collective-permute-start.6) | collective-permute-done | bytes 155680 | tf_op jit(solution)/shard_map/ppermute | solution.py:452
  79.2 2.0 %collective-permute-done.7.refs_3_ = bf16[608,128]{1,0:T(8,128)(2,1)S(1)} collective-permute-done((bf16[608,128]{1,0:T(8,128)(2,1)S(1)}, bf16[608,128]{1,0:T(8,128)(2,1)S(1)}, u32[]{:S(2)}, u32[]{:S(2)}) %collective-permute-start.7) | collective-permute-done | bytes 155680 | tf_op jit(solution)/shard_map/ppermute | solution.py:452
  83.3 2.4 %collective-permute-start.9 = (bf16[152,128]{1,0:T(8,128)(2,1)S(1)}, bf16[152,128]{1,0:T(8,128)(2,1)S(1)}, u32[]{:S(2)}, u32[]{:S(2)}) collective-permute-start(bf16[152,128]{1,0:T(8,128)(2,1)S(1)} %get-tuple-element.88), channel_id=1, source_target_pairs={{0,16},{1,17},{2,18},{3,19},{4,20},{5,21},{6,22},{7,23},{8,24},{9,... | collective-permute-start | bytes 116744 | tf_op jit(solution)/shard_map/ppermute | solution.py:452
  85.7 2.4 %shard_map.108 = bf16[1024,256]{1,0:T(8,128)(2,1)} custom-call(s32[1,1024]{1,0:T(1,128)S(1)} %get-tuple-element.90.place_ref, bf16[2048,256]{1,0:T(8,128)(2,1)S(1)} %bitcast.20), custom_call_target="tpu_custom_call" | custom-call | flops 1073741824 | bytes 1576960 | tf_op jit(solution)/shard_map/pallas_call | solution.py:35
  91.0 1.7 %collective-permute-start.13 = (bf16[152,128]{1,0:T(8,128)(2,1)S(1)}, bf16[152,128]{1,0:T(8,128)(2,1)S(1)}, u32[]{:S(2)}, u32[]{:S(2)}) collective-permute-start(bf16[152,128]{1,0:T(8,128)(2,1)S(1)} %shard_map.109.refs_0_), channel_id=1, source_target_pairs={{0,24},{1,25},{2,26},{3,27},{4,28},{5,29},{6,30},{7,31},{8,16},{9,... | collective-permute-start | bytes 116744 | tf_op jit(solution)/shard_map/ppermute | solution.py:452
  92.7 4.7 %shard_map.110.refs_0_ = bf16[32,128,256]{2,1,0:T(8,128)(2,1)} custom-call(s32[2]{0:T(128)S(1)} %add_convert_fusion.inside_ref, bf16[32,128,256]{2,1,0:T(8,128)(2,1)S(1)} %bitcast.21, bf16[32,256]{1,0:T(8,128)(2,1)S(1)} %collective-permute-done.14.left_ref, bf16[32,256]{1,0:T(8,128)(2,1)S(1)} %collective-permute-done.15.right_ref, ...), custom_call_target="tpu_custom_call" | custom-call | flops 2415919104 | bytes 5554184 | tf_op jit(solution)/shard_map/pallas_call | solution.py:35
  99.4 1.7 %collective-permute-start.20 = (bf16[608,128]{1,0:T(8,128)(2,1)S(1)}, bf16[608,128]{1,0:T(8,128)(2,1)S(1)}, u32[]{:S(2)}, u32[]{:S(2)}) collective-permute-start(bf16[608,128]{1,0:T(8,128)(2,1)S(1)} %shard_map.111.refs_0_), channel_id=1, source_target_pairs={{0,6},{1,7},{2,4},{3,5},{4,2},{5,3},{6,0},{7,1},{8,14},{9,15},{10,... | collective-permute-start | bytes 466952 | tf_op jit(solution)/shard_map/ppermute | solution.py:452
  101.0 4.7 %shard_map.112 = bf16[32,128,256]{2,1,0:T(8,128)(2,1)} custom-call(s32[2]{0:T(128)S(1)} %add_convert_fusion.inside_ref, bf16[32,128,256]{2,1,0:T(8,128)(2,1)S(1)} %bitcast.22, bf16[32,256]{1,0:T(8,128)(2,1)S(1)} %collective-permute-done.14.left_ref, bf16[32,256]{1,0:T(8,128)(2,1)S(1)} %collective-permute-done.15.right_ref, ...), custom_call_target="tpu_custom_call", output_to_operand_aliasing={{}: (7, {})} | custom-call | flops 2415919104 | bytes 7651336 | tf_op jit(solution)/shard_map/pallas_call | solution.py:35
  106.1 2.0 %collective-permute-done.21.other_ref = bf16[2432,128]{1,0:T(8,128)(2,1)S(1)} collective-permute-done((bf16[2432,128]{1,0:T(8,128)(2,1)S(1)}, bf16[2432,128]{1,0:T(8,128)(2,1)S(1)}, u32[]{:S(2)}, u32[]{:S(2)}) %collective-permute-start.21) | collective-permute-done | bytes 622624 | tf_op jit(solution)/shard_map/ppermute | solution.py:452
  (60 shorter events, 16.5 us)
Async XLA Ops:
  1.7 10.4 %collective-permute-start = (bf16[32,256]{1,0:T(8,128)(2,1)S(1)}, bf16[32,256]{1,0:T(8,128)(2,1)S(1)}, u32[]{:S(2)}, u32[]{:S(2)}) collective-permute-start(bf16[32,256]{1,0:T(8,128)(2,1)S(1)} %bitcast.24), channel_id=1, source_target_pairs={{0,4},{4,8},{8,12},{12,16},{16,20},{20,24},{24,28},{28,0},{1,5},{5... | collective-permute-start | bytes 49160 | tf_op jit(solution)/shard_map/ppermute | solution.py:218
  4.7 7.4 %collective-permute-start.1 = (bf16[32,256]{1,0:T(8,128)(2,1)S(1)}, bf16[32,256]{1,0:T(8,128)(2,1)S(1)}, u32[]{:S(2)}, u32[]{:S(2)}) collective-permute-start(bf16[32,256]{1,0:T(8,128)(2,1)S(1)} %bitcast.25), channel_id=1, source_target_pairs={{4,0},{8,4},{12,8},{16,12},{20,16},{24,20},{28,24},{0,28},{5,1},{9... | collective-permute-start | bytes 49160 | tf_op jit(solution)/shard_map/ppermute | solution.py:218
  12.2 20.3 %all-to-all-start = ((bf16[32,72,128]{2,1,0:T(8,128)(2,1)}), bf16[32,72,128]{2,1,0:T(8,128)(2,1)S(1)}, u32[]{:S(2)}, u32[]{:S(2)}) async-start(bf16[32,72,128]{2,1,0:T(8,128)(2,1)} %get-tuple-element.62), calls=%async_computation | async-start | bytes 1179648 | tf_op jit(solution)/shard_map/all_to_all | solution.py:592
  15.8 5.8 %collective-permute-start.2 = (bf16[144,256]{1,0:T(8,128)(2,1)S(1)}, bf16[144,256]{1,0:T(8,128)(2,1)S(1)}, u32[]{:S(2)}, u32[]{:S(2)}) collective-permute-start(bf16[144,256]{1,0:T(8,128)(2,1)S(1)} %get-tuple-element.63), channel_id=1, source_target_pairs={{0,1},{1,2},{2,3},{3,0},{4,5},{5,6},{6,7},{7,4},{8,9},{9,10},{10,1... | collective-permute-start | bytes 221192 | tf_op jit(solution)/shard_map/ppermute | solution.py:234
  16.1 7.1 %collective-permute-start.3 = (bf16[144,256]{1,0:T(8,128)(2,1)S(1)}, bf16[144,256]{1,0:T(8,128)(2,1)S(1)}, u32[]{:S(2)}, u32[]{:S(2)}) collective-permute-start(bf16[144,256]{1,0:T(8,128)(2,1)S(1)} %get-tuple-element.64), channel_id=1, source_target_pairs={{1,0},{2,1},{3,2},{0,3},{5,4},{6,5},{7,6},{4,7},{9,8},{10,9},{11,1... | collective-permute-start | bytes 221192 | tf_op jit(solution)/shard_map/ppermute | solution.py:234
  42.0 39.2 %all-to-all-start.1 = ((bf16[32,64,256]{2,1,0:T(8,128)(2,1)}), bf16[32,64,256]{2,1,0:T(8,128)(2,1)S(1)}, u32[]{:S(2)}, u32[]{:S(2)}) async-start(bf16[32,64,256]{2,1,0:T(8,128)(2,1)} %bitcast.23), calls=%async_computation.1 | async-start | bytes 2097152 | tf_op jit(solution)/shard_map/all_to_all | solution.py:626
  61.6 3.0 %collective-permute-start.4 = (f32[2432,128]{1,0:T(8,128)S(1)}, f32[2432,128]{1,0:T(8,128)S(1)}, u32[]{:S(2)}, u32[]{:S(2)}) collective-permute-start(f32[2432,128]{1,0:T(8,128)S(1)} %get-tuple-element.71), channel_id=1, source_target_pairs={{0,1},{1,0},{2,3},{3,2},{4,5},{5,4},{6,7},{7,6},{8,9},{9,8},{10,11... | collective-permute-start | bytes 3735560 | tf_op jit(solution)/shard_map/ppermute | solution.py:452
  64.8 9.2 %collective-permute-start.14 = (bf16[32,256]{1,0:T(8,128)(2,1)S(1)}, bf16[32,256]{1,0:T(8,128)(2,1)S(1)}, u32[]{:S(2)}, u32[]{:S(2)}) collective-permute-start(bf16[32,256]{1,0:T(8,128)(2,1)S(1)} %get-tuple-element.97), channel_id=1, source_target_pairs={{0,4},{4,8},{8,12},{12,16},{16,20},{20,24},{24,28},{28,0},{1,5},{5... | collective-permute-start | bytes 49160 | tf_op jit(solution)/shard_map/ppermute | solution.py:218
  66.6 7.4 %collective-permute-start.15 = (bf16[32,256]{1,0:T(8,128)(2,1)S(1)}, bf16[32,256]{1,0:T(8,128)(2,1)S(1)}, u32[]{:S(2)}, u32[]{:S(2)}) collective-permute-start(bf16[32,256]{1,0:T(8,128)(2,1)S(1)} %get-tuple-element.98), channel_id=1, source_target_pairs={{4,0},{8,4},{12,8},{16,12},{20,16},{24,20},{28,24},{0,28},{5,1},{9... | collective-permute-start | bytes 49160 | tf_op jit(solution)/shard_map/ppermute | solution.py:218
  70.5 6.0 %collective-permute-start.5 = (bf16[608,128]{1,0:T(8,128)(2,1)S(1)}, bf16[608,128]{1,0:T(8,128)(2,1)S(1)}, u32[]{:S(2)}, u32[]{:S(2)}) collective-permute-start(bf16[608,128]{1,0:T(8,128)(2,1)S(1)} %get-tuple-element.78), channel_id=1, source_target_pairs={{0,2},{1,3},{2,0},{3,1},{4,6},{5,7},{6,4},{7,5},{8,10},{9,11},{10,... | collective-permute-start | bytes 466952 | tf_op jit(solution)/shard_map/ppermute | solution.py:452
  72.3 6.9 %collective-permute-start.6 = (bf16[608,128]{1,0:T(8,128)(2,1)S(1)}, bf16[608,128]{1,0:T(8,128)(2,1)S(1)}, u32[]{:S(2)}, u32[]{:S(2)}) collective-permute-start(bf16[608,128]{1,0:T(8,128)(2,1)S(1)} %get-tuple-element.79), channel_id=1, source_target_pairs={{0,4},{1,5},{2,6},{3,7},{4,0},{5,1},{6,2},{7,3},{8,12},{9,13},{10,... | collective-permute-start | bytes 466952 | tf_op jit(solution)/shard_map/ppermute | solution.py:452
  72.3 8.9 %collective-permute-start.7 = (bf16[608,128]{1,0:T(8,128)(2,1)S(1)}, bf16[608,128]{1,0:T(8,128)(2,1)S(1)}, u32[]{:S(2)}, u32[]{:S(2)}) collective-permute-start(bf16[608,128]{1,0:T(8,128)(2,1)S(1)} %get-tuple-element.80), channel_id=1, source_target_pairs={{0,6},{1,7},{2,4},{3,5},{4,2},{5,3},{6,0},{7,1},{8,14},{9,15},{10,... | collective-permute-start | bytes 466952 | tf_op jit(solution)/shard_map/ppermute | solution.py:452
  74.1 18.6 %collective-permute-start.17 = (bf16[144,256]{1,0:T(8,128)(2,1)S(1)}, bf16[144,256]{1,0:T(8,128)(2,1)S(1)}, u32[]{:S(2)}, u32[]{:S(2)}) collective-permute-start(bf16[144,256]{1,0:T(8,128)(2,1)S(1)} %pad_maximum_fusion.1), channel_id=1, source_target_pairs={{1,0},{2,1},{3,2},{0,3},{5,4},{6,5},{7,6},{4,7},{9,8},{10,9},{11,1... | collective-permute-start | bytes 221192 | tf_op jit(solution)/shard_map/ppermute | solution.py:234
  74.3 18.4 %collective-permute-start.16 = (bf16[144,256]{1,0:T(8,128)(2,1)S(1)}, bf16[144,256]{1,0:T(8,128)(2,1)S(1)}, u32[]{:S(2)}, u32[]{:S(2)}) collective-permute-start(bf16[144,256]{1,0:T(8,128)(2,1)S(1)} %fusion.8), channel_id=1, source_target_pairs={{0,1},{1,2},{2,3},{3,0},{4,5},{5,6},{6,7},{7,4},{8,9},{9,10},{10,1... | collective-permute-start | bytes 221192 | tf_op jit(solution)/shard_map/ppermute | solution.py:234
  81.3 6.8 %collective-permute-start.10 = (bf16[152,128]{1,0:T(8,128)(2,1)S(1)}, bf16[152,128]{1,0:T(8,128)(2,1)S(1)}, u32[]{:S(2)}, u32[]{:S(2)}) collective-permute-start(bf16[152,128]{1,0:T(8,128)(2,1)S(1)} %get-tuple-element.89), channel_id=1, source_target_pairs={{0,24},{1,25},{2,26},{3,27},{4,28},{5,29},{6,30},{7,31},{8,16},{9,... | collective-permute-start | bytes 116744 | tf_op jit(solution)/shard_map/ppermute | solution.py:452
  82.6 5.5 %collective-permute-start.8 = (bf16[152,128]{1,0:T(8,128)(2,1)S(1)}, bf16[152,128]{1,0:T(8,128)(2,1)S(1)}, u32[]{:S(2)}, u32[]{:S(2)}) collective-permute-start(bf16[152,128]{1,0:T(8,128)(2,1)S(1)} %get-tuple-element.87), channel_id=1, source_target_pairs={{0,8},{1,9},{2,10},{3,11},{4,12},{5,13},{6,14},{7,15},{8,0},{9,1},... | collective-permute-start | bytes 116744 | tf_op jit(solution)/shard_map/ppermute | solution.py:452
  83.3 4.9 %collective-permute-start.9 = (bf16[152,128]{1,0:T(8,128)(2,1)S(1)}, bf16[152,128]{1,0:T(8,128)(2,1)S(1)}, u32[]{:S(2)}, u32[]{:S(2)}) collective-permute-start(bf16[152,128]{1,0:T(8,128)(2,1)S(1)} %get-tuple-element.88), channel_id=1, source_target_pairs={{0,16},{1,17},{2,18},{3,19},{4,20},{5,21},{6,22},{7,23},{8,24},{9,... | collective-permute-start | bytes 116744 | tf_op jit(solution)/shard_map/ppermute | solution.py:452
  88.2 9.2 %collective-permute-start.11 = (bf16[152,128]{1,0:T(8,128)(2,1)S(1)}, bf16[152,128]{1,0:T(8,128)(2,1)S(1)}, u32[]{:S(2)}, u32[]{:S(2)}) collective-permute-start(bf16[152,128]{1,0:T(8,128)(2,1)S(1)} %shard_map.109.refs_0_), channel_id=1, source_target_pairs={{0,8},{1,9},{2,10},{3,11},{4,12},{5,13},{6,14},{7,15},{8,0},{9,1},... | collective-permute-start | bytes 116744 | tf_op jit(solution)/shard_map/ppermute | solution.py:452
  89.6 7.8 %collective-permute-start.12 = (bf16[152,128]{1,0:T(8,128)(2,1)S(1)}, bf16[152,128]{1,0:T(8,128)(2,1)S(1)}, u32[]{:S(2)}, u32[]{:S(2)}) collective-permute-start(bf16[152,128]{1,0:T(8,128)(2,1)S(1)} %shard_map.109.refs_0_), channel_id=1, source_target_pairs={{0,16},{1,17},{2,18},{3,19},{4,20},{5,21},{6,22},{7,23},{8,24},{9,... | collective-permute-start | bytes 116744 | tf_op jit(solution)/shard_map/ppermute | solution.py:452
  91.0 6.5 %collective-permute-start.13 = (bf16[152,128]{1,0:T(8,128)(2,1)S(1)}, bf16[152,128]{1,0:T(8,128)(2,1)S(1)}, u32[]{:S(2)}, u32[]{:S(2)}) collective-permute-start(bf16[152,128]{1,0:T(8,128)(2,1)S(1)} %shard_map.109.refs_0_), channel_id=1, source_target_pairs={{0,24},{1,25},{2,26},{3,27},{4,28},{5,29},{6,30},{7,31},{8,16},{9,... | collective-permute-start | bytes 116744 | tf_op jit(solution)/shard_map/ppermute | solution.py:452
  97.5 8.3 %collective-permute-start.18 = (bf16[608,128]{1,0:T(8,128)(2,1)S(1)}, bf16[608,128]{1,0:T(8,128)(2,1)S(1)}, u32[]{:S(2)}, u32[]{:S(2)}) collective-permute-start(bf16[608,128]{1,0:T(8,128)(2,1)S(1)} %shard_map.111.refs_0_), channel_id=1, source_target_pairs={{0,2},{1,3},{2,0},{3,1},{4,6},{5,7},{6,4},{7,5},{8,10},{9,11},{10,... | collective-permute-start | bytes 466952 | tf_op jit(solution)/shard_map/ppermute | solution.py:452
  98.7 7.1 %collective-permute-start.19 = (bf16[608,128]{1,0:T(8,128)(2,1)S(1)}, bf16[608,128]{1,0:T(8,128)(2,1)S(1)}, u32[]{:S(2)}, u32[]{:S(2)}) collective-permute-start(bf16[608,128]{1,0:T(8,128)(2,1)S(1)} %shard_map.111.refs_0_), channel_id=1, source_target_pairs={{0,4},{1,5},{2,6},{3,7},{4,0},{5,1},{6,2},{7,3},{8,12},{9,13},{10,... | collective-permute-start | bytes 466952 | tf_op jit(solution)/shard_map/ppermute | solution.py:452
  99.4 6.5 %collective-permute-start.20 = (bf16[608,128]{1,0:T(8,128)(2,1)S(1)}, bf16[608,128]{1,0:T(8,128)(2,1)S(1)}, u32[]{:S(2)}, u32[]{:S(2)}) collective-permute-start(bf16[608,128]{1,0:T(8,128)(2,1)S(1)} %shard_map.111.refs_0_), channel_id=1, source_target_pairs={{0,6},{1,7},{2,4},{3,5},{4,2},{5,3},{6,0},{7,1},{8,14},{9,15},{10,... | collective-permute-start | bytes 466952 | tf_op jit(solution)/shard_map/ppermute | solution.py:452
  106.0 2.1 %collective-permute-start.21 = (bf16[2432,128]{1,0:T(8,128)(2,1)S(1)}, bf16[2432,128]{1,0:T(8,128)(2,1)S(1)}, u32[]{:S(2)}, u32[]{:S(2)}) collective-permute-start(bf16[2432,128]{1,0:T(8,128)(2,1)S(1)} %shard_map.113.own_ref), channel_id=1, source_target_pairs={{0,1},{1,0},{2,3},{3,2},{4,5},{5,4},{6,7},{7,6},{8,9},{9,8},{10,11... | collective-permute-start | bytes 1867784 | tf_op jit(solution)/shard_map/ppermute | solution.py:452
  (4 other events, 40.3 us)

commit v6 on v5

--- a/solution.py
+++ b/solution.py
@@ -177,11 +177,21 @@
         put(base + i + 1 - start, grid_ref[i], left32[at, :], right32[at, :])
         return carry
 
+    def fill_rows(i, j):
+        def four(k, carry):
+            for q in range(4):
+                fill(i + 4 * k + q, carry)
+            return carry
+
+        lax.fori_loop(0, (j - i) // 4, four, 0)
+        for row in range(j - (j - i) % 4, j):
+            fill(row, 0)
+
     for load, i, j in zip(loads, cuts[:-1], cuts[1:]):
         load.wait()
-        lax.fori_loop(i, j, fill, 0)
+        fill_rows(i, j)
     if not back:
-        lax.fori_loop(0, held, fill, 0)
+        fill_rows(0, held)
     stores = []
     if back:
         stores += [begin(pad_ref.at[b], pad_hbm.at[b], pad_sem.at[b]) for b in range(3)]

time: 110 us -> 110 us (level)
  no operation moved by 1% of the time
where the time goes in v6:
time: 110 us
  Pallas kernels  49.5 us (45%)
  starting transfers between devices  39.2 us (36%)
  waiting for transfers between devices  17.1 us (16%)
  local copies, waits for them, and re-layouts  2.84 us (3%)
    pallas_call x13, Pallas kernels, kernel_call(): pl.pallas_call(body, out_shape=[pltpu.HBM(o.shape, o.dtype) if i in far e...  49.5 us
    ppermute x14, starting transfers between devices, swap(): return lax.ppermute(x, AXES, [(i, i ^ bit) for i in range(count)])  16.4 us
    ppermute x14, waiting for transfers between devices, swap(): return lax.ppermute(x, AXES, [(i, i ^ bit) for i in range(count)])  11.4 us
    ppermute x4, starting transfers between devices, side_edges(): return (lax.ppermute(last, 'lon', up), lax.ppermute(first, 'lon', down))  10.9 us
    all_to_all x1, starting transfers between devices, on_device(): lax.all_to_all(grad.reshape(owners, slots, width), AXES, split_axis=0, co...  5.95 us
    ppermute x4, waiting for transfers between devices, end_edges(): return (lax.ppermute(last, 'lat', up), lax.ppermute(first, 'lat', down))  5.52 us
    all_to_all x1, starting transfers between devices, on_device(): recv = lax.all_to_all(send, AXES, split_axis=0, concat_axis=0, tiled=True)  3.59 us
    ppermute x4, starting transfers between devices, end_edges(): return (lax.ppermute(last, 'lat', up), lax.ppermute(first, 'lat', down))  2.41 us
  transfers between devices with their start and end apart: 24, of which 10 were waited for; matrix products, arithmetic and copies ran while one was open for 2% of the time, Pallas kernels for 35%

profile of v6, /device:TPU:0, one launch (start us, length us, event | category | flops | bytes accessed | tf_op | source)
XLA Modules:
  0.0 109.8 jit_solution(6875705187689687841)
XLA Ops:
  1.7 3.0 %collective-permute-start = (bf16[32,256]{1,0:T(8,128)(2,1)S(1)}, bf16[32,256]{1,0:T(8,128)(2,1)S(1)}, u32[]{:S(2)}, u32[]{:S(2)}) collective-permute-start(bf16[32,256]{1,0:T(8,128)(2,1)S(1)} %bitcast.24), channel_id=1, source_target_pairs={{0,4},{4,8},{8,12},{12,16},{16,20},{20,24},{24,28},{28,0},{1,5},{5... | collective-permute-start | bytes 49160 | tf_op jit(solution)/shard_map/ppermute | solution.py:228
  4.7 3.1 %collective-permute-start.1 = (bf16[32,256]{1,0:T(8,128)(2,1)S(1)}, bf16[32,256]{1,0:T(8,128)(2,1)S(1)}, u32[]{:S(2)}, u32[]{:S(2)}) collective-permute-start(bf16[32,256]{1,0:T(8,128)(2,1)S(1)} %bitcast.25), channel_id=1, source_target_pairs={{4,0},{8,4},{12,8},{16,12},{20,16},{24,20},{28,24},{0,28},{5,1},{9... | collective-permute-start | bytes 49160 | tf_op jit(solution)/shard_map/ppermute | solution.py:228
  8.7 3.4 %shard_map.102 = (bf16[32,72,128]{2,1,0:T(8,128)(2,1)}, s32[1,1024]{1,0:T(1,128)S(1)}) custom-call(s32[1]{0:T(128)} %bitcast.me_ref, s32[1,1024]{1,0:T(1,128)} %bitcast.27, s32[1,1024]{1,0:T(1,128)} %bitcast.28, bf16[1024,128]{1,0:T(8,128)(2,1)} %feat_hbm.1), custom_call_target="tpu_custom_call" | custom-call | flops 536870912 | bytes 864260 | tf_op jit(solution)/shard_map/pallas_call | solution.py:35
  12.2 3.6 %all-to-all-start = ((bf16[32,72,128]{2,1,0:T(8,128)(2,1)}), bf16[32,72,128]{2,1,0:T(8,128)(2,1)S(1)}, u32[]{:S(2)}, u32[]{:S(2)}) async-start(bf16[32,72,128]{2,1,0:T(8,128)(2,1)} %get-tuple-element.62), calls=%async_computation | async-start | bytes 1179648 | tf_op jit(solution)/shard_map/all_to_all | solution.py:602
  17.7 3.9 %collective-permute-done.2.top_ref = bf16[144,256]{1,0:T(8,128)(2,1)S(1)} collective-permute-done((bf16[144,256]{1,0:T(8,128)(2,1)S(1)}, bf16[144,256]{1,0:T(8,128)(2,1)S(1)}, u32[]{:S(2)}, u32[]{:S(2)}) %collective-permute-start.2) | collective-permute-done | bytes 73760 | tf_op jit(solution)/shard_map/ppermute | solution.py:244
  23.2 9.2 %shard_map.103 = (bf16[32,128,256]{2,1,0:T(8,128)(2,1)}, bf16[3,34,128,256]{3,2,1,0:T(8,128)(2,1)}) custom-call(s32[2]{0:T(128)S(1)} %add_convert_fusion.inside_ref, bf16[32,128,256]{2,1,0:T(8,128)(2,1)} %grid_hbm.1, bf16[32,256]{1,0:T(8,128)(2,1)S(1)} %collective-permute-done.left_ref, bf16[32,256]{1,0:T(8,128)(2,1)S(1)} %collective-permute-done.1.right_ref, ...), custom_call_target="tpu_custom_call" | custom-call | flops 4831838208 | bytes 12238856 | tf_op jit(solution)/shard_map/pallas_call | solution.py:35
  32.5 9.4 %shard_map.104 = (bf16[2048,256]{1,0:T(8,128)(2,1)}, f32[128,256]{1,0:T(8,128)}, bf16[2048,256]{1,0:T(8,128)(2,1)}, f32[16,128]{1,0:T(8,128)}) custom-call(bf16[32,72,128]{2,1,0:T(8,128)(2,1)S(1)} %all-to-all-done.recv_ref, bf16[4096,256]{1,0:T(8,128)(2,1)} %bitcast.29, bf16[128,256]{1,0:T(8,128)(2,1)S(1)} %copy-done.2), custom_call_target="tpu_custom_call" | custom-call | flops 4294967296 | bytes 4988928 | tf_op jit(solution)/shard_map/pallas_call | solution.py:35
  42.0 6.0 %all-to-all-start.1 = ((bf16[32,64,256]{2,1,0:T(8,128)(2,1)}), bf16[32,64,256]{2,1,0:T(8,128)(2,1)S(1)}, u32[]{:S(2)}, u32[]{:S(2)}) async-start(bf16[32,64,256]{2,1,0:T(8,128)(2,1)} %bitcast.23), calls=%async_computation.1 | async-start | bytes 2097152 | tf_op jit(solution)/shard_map/all_to_all | solution.py:636
  47.9 13.6 %shard_map.105 = (bf16[4096,256]{1,0:T(8,128)(2,1)}, f32[2432,128]{1,0:T(8,128)S(1)}, f32[2432,128]{1,0:T(8,128)S(1)}, bf16[32,256]{1,0:T(8,128)(2,1)S(1)}, bf16[32,256]{1,0:T(8,128)(2,1)S(1)}) custom-call(s32[1]{0:T(128)} %bitcast.me_ref, f32[16,128]{1,0:T(8,128)} %get-tuple-element.66.code_hbm, bf16[2048,256]{1,0:T(8,128)(2,1)} %get-tuple-element.67.embed_hbm, ...), custom_call_target="tpu_custom_call" | custom-call | flops 9126805504 | bytes 14589956 | tf_op jit(solution)/shard_map/pallas_call | solution.py:35
  61.9 2.7 %collective-permute-done.4.refs_1_ = f32[2432,128]{1,0:T(8,128)S(1)} collective-permute-done((f32[2432,128]{1,0:T(8,128)S(1)}, f32[2432,128]{1,0:T(8,128)S(1)}, u32[]{:S(2)}, u32[]{:S(2)}) %collective-permute-start.4) | collective-permute-done | bytes 1245216 | tf_op jit(solution)/shard_map/ppermute | solution.py:462
  64.8 1.8 %collective-permute-start.14 = (bf16[32,256]{1,0:T(8,128)(2,1)S(1)}, bf16[32,256]{1,0:T(8,128)(2,1)S(1)}, u32[]{:S(2)}, u32[]{:S(2)}) collective-permute-start(bf16[32,256]{1,0:T(8,128)(2,1)S(1)} %get-tuple-element.97), channel_id=1, source_target_pairs={{0,4},{4,8},{8,12},{12,16},{16,20},{20,24},{24,28},{28,0},{1,5},{5... | collective-permute-start | bytes 49160 | tf_op jit(solution)/shard_map/ppermute | solution.py:228
  66.6 3.0 %collective-permute-start.15 = (bf16[32,256]{1,0:T(8,128)(2,1)S(1)}, bf16[32,256]{1,0:T(8,128)(2,1)S(1)}, u32[]{:S(2)}, u32[]{:S(2)}) collective-permute-start(bf16[32,256]{1,0:T(8,128)(2,1)S(1)} %get-tuple-element.98), channel_id=1, source_target_pairs={{4,0},{8,4},{12,8},{16,12},{20,16},{24,20},{28,24},{0,28},{5,1},{9... | collective-permute-start | bytes 49160 | tf_op jit(solution)/shard_map/ppermute | solution.py:228
  70.4 1.8 %collective-permute-start.5 = (bf16[608,128]{1,0:T(8,128)(2,1)S(1)}, bf16[608,128]{1,0:T(8,128)(2,1)S(1)}, u32[]{:S(2)}, u32[]{:S(2)}) collective-permute-start(bf16[608,128]{1,0:T(8,128)(2,1)S(1)} %get-tuple-element.78), channel_id=1, source_target_pairs={{0,2},{1,3},{2,0},{3,1},{4,6},{5,7},{6,4},{7,5},{8,10},{9,11},{10,... | collective-permute-start | bytes 466952 | tf_op jit(solution)/shard_map/ppermute | solution.py:462
  72.3 1.7 %collective-permute-start.7 = (bf16[608,128]{1,0:T(8,128)(2,1)S(1)}, bf16[608,128]{1,0:T(8,128)(2,1)S(1)}, u32[]{:S(2)}, u32[]{:S(2)}) collective-permute-start(bf16[608,128]{1,0:T(8,128)(2,1)S(1)} %get-tuple-element.80), channel_id=1, source_target_pairs={{0,6},{1,7},{2,4},{3,5},{4,2},{5,3},{6,0},{7,1},{8,14},{9,15},{10,... | collective-permute-start | bytes 466952 | tf_op jit(solution)/shard_map/ppermute | solution.py:462
  74.7 1.7 %collective-permute-done.5.refs_1_ = bf16[608,128]{1,0:T(8,128)(2,1)S(1)} collective-permute-done((bf16[608,128]{1,0:T(8,128)(2,1)S(1)}, bf16[608,128]{1,0:T(8,128)(2,1)S(1)}, u32[]{:S(2)}, u32[]{:S(2)}) %collective-permute-start.5) | collective-permute-done | bytes 155680 | tf_op jit(solution)/shard_map/ppermute | solution.py:462
  76.4 2.8 %collective-permute-done.6.refs_2_ = bf16[608,128]{1,0:T(8,128)(2,1)S(1)} collective-permute-done((bf16[608,128]{1,0:T(8,128)(2,1)S(1)}, bf16[608,128]{1,0:T(8,128)(2,1)S(1)}, u32[]{:S(2)}, u32[]{:S(2)}) %collective-permute-start.6) | collective-permute-done | bytes 155680 | tf_op jit(solution)/shard_map/ppermute | solution.py:462
  79.2 2.0 %collective-permute-done.7.refs_3_ = bf16[608,128]{1,0:T(8,128)(2,1)S(1)} collective-permute-done((bf16[608,128]{1,0:T(8,128)(2,1)S(1)}, bf16[608,128]{1,0:T(8,128)(2,1)S(1)}, u32[]{:S(2)}, u32[]{:S(2)}) %collective-permute-start.7) | collective-permute-done | bytes 155680 | tf_op jit(solution)/shard_map/ppermute | solution.py:462
  83.3 2.4 %collective-permute-start.9 = (bf16[152,128]{1,0:T(8,128)(2,1)S(1)}, bf16[152,128]{1,0:T(8,128)(2,1)S(1)}, u32[]{:S(2)}, u32[]{:S(2)}) collective-permute-start(bf16[152,128]{1,0:T(8,128)(2,1)S(1)} %get-tuple-element.88), channel_id=1, source_target_pairs={{0,16},{1,17},{2,18},{3,19},{4,20},{5,21},{6,22},{7,23},{8,24},{9,... | collective-permute-start | bytes 116744 | tf_op jit(solution)/shard_map/ppermute | solution.py:462
  85.7 2.4 %shard_map.108 = bf16[1024,256]{1,0:T(8,128)(2,1)} custom-call(s32[1,1024]{1,0:T(1,128)S(1)} %get-tuple-element.90.place_ref, bf16[2048,256]{1,0:T(8,128)(2,1)S(1)} %bitcast.20), custom_call_target="tpu_custom_call" | custom-call | flops 1073741824 | bytes 1576960 | tf_op jit(solution)/shard_map/pallas_call | solution.py:35
  90.9 1.7 %collective-permute-start.13 = (bf16[152,128]{1,0:T(8,128)(2,1)S(1)}, bf16[152,128]{1,0:T(8,128)(2,1)S(1)}, u32[]{:S(2)}, u32[]{:S(2)}) collective-permute-start(bf16[152,128]{1,0:T(8,128)(2,1)S(1)} %shard_map.109.refs_0_), channel_id=1, source_target_pairs={{0,24},{1,25},{2,26},{3,27},{4,28},{5,29},{6,30},{7,31},{8,16},{9,... | collective-permute-start | bytes 116744 | tf_op jit(solution)/shard_map/ppermute | solution.py:462
  92.7 4.9 %shard_map.110.refs_0_ = bf16[32,128,256]{2,1,0:T(8,128)(2,1)} custom-call(s32[2]{0:T(128)S(1)} %add_convert_fusion.inside_ref, bf16[32,128,256]{2,1,0:T(8,128)(2,1)S(1)} %bitcast.21, bf16[32,256]{1,0:T(8,128)(2,1)S(1)} %collective-permute-done.14.left_ref, bf16[32,256]{1,0:T(8,128)(2,1)S(1)} %collective-permute-done.15.right_ref, ...), custom_call_target="tpu_custom_call" | custom-call | flops 2415919104 | bytes 5554184 | tf_op jit(solution)/shard_map/pallas_call | solution.py:35
  99.5 1.7 %collective-permute-start.20 = (bf16[608,128]{1,0:T(8,128)(2,1)S(1)}, bf16[608,128]{1,0:T(8,128)(2,1)S(1)}, u32[]{:S(2)}, u32[]{:S(2)}) collective-permute-start(bf16[608,128]{1,0:T(8,128)(2,1)S(1)} %shard_map.111.refs_0_), channel_id=1, source_target_pairs={{0,6},{1,7},{2,4},{3,5},{4,2},{5,3},{6,0},{7,1},{8,14},{9,15},{10,... | collective-permute-start | bytes 466952 | tf_op jit(solution)/shard_map/ppermute | solution.py:462
  101.2 4.7 %shard_map.112 = bf16[32,128,256]{2,1,0:T(8,128)(2,1)} custom-call(s32[2]{0:T(128)S(1)} %add_convert_fusion.inside_ref, bf16[32,128,256]{2,1,0:T(8,128)(2,1)S(1)} %bitcast.22, bf16[32,256]{1,0:T(8,128)(2,1)S(1)} %collective-permute-done.14.left_ref, bf16[32,256]{1,0:T(8,128)(2,1)S(1)} %collective-permute-done.15.right_ref, ...), custom_call_target="tpu_custom_call", output_to_operand_aliasing={{}: (7, {})} | custom-call | flops 2415919104 | bytes 7651336 | tf_op jit(solution)/shard_map/pallas_call | solution.py:35
  106.2 2.0 %collective-permute-done.21.other_ref = bf16[2432,128]{1,0:T(8,128)(2,1)S(1)} collective-permute-done((bf16[2432,128]{1,0:T(8,128)(2,1)S(1)}, bf16[2432,128]{1,0:T(8,128)(2,1)S(1)}, u32[]{:S(2)}, u32[]{:S(2)}) %collective-permute-start.21) | collective-permute-done | bytes 622624 | tf_op jit(solution)/shard_map/ppermute | solution.py:462
  (60 shorter events, 16.5 us)
Async XLA Ops:
  1.7 10.4 %collective-permute-start = (bf16[32,256]{1,0:T(8,128)(2,1)S(1)}, bf16[32,256]{1,0:T(8,128)(2,1)S(1)}, u32[]{:S(2)}, u32[]{:S(2)}) collective-permute-start(bf16[32,256]{1,0:T(8,128)(2,1)S(1)} %bitcast.24), channel_id=1, source_target_pairs={{0,4},{4,8},{8,12},{12,16},{16,20},{20,24},{24,28},{28,0},{1,5},{5... | collective-permute-start | bytes 49160 | tf_op jit(solution)/shard_map/ppermute | solution.py:228
  4.7 7.4 %collective-permute-start.1 = (bf16[32,256]{1,0:T(8,128)(2,1)S(1)}, bf16[32,256]{1,0:T(8,128)(2,1)S(1)}, u32[]{:S(2)}, u32[]{:S(2)}) collective-permute-start(bf16[32,256]{1,0:T(8,128)(2,1)S(1)} %bitcast.25), channel_id=1, source_target_pairs={{4,0},{8,4},{12,8},{16,12},{20,16},{24,20},{28,24},{0,28},{5,1},{9... | collective-permute-start | bytes 49160 | tf_op jit(solution)/shard_map/ppermute | solution.py:228
  12.2 20.3 %all-to-all-start = ((bf16[32,72,128]{2,1,0:T(8,128)(2,1)}), bf16[32,72,128]{2,1,0:T(8,128)(2,1)S(1)}, u32[]{:S(2)}, u32[]{:S(2)}) async-start(bf16[32,72,128]{2,1,0:T(8,128)(2,1)} %get-tuple-element.62), calls=%async_computation | async-start | bytes 1179648 | tf_op jit(solution)/shard_map/all_to_all | solution.py:602
  15.8 5.8 %collective-permute-start.2 = (bf16[144,256]{1,0:T(8,128)(2,1)S(1)}, bf16[144,256]{1,0:T(8,128)(2,1)S(1)}, u32[]{:S(2)}, u32[]{:S(2)}) collective-permute-start(bf16[144,256]{1,0:T(8,128)(2,1)S(1)} %get-tuple-element.63), channel_id=1, source_target_pairs={{0,1},{1,2},{2,3},{3,0},{4,5},{5,6},{6,7},{7,4},{8,9},{9,10},{10,1... | collective-permute-start | bytes 221192 | tf_op jit(solution)/shard_map/ppermute | solution.py:244
  16.1 7.1 %collective-permute-start.3 = (bf16[144,256]{1,0:T(8,128)(2,1)S(1)}, bf16[144,256]{1,0:T(8,128)(2,1)S(1)}, u32[]{:S(2)}, u32[]{:S(2)}) collective-permute-start(bf16[144,256]{1,0:T(8,128)(2,1)S(1)} %get-tuple-element.64), channel_id=1, source_target_pairs={{1,0},{2,1},{3,2},{0,3},{5,4},{6,5},{7,6},{4,7},{9,8},{10,9},{11,1... | collective-permute-start | bytes 221192 | tf_op jit(solution)/shard_map/ppermute | solution.py:244
  42.0 39.2 %all-to-all-start.1 = ((bf16[32,64,256]{2,1,0:T(8,128)(2,1)}), bf16[32,64,256]{2,1,0:T(8,128)(2,1)S(1)}, u32[]{:S(2)}, u32[]{:S(2)}) async-start(bf16[32,64,256]{2,1,0:T(8,128)(2,1)} %bitcast.23), calls=%async_computation.1 | async-start | bytes 2097152 | tf_op jit(solution)/shard_map/all_to_all | solution.py:636
  61.6 3.0 %collective-permute-start.4 = (f32[2432,128]{1,0:T(8,128)S(1)}, f32[2432,128]{1,0:T(8,128)S(1)}, u32[]{:S(2)}, u32[]{:S(2)}) collective-permute-start(f32[2432,128]{1,0:T(8,128)S(1)} %get-tuple-element.71), channel_id=1, source_target_pairs={{0,1},{1,0},{2,3},{3,2},{4,5},{5,4},{6,7},{7,6},{8,9},{9,8},{10,11... | collective-permute-start | bytes 3735560 | tf_op jit(solution)/shard_map/ppermute | solution.py:462
  64.8 9.2 %collective-permute-start.14 = (bf16[32,256]{1,0:T(8,128)(2,1)S(1)}, bf16[32,256]{1,0:T(8,128)(2,1)S(1)}, u32[]{:S(2)}, u32[]{:S(2)}) collective-permute-start(bf16[32,256]{1,0:T(8,128)(2,1)S(1)} %get-tuple-element.97), channel_id=1, source_target_pairs={{0,4},{4,8},{8,12},{12,16},{16,20},{20,24},{24,28},{28,0},{1,5},{5... | collective-permute-start | bytes 49160 | tf_op jit(solution)/shard_map/ppermute | solution.py:228
  66.6 7.4 %collective-permute-start.15 = (bf16[32,256]{1,0:T(8,128)(2,1)S(1)}, bf16[32,256]{1,0:T(8,128)(2,1)S(1)}, u32[]{:S(2)}, u32[]{:S(2)}) collective-permute-start(bf16[32,256]{1,0:T(8,128)(2,1)S(1)} %get-tuple-element.98), channel_id=1, source_target_pairs={{4,0},{8,4},{12,8},{16,12},{20,16},{24,20},{28,24},{0,28},{5,1},{9... | collective-permute-start | bytes 49160 | tf_op jit(solution)/shard_map/ppermute | solution.py:228
  70.4 6.0 %collective-permute-start.5 = (bf16[608,128]{1,0:T(8,128)(2,1)S(1)}, bf16[608,128]{1,0:T(8,128)(2,1)S(1)}, u32[]{:S(2)}, u32[]{:S(2)}) collective-permute-start(bf16[608,128]{1,0:T(8,128)(2,1)S(1)} %get-tuple-element.78), channel_id=1, source_target_pairs={{0,2},{1,3},{2,0},{3,1},{4,6},{5,7},{6,4},{7,5},{8,10},{9,11},{10,... | collective-permute-start | bytes 466952 | tf_op jit(solution)/shard_map/ppermute | solution.py:462
  72.3 6.9 %collective-permute-start.6 = (bf16[608,128]{1,0:T(8,128)(2,1)S(1)}, bf16[608,128]{1,0:T(8,128)(2,1)S(1)}, u32[]{:S(2)}, u32[]{:S(2)}) collective-permute-start(bf16[608,128]{1,0:T(8,128)(2,1)S(1)} %get-tuple-element.79), channel_id=1, source_target_pairs={{0,4},{1,5},{2,6},{3,7},{4,0},{5,1},{6,2},{7,3},{8,12},{9,13},{10,... | collective-permute-start | bytes 466952 | tf_op jit(solution)/shard_map/ppermute | solution.py:462
  72.3 8.9 %collective-permute-start.7 = (bf16[608,128]{1,0:T(8,128)(2,1)S(1)}, bf16[608,128]{1,0:T(8,128)(2,1)S(1)}, u32[]{:S(2)}, u32[]{:S(2)}) collective-permute-start(bf16[608,128]{1,0:T(8,128)(2,1)S(1)} %get-tuple-element.80), channel_id=1, source_target_pairs={{0,6},{1,7},{2,4},{3,5},{4,2},{5,3},{6,0},{7,1},{8,14},{9,15},{10,... | collective-permute-start | bytes 466952 | tf_op jit(solution)/shard_map/ppermute | solution.py:462
  74.1 18.6 %collective-permute-start.17 = (bf16[144,256]{1,0:T(8,128)(2,1)S(1)}, bf16[144,256]{1,0:T(8,128)(2,1)S(1)}, u32[]{:S(2)}, u32[]{:S(2)}) collective-permute-start(bf16[144,256]{1,0:T(8,128)(2,1)S(1)} %pad_maximum_fusion.1), channel_id=1, source_target_pairs={{1,0},{2,1},{3,2},{0,3},{5,4},{6,5},{7,6},{4,7},{9,8},{10,9},{11,1... | collective-permute-start | bytes 221192 | tf_op jit(solution)/shard_map/ppermute | solution.py:244
  74.3 18.4 %collective-permute-start.16 = (bf16[144,256]{1,0:T(8,128)(2,1)S(1)}, bf16[144,256]{1,0:T(8,128)(2,1)S(1)}, u32[]{:S(2)}, u32[]{:S(2)}) collective-permute-start(bf16[144,256]{1,0:T(8,128)(2,1)S(1)} %fusion.8), channel_id=1, source_target_pairs={{0,1},{1,2},{2,3},{3,0},{4,5},{5,6},{6,7},{7,4},{8,9},{9,10},{10,1... | collective-permute-start | bytes 221192 | tf_op jit(solution)/shard_map/ppermute | solution.py:244
  81.2 6.8 %collective-permute-start.10 = (bf16[152,128]{1,0:T(8,128)(2,1)S(1)}, bf16[152,128]{1,0:T(8,128)(2,1)S(1)}, u32[]{:S(2)}, u32[]{:S(2)}) collective-permute-start(bf16[152,128]{1,0:T(8,128)(2,1)S(1)} %get-tuple-element.89), channel_id=1, source_target_pairs={{0,24},{1,25},{2,26},{3,27},{4,28},{5,29},{6,30},{7,31},{8,16},{9,... | collective-permute-start | bytes 116744 | tf_op jit(solution)/shard_map/ppermute | solution.py:462
  82.6 5.5 %collective-permute-start.8 = (bf16[152,128]{1,0:T(8,128)(2,1)S(1)}, bf16[152,128]{1,0:T(8,128)(2,1)S(1)}, u32[]{:S(2)}, u32[]{:S(2)}) collective-permute-start(bf16[152,128]{1,0:T(8,128)(2,1)S(1)} %get-tuple-element.87), channel_id=1, source_target_pairs={{0,8},{1,9},{2,10},{3,11},{4,12},{5,13},{6,14},{7,15},{8,0},{9,1},... | collective-permute-start | bytes 116744 | tf_op jit(solution)/shard_map/ppermute | solution.py:462
  83.3 4.9 %collective-permute-start.9 = (bf16[152,128]{1,0:T(8,128)(2,1)S(1)}, bf16[152,128]{1,0:T(8,128)(2,1)S(1)}, u32[]{:S(2)}, u32[]{:S(2)}) collective-permute-start(bf16[152,128]{1,0:T(8,128)(2,1)S(1)} %get-tuple-element.88), channel_id=1, source_target_pairs={{0,16},{1,17},{2,18},{3,19},{4,20},{5,21},{6,22},{7,23},{8,24},{9,... | collective-permute-start | bytes 116744 | tf_op jit(solution)/shard_map/ppermute | solution.py:462
  88.2 9.3 %collective-permute-start.11 = (bf16[152,128]{1,0:T(8,128)(2,1)S(1)}, bf16[152,128]{1,0:T(8,128)(2,1)S(1)}, u32[]{:S(2)}, u32[]{:S(2)}) collective-permute-start(bf16[152,128]{1,0:T(8,128)(2,1)S(1)} %shard_map.109.refs_0_), channel_id=1, source_target_pairs={{0,8},{1,9},{2,10},{3,11},{4,12},{5,13},{6,14},{7,15},{8,0},{9,1},... | collective-permute-start | bytes 116744 | tf_op jit(solution)/shard_map/ppermute | solution.py:462
  89.6 8.0 %collective-permute-start.12 = (bf16[152,128]{1,0:T(8,128)(2,1)S(1)}, bf16[152,128]{1,0:T(8,128)(2,1)S(1)}, u32[]{:S(2)}, u32[]{:S(2)}) collective-permute-start(bf16[152,128]{1,0:T(8,128)(2,1)S(1)} %shard_map.109.refs_0_), channel_id=1, source_target_pairs={{0,16},{1,17},{2,18},{3,19},{4,20},{5,21},{6,22},{7,23},{8,24},{9,... | collective-permute-start | bytes 116744 | tf_op jit(solution)/shard_map/ppermute | solution.py:462
  90.9 6.6 %collective-permute-start.13 = (bf16[152,128]{1,0:T(8,128)(2,1)S(1)}, bf16[152,128]{1,0:T(8,128)(2,1)S(1)}, u32[]{:S(2)}, u32[]{:S(2)}) collective-permute-start(bf16[152,128]{1,0:T(8,128)(2,1)S(1)} %shard_map.109.refs_0_), channel_id=1, source_target_pairs={{0,24},{1,25},{2,26},{3,27},{4,28},{5,29},{6,30},{7,31},{8,16},{9,... | collective-permute-start | bytes 116744 | tf_op jit(solution)/shard_map/ppermute | solution.py:462
  97.6 8.3 %collective-permute-start.18 = (bf16[608,128]{1,0:T(8,128)(2,1)S(1)}, bf16[608,128]{1,0:T(8,128)(2,1)S(1)}, u32[]{:S(2)}, u32[]{:S(2)}) collective-permute-start(bf16[608,128]{1,0:T(8,128)(2,1)S(1)} %shard_map.111.refs_0_), channel_id=1, source_target_pairs={{0,2},{1,3},{2,0},{3,1},{4,6},{5,7},{6,4},{7,5},{8,10},{9,11},{10,... | collective-permute-start | bytes 466952 | tf_op jit(solution)/shard_map/ppermute | solution.py:462
  98.8 7.0 %collective-permute-start.19 = (bf16[608,128]{1,0:T(8,128)(2,1)S(1)}, bf16[608,128]{1,0:T(8,128)(2,1)S(1)}, u32[]{:S(2)}, u32[]{:S(2)}) collective-permute-start(bf16[608,128]{1,0:T(8,128)(2,1)S(1)} %shard_map.111.refs_0_), channel_id=1, source_target_pairs={{0,4},{1,5},{2,6},{3,7},{4,0},{5,1},{6,2},{7,3},{8,12},{9,13},{10,... | collective-permute-start | bytes 466952 | tf_op jit(solution)/shard_map/ppermute | solution.py:462
  99.5 6.5 %collective-permute-start.20 = (bf16[608,128]{1,0:T(8,128)(2,1)S(1)}, bf16[608,128]{1,0:T(8,128)(2,1)S(1)}, u32[]{:S(2)}, u32[]{:S(2)}) collective-permute-start(bf16[608,128]{1,0:T(8,128)(2,1)S(1)} %shard_map.111.refs_0_), channel_id=1, source_target_pairs={{0,6},{1,7},{2,4},{3,5},{4,2},{5,3},{6,0},{7,1},{8,14},{9,15},{10,... | collective-permute-start | bytes 466952 | tf_op jit(solution)/shard_map/ppermute | solution.py:462
  106.1 2.1 %collective-permute-start.21 = (bf16[2432,128]{1,0:T(8,128)(2,1)S(1)}, bf16[2432,128]{1,0:T(8,128)(2,1)S(1)}, u32[]{:S(2)}, u32[]{:S(2)}) collective-permute-start(bf16[2432,128]{1,0:T(8,128)(2,1)S(1)} %shard_map.113.own_ref), channel_id=1, source_target_pairs={{0,1},{1,0},{2,3},{3,2},{4,5},{5,4},{6,7},{7,6},{8,9},{9,8},{10,11... | collective-permute-start | bytes 1867784 | tf_op jit(solution)/shard_map/ppermute | solution.py:462
  (4 other events, 40.2 us)
